TPU v7x, 512 devices: a whole 4x8x8 slice. The times are simulated.
512 devices in a mesh: row: 64 (over y, x, core), col: 8 (over z).
Axes of the slice: x: 4, y: 8, z: 8, core: 2. Of those that a mesh axis runs over, the one named last changes fastest.
Arguments:
- near_blocks: float32 [512, 8, 256, 256], P('row', 'col'), may hold values from -0.125 to 0.125
- column_block: int32 [512, 8], P('row', 'col'), may hold values from 0 to 511, as said below
- test_panels: float32 [512, 256, 256], P(('row', 'col')), may hold values from -6 to 6
- nugget: float32 [512, 256], P('row'), may hold values from 0.5 to 2
Outputs:
- leaf_basis: float32 [512, 128, 256], P('row', None, 'col')
- leaf_miss: float32 [512, 128, 256], P('row', None, 'col')
- local_basis: float32 [448, 128, 256], P('row', None, 'col')
- upper_basis: float32 [64, 128, 256], P('row', None, 'col')
Inputs may be any that keep to these rules, and one draw needn't show every extreme that they name: `column_block`: row i names 8 different leaf blocks, i itself among them, all within i - 8 to i + 8.
All inputs are finite; a program needn't handle non-finite values.
Results may differ from a plain program's by a relative error of at most 0.0003.
Values sent between devices are 32-bit elements; how exact they have to be, the bound alone decides.
No kernel may reach another device: no remote copies, remote signals or barrier semaphores. Data moves between devices by JAX's collectives and lax.ppermute only.
A program may use at most 64 MiB of HBM per device.

v0:
```python
import math

import jax
import jax.numpy as jnp
from jax import lax
from jax.sharding import PartitionSpec as P


def padded(block, sides, width):
    for axis, dim in sides:
        count = lax.axis_size(axis)
        forward = [(i, i + 1) for i in range(count - 1)]
        backward = [(target, source) for source, target in forward]
        low = lax.ppermute(
            lax.slice_in_dim(block, block.shape[dim] - width, None, axis=dim), axis, forward
        )
        high = lax.ppermute(lax.slice_in_dim(block, 0, width, axis=dim), axis, backward)
        block = jnp.concatenate([low, block, high], axis=dim)
    return block


def from_partner(block, axis, stride):
    count = lax.axis_size(axis)
    route = []
    for low in range(count):
        high = low | 1 << stride
        if high != low and high < count:
            route += [(low, high), (high, low)]
    return lax.ppermute(block, axis, route)


def product(left, right):
    return jnp.matmul(left, right, precision=lax.Precision.HIGHEST)


def combine(factor_a, panel_a, factor_b, panel_b):
    gram_matrix = product(factor_a, jnp.swapaxes(factor_a, -1, -2)) + product(
        factor_b, jnp.swapaxes(factor_b, -1, -2)
    )
    factor = jnp.linalg.cholesky(gram_matrix)
    basis_node = jax.scipy.linalg.solve_triangular(
        factor, jnp.concatenate([factor_a, factor_b], axis=-1), lower=True
    )
    reduced = jax.scipy.linalg.solve_triangular(
        factor, product(factor_a, panel_a) + product(factor_b, panel_b), lower=True
    )
    return (basis_node, factor, reduced)


def leaf_factor(panel_one, panel_two, gram_matrix, cross_gram):
    factor = jnp.linalg.cholesky(gram_matrix)
    basis_leaf = jax.scipy.linalg.solve_triangular(factor, panel_one, lower=True)
    reduced = jax.scipy.linalg.solve_triangular(factor, cross_gram, lower=True)
    missed = panel_two - jnp.einsum(
        "ist,isa->ita", reduced, basis_leaf, precision=lax.Precision.HIGHEST
    )
    return (basis_leaf, missed, factor, reduced)


def on_device(near_blocks, column_block, test_panels, nugget):
    leaf_count = near_blocks.shape[0]
    block_size = near_blocks.shape[2]
    panel_width = test_panels.shape[2] // 2
    row_index = lax.axis_index("row")
    column_index = lax.axis_index("col")
    column_count = lax.axis_size("col")
    offsets = column_block - (row_index * leaf_count - leaf_count)
    own_within = jnp.arange(leaf_count, dtype=jnp.int32)
    own_panels = lax.all_gather(test_panels, "col", axis=0, tiled=True)
    widened = padded(own_panels, (("row", 0),), leaf_count)
    own_slots = own_within + leaf_count
    picked = jnp.take(widened, offsets, axis=0)
    partial_value = jnp.einsum(
        "ikab,ikbs->isa", near_blocks, picked, precision=lax.Precision.HIGHEST
    )
    own_rows = jnp.take(widened, own_slots, axis=0)
    sample = lax.psum(partial_value, "col") + jnp.swapaxes(own_rows, 1, 2) * nugget[:, None, :]
    panel_one = sample[:, :panel_width]
    panel_two = sample[:, panel_width:]
    gram_matrix = jnp.einsum("isa,ita->ist", panel_one, panel_one, precision=lax.Precision.HIGHEST)
    cross_gram = jnp.einsum("isa,ita->ist", panel_one, panel_two, precision=lax.Precision.HIGHEST)
    basis_leaf, missed, factor, reduced = leaf_factor(panel_one, panel_two, gram_matrix, cross_gram)
    row_share = block_size // column_count
    leaf_basis = lax.dynamic_slice_in_dim(basis_leaf, column_index * row_share, row_share, 2)
    leaf_miss = lax.dynamic_slice_in_dim(missed, column_index * row_share, row_share, 2)
    current_factor, current_panel = (factor, reduced)
    local_parts = []
    for level_index in range(leaf_count.bit_length() - 1):
        pair_count = current_factor.shape[0] // 2
        pair_factor = current_factor.reshape(pair_count, 2, panel_width, panel_width)
        pair_panel = current_panel.reshape(pair_count, 2, panel_width, panel_width)
        basis_level, current_factor, current_panel = combine(
            pair_factor[:, 0], pair_panel[:, 0], pair_factor[:, 1], pair_panel[:, 1]
        )
        local_parts.append(basis_level)
    local_basis = jnp.concatenate(local_parts, axis=0)
    factor_top = current_factor[0]
    panel_top = current_panel[0]
    levels = lax.axis_size("row").bit_length() - 1
    upper_basis = jnp.zeros((panel_width, 2 * panel_width), jnp.float32)
    for level_index in range(levels):
        stride = 1 << level_index
        partner_factor, partner_panel = from_partner((factor_top, panel_top), "row", level_index)
        upper_side = row_index // stride % 2 == 1
        left_factor = jnp.where(upper_side, partner_factor, factor_top)
        left_panel = jnp.where(upper_side, partner_panel, panel_top)
        right_factor = jnp.where(upper_side, factor_top, partner_factor)
        right_panel = jnp.where(upper_side, panel_top, partner_panel)
        basis_node, factor_top, panel_top = combine(
            left_factor, left_panel, right_factor, right_panel
        )
        upper_basis = jnp.where(row_index % (2 * stride) == stride, basis_node, upper_basis)
    root_scale = 1.0 / math.sqrt(leaf_count * lax.axis_size("row") * block_size)
    root_stack = jnp.concatenate([jnp.swapaxes(factor_top, 0, 1), panel_top], axis=1) * root_scale
    upper_basis = jnp.where(row_index == 0, root_stack, upper_basis)
    column_share = 2 * panel_width // column_count
    local_share = lax.dynamic_slice_in_dim(
        local_basis, column_index * column_share, column_share, 2
    )
    upper_share = lax.dynamic_slice_in_dim(
        upper_basis, column_index * column_share, column_share, 1
    )
    return (leaf_basis, leaf_miss, local_share, upper_share[None])


def solution(mesh):
    placed = (
        P("row", "col", None, None),
        P("row", "col"),
        P(("row", "col"), None, None),
        P("row", None),
    )
    return jax.shard_map(
        on_device,
        mesh=mesh,
        in_specs=placed,
        out_specs=(
            P("row", None, "col"),
            P("row", None, "col"),
            P("row", None, "col"),
            P("row", None, "col"),
        ),
        check_vma=False,
    )
```

profile of v0, /device:TPU:1, one launch (start us, length us, event | category | flops | bytes accessed | tf_op | source)
XLA Modules:
  0.0 769.8 jit_solution(16910002058661002841)
XLA Ops:
  8.0 47.5 %all-gather.2.cloned.1.call-done = f32[8,256,256]{2,1,0:T(8,128)} async-done(((f32[1,256,256]{2,1,0:T(8,128)}), f32[8,256,256]{2,1,0:T(8,128)}) %all-gather.2.cloned.1.call-update) | async-done | bytes 2097168 | tf_op jit(solution)/shard_map/all_gather | solution.py:69
  55.5 7.7 %collective-permute-start = (f32[8,256,256]{2,1,0:T(8,128)}, f32[8,256,256]{2,1,0:T(8,128)}, u32[]{:S(2)}, u32[]{:S(2)}) collective-permute-start(f32[8,256,256]{2,1,0:T(8,128)} %all-gather.2.cloned.1.call-done), channel_id=1, source_target_pairs={{0,8},{8,16},{16,24},{24,32},{32,40},{40,48},{48,56},{56,64},{64,7... | collective-permute-start | bytes 6291464 | tf_op jit(solution)/shard_map/ppermute | solution.py:14
  65.8 20.7 %collective-permute-done = f32[8,256,256]{2,1,0:T(8,128)} collective-permute-done((f32[8,256,256]{2,1,0:T(8,128)}, f32[8,256,256]{2,1,0:T(8,128)}, u32[]{:S(2)}, u32[]{:S(2)}) %collective-permute-start) | collective-permute-done | bytes 2097184 | tf_op jit(solution)/shard_map/ppermute | solution.py:14
  114.9 76.5 %all-reduce.2.cloned.1.call-done = f32[8,256,256]{2,1,0:T(8,128)} async-done(((f32[8,256,256]{2,1,0:T(8,128)}), f32[8,256,256]{2,1,0:T(8,128)}) %all-reduce.2.cloned.1.call-update) | async-done | bytes 2097168 | tf_op jit(solution)/shard_map/psum | solution.py:77
  198.4 94.6 %custom-call.45 = f32[8,128,128]{2,1,0:T(8,128)S(1)} custom-call(f32[8,128,128]{2,1,0:T(8,128)} %fusion.18), custom_call_target="Cholesky" | custom-call | tf_op jit(solution)/shard_map/jit(cholesky)/cholesky | solution.py:51
  295.6 47.4 %custom-call.47 = f32[4,128,128]{2,1,0:T(8,128)S(1)} custom-call(f32[4,128,128]{2,1,0:T(8,128)S(1)} %fusion.29), custom_call_target="Cholesky" | custom-call | tf_op jit(solution)/shard_map/jit(cholesky)/cholesky | solution.py:40
  344.8 23.5 %custom-call.49 = f32[2,128,128]{2,1,0:T(8,128)S(1)} custom-call(f32[2,128,128]{2,1,0:T(8,128)S(1)} %fusion.58), custom_call_target="Cholesky" | custom-call | tf_op jit(solution)/shard_map/jit(cholesky)/cholesky | solution.py:40
  375.6 13.2 %custom-call.51 = f32[1,128,128]{2,1,0:T(8,128)} custom-call(f32[1,128,128]{2,1,0:T(8,128)} %fusion.61), custom_call_target="Cholesky" | custom-call | tf_op jit(solution)/shard_map/jit(cholesky)/cholesky | solution.py:40
  399.0 80.2 %custom-call.46 = f32[8,1,128,128]{2,3,1,0:T(8,128)} custom-call(f32[8,1,128,128]{3,2,1,0:T(8,128)} %get-tuple-element.37), custom_call_target="InvertDiagBlocksLowerTriangular" | custom-call | tf_op jit(solution)/shard_map/jit(_solve_triangular)/vmap()/triangular_solve | solution.py:52
  485.2 40.8 %custom-call.48 = f32[4,1,128,128]{2,3,1,0:T(8,128)} custom-call(f32[4,1,128,128]{3,2,1,0:T(8,128)} %get-tuple-element.35), custom_call_target="InvertDiagBlocksLowerTriangular" | custom-call | tf_op jit(solution)/shard_map/jit(_solve_triangular)/vmap()/triangular_solve | solution.py:41
  528.9 20.7 %custom-call.50 = f32[2,1,128,128]{2,3,1,0:T(8,128)S(1)} custom-call(f32[2,1,128,128]{3,2,1,0:T(8,128)} %get-tuple-element.46), custom_call_target="InvertDiagBlocksLowerTriangular" | custom-call | tf_op jit(solution)/shard_map/jit(_solve_triangular)/vmap()/triangular_solve | solution.py:41
  552.6 10.6 %custom-call.64 = f32[1,128,128]{1,2,0:T(8,128)S(1)} custom-call(f32[1,128,128]{2,1,0:T(8,128)} %get-tuple-element.33), custom_call_target="InvertDiagBlocksLowerTriangular" | custom-call | tf_op jit(solution)/shard_map/jit(_solve_triangular)/triangular_solve/custom-call.11 | solution.py:41
  579.4 11.7 %cholesky.243 = f32[128,128]{1,0:T(8,128)S(1)} custom-call(f32[128,128]{1,0:T(8,128)S(1)} %fusion.88), custom_call_target="Cholesky" | custom-call | tf_op jit(solution)/shard_map/jit(cholesky)/cholesky | solution.py:40
  595.9 9.8 %custom-call.66 = f32[1,128,128]{1,2,0:T(8,128)S(1)} custom-call(f32[1,128,128]{2,1,0:T(8,128)S(1)} %get-tuple-element.31), custom_call_target="InvertDiagBlocksLowerTriangular" | custom-call | tf_op jit(solution)/shard_map/jit(_solve_triangular)/triangular_solve/custom-call.12 | solution.py:44
  610.6 11.7 %cholesky.254 = f32[128,128]{1,0:T(8,128)S(1)} custom-call(f32[128,128]{1,0:T(8,128)S(1)} %fusion.87), custom_call_target="Cholesky" | custom-call | tf_op jit(solution)/shard_map/jit(cholesky)/cholesky | solution.py:40
  623.7 9.8 %custom-call.67 = f32[1,128,128]{1,2,0:T(8,128)S(1)} custom-call(f32[1,128,128]{2,1,0:T(8,128)S(1)} %get-tuple-element.29), custom_call_target="InvertDiagBlocksLowerTriangular" | custom-call | tf_op jit(solution)/shard_map/jit(_solve_triangular)/triangular_solve/custom-call.12 | solution.py:44
  642.3 11.7 %cholesky.265 = f32[128,128]{1,0:T(8,128)S(1)} custom-call(f32[128,128]{1,0:T(8,128)S(1)} %fusion.86), custom_call_target="Cholesky" | custom-call | tf_op jit(solution)/shard_map/jit(cholesky)/cholesky | solution.py:40
  655.3 9.8 %custom-call.68 = f32[1,128,128]{1,2,0:T(8,128)S(1)} custom-call(f32[1,128,128]{2,1,0:T(8,128)S(1)} %get-tuple-element.27), custom_call_target="InvertDiagBlocksLowerTriangular" | custom-call | tf_op jit(solution)/shard_map/jit(_solve_triangular)/triangular_solve/custom-call.12 | solution.py:44
  672.5 11.7 %cholesky.276 = f32[128,128]{1,0:T(8,128)S(1)} custom-call(f32[128,128]{1,0:T(8,128)S(1)} %fusion.85), custom_call_target="Cholesky" | custom-call | tf_op jit(solution)/shard_map/jit(cholesky)/cholesky | solution.py:40
  685.5 9.8 %custom-call.69 = f32[1,128,128]{1,2,0:T(8,128)S(1)} custom-call(f32[1,128,128]{2,1,0:T(8,128)S(1)} %get-tuple-element.25), custom_call_target="InvertDiagBlocksLowerTriangular" | custom-call | tf_op jit(solution)/shard_map/jit(_solve_triangular)/triangular_solve/custom-call.12 | solution.py:44
  703.6 11.7 %cholesky.287 = f32[128,128]{1,0:T(8,128)S(1)} custom-call(f32[128,128]{1,0:T(8,128)S(1)} %fusion.84), custom_call_target="Cholesky" | custom-call | tf_op jit(solution)/shard_map/jit(cholesky)/cholesky | solution.py:40
  716.6 9.8 %custom-call.70 = f32[1,128,128]{1,2,0:T(8,128)S(1)} custom-call(f32[1,128,128]{2,1,0:T(8,128)S(1)} %get-tuple-element.23), custom_call_target="InvertDiagBlocksLowerTriangular" | custom-call | tf_op jit(solution)/shard_map/jit(_solve_triangular)/triangular_solve/custom-call.12 | solution.py:44
  737.8 11.7 %cholesky.298 = f32[128,128]{1,0:T(8,128)S(1)} custom-call(f32[128,128]{1,0:T(8,128)S(1)} %fusion.83), custom_call_target="Cholesky" | custom-call | tf_op jit(solution)/shard_map/jit(cholesky)/cholesky | solution.py:40
  750.8 9.8 %custom-call.71 = f32[1,128,128]{1,2,0:T(8,128)S(1)} custom-call(f32[1,128,128]{2,1,0:T(8,128)S(1)} %get-tuple-element.61), custom_call_target="InvertDiagBlocksLowerTriangular" | custom-call | tf_op jit(solution)/shard_map/jit(_solve_triangular)/triangular_solve/custom-call.12 | solution.py:44
  (202 shorter events, 141.6 us)
Async XLA Ops:
  7.2 94.7 %copy-start = (f32[8,1,256,256]{3,2,1,0:T(8,128)S(1)}, f32[8,1,256,256]{3,2,1,0:T(8,128)}, u32[]{:S(2)}) copy-start(f32[8,1,256,256]{3,2,1,0:T(8,128)} %param.9) | copy-start | bytes 6291460
  7.2 48.3 %all-gather.2.cloned.1.call-start = ((), (), s32[]{:S(2)}) async-start(), calls=%async_computation | async-start | bytes 2359296 | tf_op jit(solution)/shard_map/all_gather | solution.py:69
  7.9 183.5 %all-reduce.2.cloned.1.call-start = ((), (), s32[]{:S(2)}) async-start(), calls=%async_computation.1 | async-start | bytes 4194304 | tf_op jit(solution)/shard_map/psum | solution.py:77
  55.5 31.0 %collective-permute-start = (f32[8,256,256]{2,1,0:T(8,128)}, f32[8,256,256]{2,1,0:T(8,128)}, u32[]{:S(2)}, u32[]{:S(2)}) collective-permute-start(f32[8,256,256]{2,1,0:T(8,128)} %all-gather.2.cloned.1.call-done), channel_id=1, source_target_pairs={{0,8},{8,16},{16,24},{24,32},{32,40},{40,48},{48,56},{56,64},{64,7... | collective-permute-start | bytes 6291464 | tf_op jit(solution)/shard_map/ppermute | solution.py:14
  63.2 27.8 %collective-permute-start.1 = (f32[8,256,256]{2,1,0:T(8,128)}, f32[8,256,256]{2,1,0:T(8,128)}, u32[]{:S(2)}, u32[]{:S(2)}) collective-permute-start(f32[8,256,256]{2,1,0:T(8,128)} %all-gather.2.cloned.1.call-done), channel_id=1, source_target_pairs={{8,0},{16,8},{24,16},{32,24},{40,32},{48,40},{56,48},{64,56},{72,6... | collective-permute-start | bytes 6291464 | tf_op jit(solution)/shard_map/ppermute | solution.py:17
  65.8 23.7 %copy-start.6 = (f32[8,256,256]{2,1,0:T(8,128)S(1)}, f32[8,256,256]{2,1,0:T(8,128)}, u32[]{:S(2)}) copy-start(f32[8,256,256]{2,1,0:T(8,128)} %all-gather.2.cloned.1.call-done) | copy-start | bytes 6291460
  112.0 79.5 %copy-start.14 = (f32[8,256]{1,0:T(8,128)S(1)}, f32[8,256]{1,0:T(8,128)}, u32[]{:S(2)}) copy-start(f32[8,256]{1,0:T(8,128)} %param.12) | copy-start | bytes 24580
  371.7 111.0 %copy-start.4 = (f32[8,128,128]{2,1,0:T(8,128)S(1)}, f32[8,128,128]{2,1,0:T(8,128)}, u32[]{:S(2)}) copy-start(f32[8,128,128]{2,1,0:T(8,128)} %fusion.5) | copy-start | bytes 1572868
  392.4 185.4 %collective-permute-start.2 = (f32[128,128]{1,0:T(8,128)}, f32[128,128]{1,0:T(8,128)}, u32[]{:S(2)}, u32[]{:S(2)}) collective-permute-start(f32[128,128]{1,0:T(8,128)} %get-tuple-element.34), channel_id=1, source_target_pairs={{0,8},{8,0},{16,24},{24,16},{32,40},{40,32},{48,56},{56,48},{64,72... | collective-permute-start | bytes 196616 | tf_op jit(solution)/shard_map/ppermute | solution.py:29
  485.2 81.3 %copy-start.2 = (f32[8,128,256]{2,1,0:T(8,128)S(1)}, f32[8,128,256]{2,1,0:T(8,128)}, u32[]{:S(2)}) copy-start(f32[8,128,256]{2,1,0:T(8,128)} %fusion.7) | copy-start | bytes 3145732
  551.5 19.7 %copy-start.9 = (f32[4,1,128,128]{2,3,1,0:T(8,128)S(1)}, f32[4,1,128,128]{2,3,1,0:T(8,128)}, u32[]{:S(2)}) copy-start(f32[4,1,128,128]{2,3,1,0:T(8,128)} %custom-call.48) | copy-start | bytes 786436
  563.2 8.0 %copy-start.10 = (f32[4,128,128]{2,1,0:T(8,128)S(1)}, f32[4,128,128]{2,1,0:T(8,128)}, u32[]{:S(2)}) copy-start(f32[4,128,128]{2,1,0:T(8,128)} %get-tuple-element.41) | copy-start | bytes 786436
  563.3 8.0 %copy-start.11 = (f32[4,128,128]{2,1,0:T(8,128)S(1)}, f32[4,128,128]{2,1,0:T(8,128)}, u32[]{:S(2)}) copy-start(f32[4,128,128]{2,1,0:T(8,128)} %get-tuple-element.42) | copy-start | bytes 786436
  564.5 41.7 %collective-permute-start.8 = (f32[128,128]{1,0:T(8,128)S(1)}, f32[128,128]{1,0:T(8,128)}, u32[]{:S(2)}, u32[]{:S(2)}) collective-permute-start(f32[128,128]{1,0:T(8,128)S(1)} %fusion.89), channel_id=1, source_target_pairs={{0,8},{8,0},{16,24},{24,16},{32,40},{40,32},{48,56},{56,48},{64,72... | collective-permute-start | bytes 196616 | tf_op jit(solution)/shard_map/ppermute | solution.py:29
  592.4 17.5 %collective-permute-start.3 = (f32[128,128]{1,0:T(8,128)S(1)}, f32[128,128]{1,0:T(8,128)S(1)}, u32[]{:S(2)}, u32[]{:S(2)}) collective-permute-start(f32[128,128]{1,0:T(8,128)S(1)} %get-tuple-element.32), channel_id=1, source_target_pairs={{0,16},{16,0},{8,24},{24,8},{32,48},{48,32},{40,56},{56,40},{64,80... | collective-permute-start | bytes 196616 | tf_op jit(solution)/shard_map/ppermute | solution.py:29
  607.7 30.8 %collective-permute-start.9 = (f32[128,128]{1,0:T(8,128)S(1)}, f32[128,128]{1,0:T(8,128)S(1)}, u32[]{:S(2)}, u32[]{:S(2)}) collective-permute-start(f32[128,128]{1,0:T(8,128)S(1)} %fusion.66), channel_id=1, source_target_pairs={{0,16},{16,0},{8,24},{24,8},{32,48},{48,32},{40,56},{56,40},{64,80... | collective-permute-start | bytes 196616 | tf_op jit(solution)/shard_map/ppermute | solution.py:29
  633.9 7.7 %collective-permute-start.4 = (f32[128,128]{1,0:T(8,128)S(1)}, f32[128,128]{1,0:T(8,128)S(1)}, u32[]{:S(2)}, u32[]{:S(2)}) collective-permute-start(f32[128,128]{1,0:T(8,128)S(1)} %get-tuple-element.30), channel_id=1, source_target_pairs={{0,32},{32,0},{8,40},{40,8},{16,48},{48,16},{24,56},{56,24},{64,96... | collective-permute-start | bytes 196616 | tf_op jit(solution)/shard_map/ppermute | solution.py:29
  639.2 29.4 %collective-permute-start.10 = (f32[128,128]{1,0:T(8,128)S(1)}, f32[128,128]{1,0:T(8,128)S(1)}, u32[]{:S(2)}, u32[]{:S(2)}) collective-permute-start(f32[128,128]{1,0:T(8,128)S(1)} %fusion.69), channel_id=1, source_target_pairs={{0,32},{32,0},{8,40},{40,8},{16,48},{48,16},{24,56},{56,24},{64,96... | collective-permute-start | bytes 196616 | tf_op jit(solution)/shard_map/ppermute | solution.py:29
  665.5 6.2 collective-permute-start.5
  669.4 30.4 %collective-permute-start.11 = (f32[128,128]{1,0:T(8,128)S(1)}, f32[128,128]{1,0:T(8,128)S(1)}, u32[]{:S(2)}, u32[]{:S(2)}) collective-permute-start(f32[128,128]{1,0:T(8,128)S(1)} %fusion.72), channel_id=1, source_target_pairs={{0,64},{64,0},{8,72},{72,8},{16,80},{80,16},{24,88},{88,24},{32,96... | collective-permute-start | bytes 196616 | tf_op jit(solution)/shard_map/ppermute | solution.py:29
  695.7 7.2 collective-permute-start.6
  700.5 33.5 %collective-permute-start.12 = (f32[128,128]{1,0:T(8,128)S(1)}, f32[128,128]{1,0:T(8,128)S(1)}, u32[]{:S(2)}, u32[]{:S(2)}) collective-permute-start(f32[128,128]{1,0:T(8,128)S(1)} %fusion.75), channel_id=1, source_target_pairs={{0,128},{128,0},{8,136},{136,8},{16,144},{144,16},{24,152},{152,24... | collective-permute-start | bytes 196616 | tf_op jit(solution)/shard_map/ppermute | solution.py:29
  726.9 10.2 %collective-permute-start.7 = (f32[128,128]{1,0:T(8,128)S(1)}, f32[128,128]{1,0:T(8,128)S(1)}, u32[]{:S(2)}, u32[]{:S(2)}) collective-permute-start(f32[128,128]{1,0:T(8,128)S(1)} %get-tuple-element.24), channel_id=1, source_target_pairs={{0,256},{256,0},{8,264},{264,8},{16,272},{272,16},{24,280},{280,24... | collective-permute-start | bytes 196616 | tf_op jit(solution)/shard_map/ppermute | solution.py:29
  734.7 26.3 %collective-permute-start.13 = (f32[128,128]{1,0:T(8,128)S(1)}, f32[128,128]{1,0:T(8,128)S(1)}, u32[]{:S(2)}, u32[]{:S(2)}) collective-permute-start(f32[128,128]{1,0:T(8,128)S(1)} %fusion.78), channel_id=1, source_target_pairs={{0,256},{256,0},{8,264},{264,8},{16,272},{272,16},{24,280},{280,24... | collective-permute-start | bytes 196616 | tf_op jit(solution)/shard_map/ppermute | solution.py:29
  (8 other events, 27.5 us)
Sparse Core Ops, SparseCore 0:
  10.1 45.3 all-gather.1
  107.0 84.3 all-reduce.1
where the time goes:
time: 782 us; the launch traced here: 770 us
  other arithmetic  484 us (62%)
  waiting for transfers between devices  145 us (19%)
  starting transfers between devices  52.5 us (7%)
  matrix products  39.5 us (5%)
  local copies, waits for them, and re-layouts  32.2 us (4%)
  between operations  15.7 us (2%)
    another operation x27, other arithmetic, combine(): factor = jnp.linalg.cholesky(gram_matrix)  160 us
    another operation x4, other arithmetic, leaf_factor(): factor = jnp.linalg.cholesky(gram_matrix)  94.7 us
    another operation x3, other arithmetic, leaf_factor(): jax.scipy.linalg.solve_triangular(factor, panel_one, lower=True)  81.2 us
    psum x1, waiting for transfers between devices, on_device(): lax.psum(partial_value, 'col')  76.5 us
    another operation x5, other arithmetic, combine(): jax.scipy.linalg.solve_triangular(factor, jnp.concatenate([factor_a, fact...  75.1 us
    another operation x12, other arithmetic, combine(): jax.scipy.linalg.solve_triangular(factor, product(factor_a, panel_a) + pr...  62.8 us
    all_gather x1, waiting for transfers between devices, on_device(): own_panels = lax.all_gather(test_panels, 'col', axis=0, tiled=True)  47.5 us
    ppermute x12, starting transfers between devices, from_partner(): return lax.ppermute(block, axis, route)  42.7 us
  transfers between devices with their start and end apart: 16, of which 3 were waited for; matrix products, arithmetic and copies ran while one was open for 44% of the time, Pallas kernels for 0%

commit v1 on v0

v1 whole, which is shorter than its diff:
```python
import math

import jax
import jax.numpy as jnp
from jax import lax
from jax.experimental import pallas as pl
from jax.experimental.pallas import tpu as pltpu
from jax.sharding import PartitionSpec as P

HIGHEST = lax.Precision.HIGHEST


def dot(left, right, dims):
    return lax.dot_general(
        left, right, (dims, ((), ())), precision=HIGHEST, preferred_element_type=jnp.float32
    )


def iota(shape, dim):
    return lax.broadcasted_iota(jnp.int32, shape, dim)


def factorize(m_ref, u_ref, group, block):
    n, width, _ = m_ref.shape
    sub = iota((n, 8, width), 1)
    lane = iota((n, 8, width), 2)

    def spread(value):
        return jnp.broadcast_to(value, (n, 8, width))

    for base in range(0, width, group):
        count = group // 8
        m = [m_ref[:, base + 8 * q : base + 8 * q + 8, :] for q in range(count)]
        for q in range(count):
            row = base + 8 * q
            diagonal = None
            upper = m[q]
            for start in range(0, 8, block):
                first = row + start
                e = {
                    i: [spread(m[i][:, :, first + k : first + k + 1]) for k in range(block)]
                    for i in range(q, count)
                }
                inside = (lane >= first) & (lane < first + block)
                for i in range(q, count):
                    fill = jnp.where((lane - row) == sub, 1.0, 0.0) if i == q else 0.0
                    m[i] = jnp.where(inside, fill, m[i])
                for k in range(block):
                    s = start + k
                    inverse = 1.0 / spread(e[q][k][:, s : s + 1, :])
                    pivot_row = spread(m[q][:, s : s + 1, :])
                    pivot_e = [spread(e[q][j][:, s : s + 1, :]) for j in range(k + 1, block)]
                    for i in range(q, count):
                        f = e[i][k] * inverse
                        if i == q:
                            f = jnp.where(sub > s, f, 0.0)
                        for j in range(k + 1, block):
                            e[i][j] = e[i][j] - f * pivot_e[j - k - 1]
                        m[i] = m[i] - f * pivot_row
                for k in range(block):
                    diagonal = e[q][k] if diagonal is None else jnp.where(sub >= start + k, e[q][k], diagonal)
                    upper = jnp.where(lane == first + k, e[q][k], upper)
            scale = lax.rsqrt(diagonal)
            inside = (lane >= row) & (lane < row + 8)
            u_ref[:, row : row + 8, :] = jnp.where(
                lane >= sub + row, jnp.where(inside, upper, m[q]) * scale, 0.0
            )
            m_ref[:, row : row + 8, :] = jnp.where(lane <= sub + row, m[q] * scale, 0.0)
        after = base + group
        if after < width:
            lane_rest = iota((width - after, width), 1)
            lane_panel = iota((group, width), 1)
            for b in range(n):
                u = u_ref[b, base:after, :]
                right = jnp.where(lane_panel < after, m_ref[b, base:after, :], u)
                update = dot(u, right, ((0,), (0,)))
                old = m_ref[b, after:, :]
                old = jnp.where((lane_rest >= base) & (lane_rest < after), 0.0, old)
                m_ref[b, after:, :] = old - update[after:]


def vmem():
    return pl.BlockSpec(memory_space=pltpu.VMEM)


def shape(*dims):
    return jax.ShapeDtypeStruct(dims, jnp.float32)


def near_products(offsets, near_blocks, low, own, high):
    leaf_count, _, size, _ = near_blocks.shape
    width = own.shape[2]

    def kernel(offset_ref, near_ref, low_ref, own_ref, high_ref, out_ref):
        offset = offset_ref[pl.program_id(0)]
        for part, ref in enumerate((low_ref, own_ref, high_ref)):

            @pl.when(offset // leaf_count == part)
            def _():
                out_ref[0] = dot(near_ref[0, 0], ref[0], ((1,), (0,)))

    def panel_spec(part):
        return pl.BlockSpec(
            (1, size, width),
            lambda i, offset_ref: (jnp.clip(offset_ref[i] - part * leaf_count, 0, leaf_count - 1), 0, 0),
        )

    return pl.pallas_call(
        kernel,
        grid_spec=pltpu.PrefetchScalarGridSpec(
            num_scalar_prefetch=1,
            grid=(leaf_count,),
            in_specs=[
                pl.BlockSpec((1, 1, size, size), lambda i, offset_ref: (i, 0, 0, 0)),
                panel_spec(0),
                panel_spec(1),
                panel_spec(2),
            ],
            out_specs=pl.BlockSpec((1, size, width), lambda i, offset_ref: (i, 0, 0)),
        ),
        out_shape=shape(leaf_count, size, width),
        name="near_products",
    )(offsets, near_blocks, low, own, high)


def leaf_grams(partial_sum, panel, nugget):
    size, width = panel.shape

    def kernel(sum_ref, panel_ref, nugget_ref, sample_ref, gram_ref):
        sample = sum_ref[...] + nugget_ref[...] * panel_ref[...]
        sample_ref[...] = sample
        gram_ref[...] = dot(sample[:, : width // 2], sample, ((0,), (0,)))

    return pl.pallas_call(
        kernel,
        in_specs=[vmem()] * 3,
        out_specs=[vmem()] * 2,
        out_shape=[shape(size, width), shape(width // 2, width)],
        name="leaf_grams",
    )(partial_sum, panel, nugget)


def node_children(leaf_count):
    level = [[i] for i in range(leaf_count)]
    nodes = []
    while len(level) > 1:
        pairs = [(level[2 * i], level[2 * i + 1]) for i in range(len(level) // 2)]
        nodes += pairs
        level = [a + b for a, b in pairs]
    return nodes


def local_sums(grams, row_count):
    leaf_count, rows, width = grams.shape
    half = width // 2
    nodes = node_children(leaf_count)
    nodes = nodes + [nodes[-1]] * (leaf_count - len(nodes))

    def kernel(grams_ref, local_ref, sums_ref):
        known = {(i,): grams_ref[i] for i in range(leaf_count)}
        for n, children in enumerate(nodes):
            a, b = tuple(children[0]), tuple(children[1])
            local_ref[n, 0] = known[a][:, :half]
            local_ref[n, 1] = known[b][:, :half]
            known[a + b] = known[a] + known[b]
        total = known[tuple(range(leaf_count))]
        sums_ref[...] = jnp.zeros_like(sums_ref)
        sums_ref[:rows] = total[:, :half]
        sums_ref[rows : 2 * rows] = total[:, half:]

    return pl.pallas_call(
        kernel,
        in_specs=[vmem()],
        out_specs=[vmem()] * 2,
        out_shape=[shape(leaf_count, 2, rows, half), shape(row_count, half)],
        name="local_sums",
    )(grams)


def tree_sums(rows_of_all):
    count, width = rows_of_all.shape

    def kernel(rows_ref, out_ref):
        r = iota((count, count), 0)
        s = iota((count, count), 1)
        stride = r & -r
        root = r == 0
        left = root | ((s >= r - stride) & (s < r))
        right = root | ((s >= r) & (s < r + stride))
        rows = rows_ref[...]
        out_ref[:, :width] = dot(jnp.where(left, 1.0, 0.0), rows, ((1,), (0,)))
        out_ref[:, width:] = dot(jnp.where(right, 1.0, 0.0), rows, ((1,), (0,)))

    return pl.pallas_call(
        kernel, in_specs=[vmem()], out_specs=vmem(), out_shape=shape(count, 2 * width), name="tree_sums"
    )(rows_of_all)


def gram_message(local, sums, row_index):
    leaf_count, _, rows, half = local.shape

    def kernel(row_ref, local_ref, sums_ref, out_ref):
        root = row_ref[0] == 0
        a = sums_ref[:rows, :half]
        b = sums_ref[:rows, half:]
        cross = sums_ref[rows : 2 * rows, :half]
        total = jnp.where(root, a, a + b)
        for c in range(leaf_count):
            out_ref[c, 0] = local_ref[c, 0]
            out_ref[c, 1] = local_ref[c, 1]
            out_ref[c, 2] = jnp.where(root, cross, a if c < leaf_count // 2 else b)
            out_ref[c, 3] = total

    return pl.pallas_call(
        kernel,
        in_specs=[pl.BlockSpec(memory_space=pltpu.SMEM), vmem(), vmem()],
        out_specs=vmem(),
        out_shape=shape(leaf_count, 4, rows, half),
        name="gram_message",
    )(row_index, local, sums)


def node_bases(index, received, gram, sample, root_scale):
    parts, _, rows, half = received.shape
    size, width = sample.shape
    share = width // parts

    def kernel(index_ref, received_ref, gram_ref, sample_ref, message_ref, upper_ref, m_ref, u_ref):
        for c in range(parts):
            piece = slice(rows * c, rows * (c + 1))
            a, b = received_ref[c, 0], received_ref[c, 1]
            m_ref[0, piece, :] = gram_ref[piece, :half]
            m_ref[1, piece, :] = a
            m_ref[2, piece, :] = b
            m_ref[3, piece, :] = a + b
            m_ref[4, piece, :] = received_ref[c, 2]
            m_ref[5, piece, :] = received_ref[c, 3]
        factorize(m_ref, u_ref, 32, 8)
        inverse = m_ref[0]
        basis = dot(sample_ref[:, :half], inverse, ((1,), (1,)))
        reduced = dot(inverse, gram_ref[:, half:], ((1,), (0,)))
        missed = sample_ref[:, half:] - dot(basis, reduced, ((1,), (0,)))
        node_a = dot(u_ref[1], m_ref[3], ((1,), (1,)))
        node_b = dot(u_ref[2], m_ref[3], ((1,), (1,)))
        for c in range(parts):
            message_ref[c, 0] = basis[share * c : share * (c + 1)]
            message_ref[c, 1] = missed[share * c : share * (c + 1)]
            node = node_a if c < parts // 2 else node_b
            at = share * (c % (parts // 2))
            message_ref[c, 2] = node[at : at + share]
        root = index_ref[0] == 0
        column = index_ref[1]

        @pl.when(root)
        def _():
            for c in range(parts):
                piece = slice(rows * c, rows * (c + 1))
                u_ref[4, piece, :] = received_ref[c, 2]

        at = pl.multiple_of(share * lax.rem(column, parts // 2), share)

        @pl.when(jnp.logical_not(root))
        def _():
            upper_ref[...] = dot(m_ref[5], u_ref[4, pl.ds(at, share), :], ((1,), (1,)))

        @pl.when(root)
        def _():
            reduced_root = dot(m_ref[5], u_ref[4], ((1,), (0,)))
            u_ref[0] = jnp.where(column < parts // 2, u_ref[5], reduced_root).T * root_scale
            upper_ref[...] = u_ref[0, pl.ds(at, share), :].T

    return pl.pallas_call(
        kernel,
        in_specs=[pl.BlockSpec(memory_space=pltpu.SMEM), vmem(), vmem(), vmem()],
        out_specs=[vmem()] * 2,
        out_shape=[shape(parts, 3, share, half), shape(half, share)],
        scratch_shapes=[pltpu.VMEM((6, half, half), jnp.float32)] * 2,
        name="node_bases",
    )(index, received, gram, sample)


def placed_outputs(received):
    parts, _, share, half = received.shape

    def kernel(received_ref, basis_ref, miss_ref, local_ref):
        for c in range(parts):
            basis_ref[c] = received_ref[c, 0].T
            miss_ref[c] = received_ref[c, 1].T
            if c < parts - 1:
                local_ref[c] = received_ref[c, 2].T

    return pl.pallas_call(
        kernel,
        in_specs=[vmem()],
        out_specs=[vmem()] * 3,
        out_shape=[shape(parts, half, share), shape(parts, half, share), shape(parts - 1, half, share)],
        name="placed_outputs",
    )(received)


def neighbours(block):
    count = lax.axis_size("row")
    forward = [(i, i + 1) for i in range(count - 1)]
    backward = [(i + 1, i) for i in range(count - 1)]
    return lax.ppermute(block, "row", forward), lax.ppermute(block, "row", backward)


def exchange(block, axis):
    return lax.all_to_all(block, axis, 0, 0, tiled=True)


def on_device(near_blocks, column_block, test_panels, nugget):
    leaf_count = near_blocks.shape[0]
    size = near_blocks.shape[2]
    half = test_panels.shape[2] // 2
    row_count = lax.axis_size("row")
    col_count = lax.axis_size("col")
    row_index = lax.axis_index("row")
    col_index = lax.axis_index("col")
    index = jnp.stack([row_index, col_index]).astype(jnp.int32)
    offsets = (column_block - (row_index - 1) * leaf_count).reshape(-1)

    own = lax.all_gather(test_panels, "col", axis=0, tiled=True)
    low, high = neighbours(own)
    partial_sums = near_products(offsets, near_blocks, low, own, high)
    summed = lax.psum_scatter(partial_sums, "col", scatter_dimension=0, tiled=True)
    own_nugget = lax.dynamic_slice_in_dim(nugget, col_index, 1, 0).reshape(size, 1)
    sample, gram = leaf_grams(summed[0], test_panels[0], own_nugget)

    grams = exchange(gram.reshape(col_count, half // col_count, 2 * half), "col")
    local, sums = local_sums(grams, row_count)
    sums = exchange(tree_sums(exchange(sums, "row")), "row")
    received = exchange(gram_message(local, sums, index), "col")
    root_scale = 1.0 / math.sqrt(leaf_count * row_count * size)
    message, upper = node_bases(index, received, gram, sample, root_scale)
    leaf_basis, leaf_miss, local_basis = placed_outputs(exchange(message, "col"))
    return leaf_basis, leaf_miss, local_basis, upper[None]


def solution(mesh):
    placed = (
        P("row", "col", None, None),
        P("row", "col"),
        P(("row", "col"), None, None),
        P("row", None),
    )
    return jax.shard_map(
        on_device,
        mesh=mesh,
        in_specs=placed,
        out_specs=(P("row", None, "col"),) * 4,
        check_vma=False,
    )
```

time: 782 us -> 265 us (0.34); the launches traced: 770 us -> 263 us
  other arithmetic: 484 us -> 1.77 us
  blocking collectives: 0 us -> 53.4 us
  matrix products: 39.5 us -> 0 us
  starting transfers between devices: 52.5 us -> 17.7 us
  Pallas kernels: 0 us -> 29.7 us
  local copies, waits for them, and re-layouts: 32.2 us -> 10.8 us
  waiting for transfers between devices: 145 us -> 136 us
    another operation x51 -> x1, other arithmetic: 474 us -> 0.61 us  [on_device(): index = jnp.stack([row_index, col_index]).astype(jnp.int32)]
    psum x1 -> x0, waiting for transfers between devices: 76.5 us -> none  [on_device(): lax.psum(partial_value, 'col')]
    all_to_all x0 -> x3, blocking collectives: none -> 53.4 us  [exchange(): return lax.all_to_all(block, axis, 0, 0, tiled=True)]
    ppermute x14 -> x2, starting transfers between devices: 52.4 us -> 9.67 us  [the longest x1 7.74 us: neighbours(): lax.ppermute(block, 'row', forward)]
    reduce_scatter x0 -> x1, waiting for transfers between devices: none -> 41.2 us  [on_device(): lax.psum_scatter(partial_sums, 'col', scatter_dimension=0, tiled=True)]
    pallas_call x0 -> x7, Pallas kernels: none -> 29.7 us  [the longest x1 11.7 us: node_bases(): pl.pallas_call(kernel, in_specs=[pl.BlockSpec(memory_space=pltpu.SMEM), v...]
    dot_general x40 -> x0, matrix products: 23.7 us -> none  [the longest x36 13.5 us: product(): return jnp.matmul(left, right, precision=lax.Precision.HIGHEST)]
    all_to_all x0 -> x2, waiting for transfers between devices: none -> 22 us  [exchange(): return lax.all_to_all(block, axis, 0, 0, tiled=True)]
  transfers between devices with their start and end apart: 16 -> 6, of which waited for: 3 -> 6; matrix products, arithmetic and copies ran while one was open for 44% -> 2% of each run, Pallas kernels for 0% -> 0%
where the time goes in v1:
time: 265 us; the launch traced here: 263 us
  waiting for transfers between devices  136 us (51%)
  blocking collectives  53.4 us (20%)
  Pallas kernels  29.7 us (11%)
  starting transfers between devices  17.7 us (7%)
  between operations  14.1 us (5%)
  local copies, waits for them, and re-layouts  10.8 us (4%)
    all_to_all x3, blocking collectives, exchange(): return lax.all_to_all(block, axis, 0, 0, tiled=True)  53.4 us
    all_gather x1, waiting for transfers between devices, on_device(): own = lax.all_gather(test_panels, 'col', axis=0, tiled=True)  47.5 us
    reduce_scatter x1, waiting for transfers between devices, on_device(): lax.psum_scatter(partial_sums, 'col', scatter_dimension=0, tiled=True)  41.2 us
    all_to_all x2, waiting for transfers between devices, exchange(): return lax.all_to_all(block, axis, 0, 0, tiled=True)  22 us
    ppermute x1, waiting for transfers between devices, neighbours(): lax.ppermute(block, 'row', forward)  20.2 us
    pallas_call x1, Pallas kernels, node_bases(): pl.pallas_call(kernel, in_specs=[pl.BlockSpec(memory_space=pltpu.SMEM), v...  11.7 us
    pallas_call x1, Pallas kernels, near_products(): pl.pallas_call(kernel, grid_spec=pltpu.PrefetchScalarGridSpec(num_scalar_...  8.52 us
    unnamed x11, local copies, waits for them, and re-layouts  8.49 us
  transfers between devices with their start and end apart: 6, of which 6 were waited for; matrix products, arithmetic and copies ran while one was open for 2% of the time, Pallas kernels for 0%

profile of v1, /device:TPU:1, one launch (start us, length us, event | category | flops | bytes accessed | tf_op | source)
XLA Modules:
  0.0 263.4 jit_solution(8657116337989730601)
XLA Ops:
  8.0 47.5 %all-gather.2.cloned.1.call-done.own_ref = f32[8,256,256]{2,1,0:T(8,128)} async-done(((f32[1,256,256]{2,1,0:T(8,128)}), f32[8,256,256]{2,1,0:T(8,128)}) %all-gather.2.cloned.1.call-update) | async-done | bytes 2097168 | tf_op jit(solution)/shard_map/all_gather | solution.py:323
  55.5 7.7 %collective-permute-start = (f32[8,256,256]{2,1,0:T(8,128)}, f32[8,256,256]{2,1,0:T(8,128)S(1)}, u32[]{:S(2)}, u32[]{:S(2)}) collective-permute-start(f32[8,256,256]{2,1,0:T(8,128)} %all-gather.2.cloned.1.call-done.own_ref), channel_id=1, source_target_pairs={{0,8},{8,16},{16,24},{24,32},{32,40},{40,48},{48,56},{56,64},{64,7... | collective-permute-start | bytes 6291464 | tf_op jit(solution)/shard_map/ppermute | solution.py:305
  63.2 1.9 collective-permute-start.1
  66.3 20.2 %collective-permute-done.low_ref = f32[8,256,256]{2,1,0:T(8,128)S(1)} collective-permute-done((f32[8,256,256]{2,1,0:T(8,128)}, f32[8,256,256]{2,1,0:T(8,128)S(1)}, u32[]{:S(2)}, u32[]{:S(2)}) %collective-permute-start) | collective-permute-done | bytes 2097184 | tf_op jit(solution)/shard_map/ppermute | solution.py:305
  86.5 4.4 %collective-permute-done.1.high_ref = f32[8,256,256]{2,1,0:T(8,128)} collective-permute-done((f32[8,256,256]{2,1,0:T(8,128)}, f32[8,256,256]{2,1,0:T(8,128)}, u32[]{:S(2)}, u32[]{:S(2)}) %collective-permute-start.1) | collective-permute-done | bytes 2097184 | tf_op jit(solution)/shard_map/ppermute | solution.py:305
  90.9 8.5 %near_products.1 = f32[8,256,256]{2,1,0:T(8,128)} custom-call(s32[8]{0:T(128)} %subtract_bitcast_fusion.offset_ref, f32[8,1,256,256]{3,2,1,0:T(8,128)} %near_ref.1, f32[8,256,256]{2,1,0:T(8,128)} %copy-done.1, f32[8,256,256]{2,1,0:T(8,128)} %all-gather.2.cloned.1.call-done.own_ref, f32[8,256,256]{2,1,0:T(8,128)} %collective-permute-done.1.high_ref), custom_call_target="tpu_custom_call" | custom-call | tf_op jit(solution)/shard_map/near_products/pallas_call | solution.py:108
  100.3 41.2 %reduce-scatter.2.cloned.1.call-done = f32[1,256,256]{2,1,0:T(8,128)} async-done(((f32[8,256,256]{2,1,0:T(8,128)}), f32[1,256,256]{2,1,0:T(8,128)}) %reduce-scatter.2.cloned.1.call-update) | async-done | bytes 262160 | tf_op jit(solution)/shard_map/reduce_scatter | solution.py:326
  141.5 2.1 leaf_grams.1
  143.6 12.6 %all_to_all.37.grams_ref = f32[8,16,256]{2,1,0:T(8,128)} all-to-all(f32[8,16,256]{2,1,0:T(8,128)} %bitcast.19), channel_id=1, replica_groups=mesh['row'=64,'col'=8] {'col'}, dimensions={0} | all-to-all | bytes 262144 | tf_op jit(solution)/shard_map/all_to_all | solution.py:309
  156.2 1.6 local_sums.1
  157.8 24.7 %all_to_all.38 = f32[64,1,128]{2,1,0:T(1,128)} all-to-all(f32[64,1,128]{2,1,0:T(1,128)} %bitcast.25), channel_id=1, replica_groups=mesh['row'=64,'col'=8] {'row'}, dimensions={0} | all-to-all | bytes 65536 | tf_op jit(solution)/shard_map/all_to_all | solution.py:309
  182.5 1.6 tree_sums.1
  184.1 1.5 copy.19
  185.6 4.5 %all-to-all-start.2 = ((f32[64,1,256]{2,1,0:T(1,128)}), f32[64,1,256]{2,1,0:T(1,128)S(1)}, u32[]{:S(2)}, u32[]{:S(2)}) async-start(f32[64,1,256]{2,1,0:T(1,128)} %copy.19), calls=%async_computation.3 | async-start | bytes 131072 | tf_op jit(solution)/shard_map/all_to_all | solution.py:309
  190.8 9.5 %all-to-all-done.2 = f32[64,1,256]{2,1,0:T(1,128)S(1)} async-done(((f32[64,1,256]{2,1,0:T(1,128)}), f32[64,1,256]{2,1,0:T(1,128)S(1)}, u32[]{:S(2)}, u32[]{:S(2)}) %all-to-all-start.2) | async-done | bytes 65568 | tf_op jit(solution)/shard_map/all_to_all | solution.py:309
  200.9 1.6 gram_message.1
  202.5 16.0 %all_to_all.39.received_ref = f32[8,4,16,128]{3,2,1,0:T(8,128)} all-to-all(f32[8,4,16,128]{3,2,1,0:T(8,128)} %gram_message.1), channel_id=1, replica_groups=mesh['row'=64,'col'=8] {'col'}, dimensions={0} | all-to-all | bytes 524288 | tf_op jit(solution)/shard_map/all_to_all | solution.py:309
  218.5 11.7 %node_bases.1 = (f32[8,3,32,128]{3,2,1,0:T(8,128)}, f32[128,32]{1,0:T(8,128)}) custom-call(s32[2]{0:T(128)} %pad_add_fusion.row_ref.index_ref, f32[8,4,16,128]{3,2,1,0:T(8,128)} %all_to_all.39.received_ref, f32[128,256]{1,0:T(8,128)} %get-tuple-element.13.gram_ref, f32[256,256]{1,0:T(8,128)} %get-tuple-element.16.sample_ref), custom_call_target="tpu_custom_call" | custom-call | tf_op jit(solution)/shard_map/node_bases/pallas_call | solution.py:272
  230.2 3.5 %all-to-all-start.4 = ((f32[8,3,32,128]{3,2,1,0:T(8,128)}), f32[8,3,32,128]{3,2,1,0:T(8,128)S(1)}, u32[]{:S(2)}, u32[]{:S(2)}) async-start(f32[8,3,32,128]{3,2,1,0:T(8,128)} %get-tuple-element.17), calls=%async_computation.5 | async-start | bytes 786432 | tf_op jit(solution)/shard_map/all_to_all | solution.py:309
  235.2 12.5 %all-to-all-done.4.received_ref = f32[8,3,32,128]{3,2,1,0:T(8,128)S(1)} async-done(((f32[8,3,32,128]{3,2,1,0:T(8,128)}), f32[8,3,32,128]{3,2,1,0:T(8,128)S(1)}, u32[]{:S(2)}, u32[]{:S(2)}) %all-to-all-start.4) | async-done | bytes 393248 | tf_op jit(solution)/shard_map/all_to_all | solution.py:309
  248.4 2.6 placed_outputs.1
  251.0 1.9 copy.20
  252.9 1.9 copy.21
  254.7 1.8 copy.22
  (16 shorter events, 6.3 us)
Async XLA Ops:
  7.2 92.3 %copy-start = (f32[8,256]{1,0:T(8,128)S(1)}, f32[8,256]{1,0:T(8,128)}, u32[]{:S(2)}) copy-start(f32[8,256]{1,0:T(8,128)} %param.7) | copy-start | bytes 24580
  7.2 48.3 %all-gather.2.cloned.1.call-start = ((), (), s32[]{:S(2)}) async-start(), calls=%async_computation.6 | async-start | bytes 2359296 | tf_op jit(solution)/shard_map/all_gather | solution.py:323
  7.9 133.6 %reduce-scatter.2.cloned.1.call-start = ((), (), s32[]{:S(2)}) async-start(), calls=%async_computation.7 | async-start | bytes 2359296 | tf_op jit(solution)/shard_map/reduce_scatter | solution.py:326
  55.5 31.0 %collective-permute-start = (f32[8,256,256]{2,1,0:T(8,128)}, f32[8,256,256]{2,1,0:T(8,128)S(1)}, u32[]{:S(2)}, u32[]{:S(2)}) collective-permute-start(f32[8,256,256]{2,1,0:T(8,128)} %all-gather.2.cloned.1.call-done.own_ref), channel_id=1, source_target_pairs={{0,8},{8,16},{16,24},{24,32},{32,40},{40,48},{48,56},{56,64},{64,7... | collective-permute-start | bytes 6291464 | tf_op jit(solution)/shard_map/ppermute | solution.py:305
  63.2 27.7 %collective-permute-start.1 = (f32[8,256,256]{2,1,0:T(8,128)}, f32[8,256,256]{2,1,0:T(8,128)}, u32[]{:S(2)}, u32[]{:S(2)}) collective-permute-start(f32[8,256,256]{2,1,0:T(8,128)} %all-gather.2.cloned.1.call-done.own_ref), channel_id=1, source_target_pairs={{8,0},{16,8},{24,16},{32,24},{40,32},{48,40},{56,48},{64,56},{72,6... | collective-permute-start | bytes 6291464 | tf_op jit(solution)/shard_map/ppermute | solution.py:305
  86.5 4.4 %copy-start.1 = (f32[8,256,256]{2,1,0:T(8,128)}, f32[8,256,256]{2,1,0:T(8,128)S(1)}, u32[]{:S(2)}) copy-start(f32[8,256,256]{2,1,0:T(8,128)S(1)} %collective-permute-done.low_ref) | copy-start | bytes 6291460
  185.6 14.6 %all-to-all-start.2 = ((f32[64,1,256]{2,1,0:T(1,128)}), f32[64,1,256]{2,1,0:T(1,128)S(1)}, u32[]{:S(2)}, u32[]{:S(2)}) async-start(f32[64,1,256]{2,1,0:T(1,128)} %copy.19), calls=%async_computation.3 | async-start | bytes 131072 | tf_op jit(solution)/shard_map/all_to_all | solution.py:309
  230.2 17.5 %all-to-all-start.4 = ((f32[8,3,32,128]{3,2,1,0:T(8,128)}), f32[8,3,32,128]{3,2,1,0:T(8,128)S(1)}, u32[]{:S(2)}, u32[]{:S(2)}) async-start(f32[8,3,32,128]{3,2,1,0:T(8,128)} %get-tuple-element.17), calls=%async_computation.5 | async-start | bytes 786432 | tf_op jit(solution)/shard_map/all_to_all | solution.py:309
  247.7 0.7 copy-start.2
Sparse Core Ops, SparseCore 0:
  10.1 45.3 all-gather.1
  99.6 41.8 reduce-scatter.1

commit v2 on v1

--- a/solution.py
+++ b/solution.py
@@ -87,57 +87,88 @@
     return jax.ShapeDtypeStruct(dims, jnp.float32)
 
 
-def near_products(offsets, near_blocks, low, own, high):
-    leaf_count, _, size, _ = near_blocks.shape
-    width = own.shape[2]
-
-    def kernel(offset_ref, near_ref, low_ref, own_ref, high_ref, out_ref):
-        offset = offset_ref[pl.program_id(0)]
-        for part, ref in enumerate((low_ref, own_ref, high_ref)):
-
-            @pl.when(offset // leaf_count == part)
-            def _():
-                out_ref[0] = dot(near_ref[0, 0], ref[0], ((1,), (0,)))
-
-    def panel_spec(part):
-        return pl.BlockSpec(
-            (1, size, width),
-            lambda i, offset_ref: (jnp.clip(offset_ref[i] - part * leaf_count, 0, leaf_count - 1), 0, 0),
-        )
-
-    return pl.pallas_call(
-        kernel,
-        grid_spec=pltpu.PrefetchScalarGridSpec(
-            num_scalar_prefetch=1,
-            grid=(leaf_count,),
-            in_specs=[
-                pl.BlockSpec((1, 1, size, size), lambda i, offset_ref: (i, 0, 0, 0)),
-                panel_spec(0),
-                panel_spec(1),
-                panel_spec(2),
-            ],
-            out_specs=pl.BlockSpec((1, size, width), lambda i, offset_ref: (i, 0, 0)),
+def near_products(index, offsets, near_blocks, own, low, high, targets):
+    parts, _, size, _ = near_blocks.shape
+    width = own[0].shape[-1]
+    count = len(targets)
+    groups = [low, own, high]
+    operands = [piece for group in groups for piece in group]
+
+    def kernel(index_ref, offset_ref, near_ref, *refs):
+        panels, (out_ref, near_buffer, panel_buffer, sems) = refs[: len(operands)], refs[len(operands) :]
+        column = index_ref[1]
+        for i, target in enumerate(targets):
+            leaf = lax.rem(column + target, parts)
+            offset = offset_ref[leaf]
+            row_part = offset // parts
+            back = lax.rem(column - lax.rem(offset, parts) + parts + AHEAD, parts)
+            pltpu.make_async_copy(near_ref.at[leaf, 0], near_buffer.at[i], sems.at[0, i]).start()
+            at = 0
+            for g, group in enumerate(groups):
+                first = 0
+                for piece in group:
+                    length = piece.shape[0]
+                    ref, begin = panels[at], first
+
+                    @pl.when((row_part == g) & (back >= begin) & (back < begin + length))
+                    def _():
+                        pltpu.make_async_copy(
+                            ref.at[back - begin if length > 1 else 0], panel_buffer.at[i], sems.at[1, i]
+                        ).start()
+
+                    at += 1
+                    first += length
+        for i in range(count):
+            pltpu.make_async_copy(near_ref.at[0, 0], near_buffer.at[i], sems.at[0, i]).wait()
+            pltpu.make_async_copy(panels[0].at[0], panel_buffer.at[i], sems.at[1, i]).wait()
+            out_ref[i] = dot(near_buffer[i], panel_buffer[i], ((1,), (0,)))
+
+    anywhere = pl.BlockSpec(memory_space=pl.ANY)
+    smem = pl.BlockSpec(memory_space=pltpu.SMEM)
+    return pl.pallas_call(
+        kernel,
+        in_specs=[smem, smem, anywhere] + [anywhere] * len(operands),
+        out_specs=vmem(),
+        out_shape=shape(count, size, width),
+        scratch_shapes=[
+            pltpu.VMEM((count, size, size), jnp.float32),
+            pltpu.VMEM((count, size, width), jnp.float32),
+            pltpu.SemaphoreType.DMA((2, count)),
+        ],
+        cost_estimate=pl.CostEstimate(
+            flops=12 * count * size * size * width,
+            bytes_accessed=12 * count * size * width,
+            transcendentals=0,
         ),
-        out_shape=shape(leaf_count, size, width),
         name="near_products",
-    )(offsets, near_blocks, low, own, high)
-
-
-def leaf_grams(partial_sum, panel, nugget):
-    size, width = panel.shape
-
-    def kernel(sum_ref, panel_ref, nugget_ref, sample_ref, gram_ref):
-        sample = sum_ref[...] + nugget_ref[...] * panel_ref[...]
+    )(index, offsets, near_blocks, *operands)
+
+
+def leaf_grams(index, left, right, products, panel, nugget):
+    _, size, width = panel.shape
+
+    def kernel(index_ref, left_ref, right_ref, product_ref, panel_ref, nugget_ref, sample_ref, gram_ref):
+        row = nugget_ref[pl.ds(index_ref[1], 1), :]
+        column = jnp.broadcast_to(row, (8, size)).T[:, :1]
+        sample = left_ref[0] + right_ref[0] + product_ref[0] + column * panel_ref[0]
         sample_ref[...] = sample
         gram_ref[...] = dot(sample[:, : width // 2], sample, ((0,), (0,)))
 
     return pl.pallas_call(
         kernel,
-        in_specs=[vmem()] * 3,
+        grid=(1,),
+        in_specs=[
+            pl.BlockSpec(memory_space=pltpu.SMEM),
+            vmem(),
+            vmem(),
+            pl.BlockSpec((1, size, width), lambda i: (products.shape[0] - 1, 0, 0)),
+            vmem(),
+            vmem(),
+        ],
         out_specs=[vmem()] * 2,
         out_shape=[shape(size, width), shape(width // 2, width)],
         name="leaf_grams",
-    )(partial_sum, panel, nugget)
+    )(index, left, right, products, panel, nugget)
 
 
 def node_children(leaf_count):
@@ -261,41 +292,22 @@
 
         @pl.when(jnp.logical_not(root))
         def _():
-            upper_ref[...] = dot(m_ref[5], u_ref[4, pl.ds(at, share), :], ((1,), (1,)))
+            upper_ref[...] = dot(u_ref[4, pl.ds(at, share), :], m_ref[5], ((1,), (1,)))
 
         @pl.when(root)
         def _():
             reduced_root = dot(m_ref[5], u_ref[4], ((1,), (0,)))
             u_ref[0] = jnp.where(column < parts // 2, u_ref[5], reduced_root).T * root_scale
-            upper_ref[...] = u_ref[0, pl.ds(at, share), :].T
+            upper_ref[...] = u_ref[0, pl.ds(at, share), :]
 
     return pl.pallas_call(
         kernel,
         in_specs=[pl.BlockSpec(memory_space=pltpu.SMEM), vmem(), vmem(), vmem()],
         out_specs=[vmem()] * 2,
-        out_shape=[shape(parts, 3, share, half), shape(half, share)],
+        out_shape=[shape(parts, 3, share, half), shape(share, half)],
         scratch_shapes=[pltpu.VMEM((6, half, half), jnp.float32)] * 2,
         name="node_bases",
     )(index, received, gram, sample)
-
-
-def placed_outputs(received):
-    parts, _, share, half = received.shape
-
-    def kernel(received_ref, basis_ref, miss_ref, local_ref):
-        for c in range(parts):
-            basis_ref[c] = received_ref[c, 0].T
-            miss_ref[c] = received_ref[c, 1].T
-            if c < parts - 1:
-                local_ref[c] = received_ref[c, 2].T
-
-    return pl.pallas_call(
-        kernel,
-        in_specs=[vmem()],
-        out_specs=[vmem()] * 3,
-        out_shape=[shape(parts, half, share), shape(parts, half, share), shape(parts - 1, half, share)],
-        name="placed_outputs",
-    )(received)
 
 
 def neighbours(block):
@@ -303,6 +315,28 @@
     forward = [(i, i + 1) for i in range(count - 1)]
     backward = [(i + 1, i) for i in range(count - 1)]
     return lax.ppermute(block, "row", forward), lax.ppermute(block, "row", backward)
+
+
+def along_col(block, step):
+    count = lax.axis_size("col")
+    return lax.ppermute(block, "col", [(i, (i + step) % count) for i in range(count)])
+
+
+def gathered(block):
+    back, ahead = [block], [block]
+    for _ in range(2):
+        back.append(along_col(back[-1], 1))
+        ahead.append(along_col(ahead[-1], -1))
+    first = [ahead[2], ahead[1], block, back[1], back[2]]
+    low_first, high_first = neighbours(jnp.concatenate(first, axis=0))
+    three_back = along_col(back[2], 1)
+    three_ahead = along_col(ahead[2], -1)
+    second = [three_back, along_col(three_back, 1), three_ahead]
+    low_second, high_second = neighbours(jnp.concatenate(second, axis=0))
+    return first + second, [low_first, low_second], [high_first, high_second]
+
+
+AHEAD = 2
 
 
 def exchange(block, axis):
@@ -320,12 +354,17 @@
     index = jnp.stack([row_index, col_index]).astype(jnp.int32)
     offsets = (column_block - (row_index - 1) * leaf_count).reshape(-1)
 
-    own = lax.all_gather(test_panels, "col", axis=0, tiled=True)
-    low, high = neighbours(own)
-    partial_sums = near_products(offsets, near_blocks, low, own, high)
-    summed = lax.psum_scatter(partial_sums, "col", scatter_dimension=0, tiled=True)
-    own_nugget = lax.dynamic_slice_in_dim(nugget, col_index, 1, 0).reshape(size, 1)
-    sample, gram = leaf_grams(summed[0], test_panels[0], own_nugget)
+    own, low, high = gathered(test_panels)
+    far = near_products(index, offsets, near_blocks, own, low, high, (4, 3))
+    rest = near_products(index, offsets, near_blocks, own, low, high, (5, 2, 6, 1, 7, 0))
+    right = along_col(far[:1], -1)
+    left = along_col(far[1:], 1)
+    right = along_col(right + rest[0:1], -1)
+    left = along_col(left + rest[1:2], 1)
+    right = along_col(right + rest[2:3], -1)
+    left = along_col(left + rest[3:4], 1)
+    right = along_col(right + rest[4:5], -1)
+    sample, gram = leaf_grams(index, left, right, rest, test_panels, nugget)
 
     grams = exchange(gram.reshape(col_count, half // col_count, 2 * half), "col")
     local, sums = local_sums(grams, row_count)
@@ -333,8 +372,9 @@
     received = exchange(gram_message(local, sums, index), "col")
     root_scale = 1.0 / math.sqrt(leaf_count * row_count * size)
     message, upper = node_bases(index, received, gram, sample, root_scale)
-    leaf_basis, leaf_miss, local_basis = placed_outputs(exchange(message, "col"))
-    return leaf_basis, leaf_miss, local_basis, upper[None]
+    outputs = exchange(message, "col")
+    stored = (outputs[:, 0], outputs[:, 1], outputs[: col_count - 1, 2], upper[None])
+    return tuple(jnp.swapaxes(output, 1, 2) for output in stored)
 
 
 def solution(mesh):

time: 265 us -> 239 us (0.902)
  waiting for transfers between devices: 136 us -> 34.8 us
  starting transfers between devices: 17.7 us -> 65.1 us
  blocking collectives: 53.4 us -> 90.1 us
  between operations: 14.1 us -> 0.92 us
  local copies, waits for them, and re-layouts: 10.8 us -> 13.6 us
    ppermute x0 -> x14, starting transfers between devices: none -> 52.5 us  [along_col(): lax.ppermute(block, 'col', [(i, (i + step) % count) for i in range(count)])]
    all_gather x1 -> x0, waiting for transfers between devices: 47.5 us -> none  [on_device(): own = lax.all_gather(test_panels, 'col', axis=0, tiled=True)]
    reduce_scatter x1 -> x0, waiting for transfers between devices: 41.2 us -> none  [on_device(): lax.psum_scatter(partial_sums, 'col', scatter_dimension=0, tiled=True)]
    all_to_all x3 -> x5, blocking collectives: 53.4 us -> 90.1 us  [exchange(): return lax.all_to_all(block, axis, 0, 0, tiled=True)]
    ppermute x0 -> x14, waiting for transfers between devices: none -> 26.7 us  [along_col(): lax.ppermute(block, 'col', [(i, (i + step) % count) for i in range(count)])]
    all_to_all x2 -> x0, waiting for transfers between devices: 22 us -> none  [exchange(): return lax.all_to_all(block, axis, 0, 0, tiled=True)]
    ppermute x1 -> x2, waiting for transfers between devices: 20.2 us -> 1.3 us  [neighbours(): lax.ppermute(block, 'row', forward)]
    all_to_all x2 -> x0, starting transfers between devices: 7.97 us -> none  [exchange(): return lax.all_to_all(block, axis, 0, 0, tiled=True)]
  transfers between devices with their start and end apart: 6 -> 18, of which waited for: 6 -> 11; matrix products, arithmetic and copies ran while one was open for 2% -> 4% of each run, Pallas kernels for 0% -> 3%
where the time goes in v2:
time: 239 us; the launch traced here: 238 us
  blocking collectives  90.1 us (38%)
  starting transfers between devices  65.1 us (27%)
  waiting for transfers between devices  34.8 us (15%)
  Pallas kernels  28.9 us (12%)
  local copies, waits for them, and re-layouts  13.6 us (6%)
  other arithmetic  4.28 us (2%)
    all_to_all x5, blocking collectives, exchange(): return lax.all_to_all(block, axis, 0, 0, tiled=True)  90.1 us
    ppermute x14, starting transfers between devices, along_col(): lax.ppermute(block, 'col', [(i, (i + step) % count) for i in range(count)])  52.5 us
    ppermute x14, waiting for transfers between devices, along_col(): lax.ppermute(block, 'col', [(i, (i + step) % count) for i in range(count)])  26.7 us
    pallas_call x1, Pallas kernels, node_bases(): pl.pallas_call(kernel, in_specs=[pl.BlockSpec(memory_space=pltpu.SMEM), v...  11.7 us
    pallas_call x2, Pallas kernels, near_products(): pl.pallas_call(kernel, in_specs=[smem, smem, anywhere] + [anywhere] * len...  10 us
    unnamed x33, local copies, waits for them, and re-layouts  8.82 us
    ppermute x2, waiting for transfers between devices, neighbours(): lax.ppermute(block, 'row', backward)  6.82 us
    ppermute x2, starting transfers between devices, neighbours(): lax.ppermute(block, 'row', forward)  6.39 us
  transfers between devices with their start and end apart: 18, of which 11 were waited for; matrix products, arithmetic and copies ran while one was open for 4% of the time, Pallas kernels for 3%

profile of v2, /device:TPU:1, one launch (start us, length us, event | category | flops | bytes accessed | tf_op | source)
XLA Modules:
  0.0 237.7 jit_solution(14273451359176404023)
XLA Ops:
  0.6 4.8 %collective-permute-start.2 = (f32[1,256,256]{2,1,0:T(8,128)}, f32[1,256,256]{2,1,0:T(8,128)S(1)}, u32[]{:S(2)}, u32[]{:S(2)}) collective-permute-start(f32[1,256,256]{2,1,0:T(8,128)} %panel_ref.1), channel_id=1, source_target_pairs={{0,1},{1,2},{2,3},{3,4},{4,5},{5,6},{6,7},{7,0},{8,9},{9,10},{10,1... | collective-permute-start | bytes 786440 | tf_op jit(solution)/shard_map/ppermute | solution.py:322
  5.5 8.6 %collective-permute-start = (f32[1,256,256]{2,1,0:T(8,128)}, f32[1,256,256]{2,1,0:T(8,128)S(1)}, u32[]{:S(2)}, u32[]{:S(2)}) collective-permute-start(f32[1,256,256]{2,1,0:T(8,128)} %panel_ref.1), channel_id=1, source_target_pairs={{0,7},{1,0},{2,1},{3,2},{4,3},{5,4},{6,5},{7,6},{8,15},{9,8},{10,9... | collective-permute-start | bytes 786440 | tf_op jit(solution)/shard_map/ppermute | solution.py:322
  14.1 4.3 %collective-permute-done.2.refs_5_ = f32[1,256,256]{2,1,0:T(8,128)S(1)} collective-permute-done((f32[1,256,256]{2,1,0:T(8,128)}, f32[1,256,256]{2,1,0:T(8,128)S(1)}, u32[]{:S(2)}, u32[]{:S(2)}) %collective-permute-start.2) | collective-permute-done | bytes 262176 | tf_op jit(solution)/shard_map/ppermute | solution.py:322
  20.3 4.6 %collective-permute-start.1 = (f32[1,256,256]{2,1,0:T(8,128)S(1)}, f32[1,256,256]{2,1,0:T(8,128)S(1)}, u32[]{:S(2)}, u32[]{:S(2)}) collective-permute-start(f32[1,256,256]{2,1,0:T(8,128)S(1)} %collective-permute-done.refs_3_), channel_id=1, source_target_pairs={{0,7},{1,0},{2,1},{3,2},{4,3},{5,4},{6,5},{7,6},{8,15},{9,8},{10,9... | collective-permute-start | bytes 786440 | tf_op jit(solution)/shard_map/ppermute | solution.py:322
  24.9 3.2 %collective-permute-done.3.refs_6_ = f32[1,256,256]{2,1,0:T(8,128)S(1)} collective-permute-done((f32[1,256,256]{2,1,0:T(8,128)S(1)}, f32[1,256,256]{2,1,0:T(8,128)S(1)}, u32[]{:S(2)}, u32[]{:S(2)}) %collective-permute-start.3) | collective-permute-done | bytes 262176 | tf_op jit(solution)/shard_map/ppermute | solution.py:322
  34.6 4.0 %collective-permute-start.9 = (f32[5,256,256]{2,1,0:T(8,128)}, f32[5,256,256]{2,1,0:T(8,128)S(1)}, u32[]{:S(2)}, u32[]{:S(2)}) collective-permute-start(f32[5,256,256]{2,1,0:T(8,128)} %constant_dynamic-update-slice_fusion), channel_id=1, source_target_pairs={{8,0},{16,8},{24,16},{32,24},{40,32},{48,40},{56,48},{64,56},{72,6... | collective-permute-start | bytes 3932168 | tf_op jit(solution)/shard_map/ppermute | solution.py:317
  43.5 4.9 %collective-permute-start.7 = (f32[1,256,256]{2,1,0:T(8,128)S(1)}, f32[1,256,256]{2,1,0:T(8,128)S(1)}, u32[]{:S(2)}, u32[]{:S(2)}) collective-permute-start(f32[1,256,256]{2,1,0:T(8,128)S(1)} %collective-permute-done.1.refs_2_), channel_id=1, source_target_pairs={{0,7},{1,0},{2,1},{3,2},{4,3},{5,4},{6,5},{7,6},{8,15},{9,8},{10,9... | collective-permute-start | bytes 786440 | tf_op jit(solution)/shard_map/ppermute | solution.py:322
  49.1 3.6 %collective-permute-done.6.refs_8_ = f32[1,256,256]{2,1,0:T(8,128)S(1)} collective-permute-done((f32[1,256,256]{2,1,0:T(8,128)S(1)}, f32[1,256,256]{2,1,0:T(8,128)S(1)}, u32[]{:S(2)}, u32[]{:S(2)}) %collective-permute-start.6) | collective-permute-done | bytes 262176 | tf_op jit(solution)/shard_map/ppermute | solution.py:322
  57.5 3.4 %collective-permute-start.8 = (f32[3,256,256]{2,1,0:T(8,128)}, f32[3,256,256]{2,1,0:T(8,128)}, u32[]{:S(2)}, u32[]{:S(2)}) collective-permute-start(f32[3,256,256]{2,1,0:T(8,128)} %constant_dynamic-update-slice_fusion.5), channel_id=1, source_target_pairs={{0,8},{8,16},{16,24},{24,32},{32,40},{40,48},{48,56},{56,64},{64,7... | collective-permute-start | bytes 2359304 | tf_op jit(solution)/shard_map/ppermute | solution.py:317
  62.0 6.8 %collective-permute-done.10.refs_11_ = f32[3,256,256]{2,1,0:T(8,128)S(1)} collective-permute-done((f32[3,256,256]{2,1,0:T(8,128)}, f32[3,256,256]{2,1,0:T(8,128)S(1)}, u32[]{:S(2)}, u32[]{:S(2)}) %collective-permute-start.10) | collective-permute-done | bytes 786464 | tf_op jit(solution)/shard_map/ppermute | solution.py:317
  72.2 3.7 %near_products.2 = f32[2,256,256]{2,1,0:T(8,128)} custom-call(s32[2]{0:T(128)} %pad_add_fusion.index_ref.row_ref, s32[8]{0:T(128)} %subtract_bitcast_fusion.offset_ref, f32[8,1,256,256]{3,2,1,0:T(8,128)} %near_ref.3, f32[5,256,256]{2,1,0:T(8,128)} %copy-done.1, f32[3,256,256]{2,1,0:T(8,128)} %collective-permute-done.8.refs_1_, f32[1,256,256]{2,1,0:T(8,128)} %copy-done.6, ...), custom_call_target="tpu_custom_call" | custom-call | flops 402653184 | bytes 1572864 | tf_op jit(solution)/shard_map/near_products/pallas_call | solution.py:128
  76.9 5.2 %collective-permute-start.14 = (f32[1,256,256]{2,1,0:T(8,128)S(1)}, f32[1,256,256]{2,1,0:T(8,128)S(1)}, u32[]{:S(2)}, u32[]{:S(2)}) collective-permute-start(f32[1,256,256]{2,1,0:T(8,128)S(1)} %get-tuple-element.20), channel_id=1, source_target_pairs={{0,7},{1,0},{2,1},{3,2},{4,3},{5,4},{6,5},{7,6},{8,15},{9,8},{10,9... | collective-permute-start | bytes 786440 | tf_op jit(solution)/shard_map/ppermute | solution.py:322
  84.1 6.4 %near_products.3.product_ref = f32[6,256,256]{2,1,0:T(8,128)} custom-call(s32[2]{0:T(128)} %pad_add_fusion.index_ref.row_ref, s32[8]{0:T(128)} %subtract_bitcast_fusion.offset_ref, f32[8,1,256,256]{3,2,1,0:T(8,128)} %near_ref.3, f32[5,256,256]{2,1,0:T(8,128)} %copy-done.1, f32[3,256,256]{2,1,0:T(8,128)} %collective-permute-done.8.refs_1_, ...), custom_call_target="tpu_custom_call" | custom-call | flops 1207959552 | bytes 4718592 | tf_op jit(solution)/shard_map/near_products/pallas_call | solution.py:128
  91.4 4.6 %collective-permute-start.15 = (f32[1,256,256]{2,1,0:T(8,128)S(1)}, f32[1,256,256]{2,1,0:T(8,128)S(1)}, u32[]{:S(2)}, u32[]{:S(2)}) collective-permute-start(f32[1,256,256]{2,1,0:T(8,128)S(1)} %slice_add_fusion.2), channel_id=1, source_target_pairs={{0,7},{1,0},{2,1},{3,2},{4,3},{5,4},{6,5},{7,6},{8,15},{9,8},{10,9... | collective-permute-start | bytes 786440 | tf_op jit(solution)/shard_map/ppermute | solution.py:322
  96.0 3.3 %collective-permute-done.15 = f32[1,256,256]{2,1,0:T(8,128)S(1)} collective-permute-done((f32[1,256,256]{2,1,0:T(8,128)S(1)}, f32[1,256,256]{2,1,0:T(8,128)S(1)}, u32[]{:S(2)}, u32[]{:S(2)}) %collective-permute-start.15) | collective-permute-done | bytes 262176 | tf_op jit(solution)/shard_map/ppermute | solution.py:322
  100.4 5.0 %collective-permute-start.16 = (f32[1,256,256]{2,1,0:T(8,128)S(1)}, f32[1,256,256]{2,1,0:T(8,128)S(1)}, u32[]{:S(2)}, u32[]{:S(2)}) collective-permute-start(f32[1,256,256]{2,1,0:T(8,128)S(1)} %get-tuple-element.18), channel_id=1, source_target_pairs={{0,7},{1,0},{2,1},{3,2},{4,3},{5,4},{6,5},{7,6},{8,15},{9,8},{10,9... | collective-permute-start | bytes 786440 | tf_op jit(solution)/shard_map/ppermute | solution.py:322
  108.7 5.0 %collective-permute-done.12 = f32[1,256,256]{2,1,0:T(8,128)S(1)} collective-permute-done((f32[1,256,256]{2,1,0:T(8,128)S(1)}, f32[1,256,256]{2,1,0:T(8,128)S(1)}, u32[]{:S(2)}, u32[]{:S(2)}) %collective-permute-start.12) | collective-permute-done | bytes 262176 | tf_op jit(solution)/shard_map/ppermute | solution.py:322
  116.8 3.4 %collective-permute-start.13 = (f32[1,256,256]{2,1,0:T(8,128)S(1)}, f32[1,256,256]{2,1,0:T(8,128)S(1)}, u32[]{:S(2)}, u32[]{:S(2)}) collective-permute-start(f32[1,256,256]{2,1,0:T(8,128)S(1)} %get-tuple-element.17), channel_id=1, source_target_pairs={{0,1},{1,2},{2,3},{3,4},{4,5},{5,6},{6,7},{7,0},{8,9},{9,10},{10,1... | collective-permute-start | bytes 786440 | tf_op jit(solution)/shard_map/ppermute | solution.py:322
  128.2 11.9 %all_to_all.37.grams_ref = f32[8,16,256]{2,1,0:T(8,128)} all-to-all(f32[8,16,256]{2,1,0:T(8,128)} %bitcast.28), channel_id=1, replica_groups=mesh['row'=64,'col'=8] {'col'}, dimensions={0} | all-to-all | bytes 262144 | tf_op jit(solution)/shard_map/all_to_all | solution.py:343
  141.7 31.4 %all_to_all.38 = f32[64,1,128]{2,1,0:T(1,128)} all-to-all(f32[64,1,128]{2,1,0:T(1,128)} %bitcast.32), channel_id=1, replica_groups=mesh['row'=64,'col'=8] {'row'}, dimensions={0} | all-to-all | bytes 65536 | tf_op jit(solution)/shard_map/all_to_all | solution.py:343
  175.6 13.9 %all_to_all.39 = f32[64,1,256]{2,1,0:T(1,128)S(1)} all-to-all(f32[64,1,256]{2,1,0:T(1,128)S(1)} %copy.9), channel_id=1, replica_groups=mesh['row'=64,'col'=8] {'row'}, dimensions={0} | all-to-all | bytes 131072 | tf_op jit(solution)/shard_map/all_to_all | solution.py:343
  191.7 16.0 %all_to_all.40.received_ref = f32[8,4,16,128]{3,2,1,0:T(8,128)} all-to-all(f32[8,4,16,128]{3,2,1,0:T(8,128)} %gram_message.1), channel_id=1, replica_groups=mesh['row'=64,'col'=8] {'col'}, dimensions={0} | all-to-all | bytes 524288 | tf_op jit(solution)/shard_map/all_to_all | solution.py:343
  207.7 11.7 %node_bases.1 = (f32[8,3,32,128]{3,2,1,0:T(8,128)}, f32[32,128]{1,0:T(8,128)}) custom-call(s32[2]{0:T(128)} %pad_add_fusion.index_ref.row_ref, f32[8,4,16,128]{3,2,1,0:T(8,128)} %all_to_all.40.received_ref, f32[128,256]{1,0:T(8,128)} %get-tuple-element.10.gram_ref, f32[256,256]{1,0:T(8,128)} %get-tuple-element.13.sample_ref), custom_call_target="tpu_custom_call" | custom-call | tf_op jit(solution)/shard_map/node_bases/pallas_call | solution.py:303
  219.4 16.9 %all_to_all.41 = f32[8,3,32,128]{3,2,1,0:T(8,128)S(1)} all-to-all(f32[8,3,32,128]{3,2,1,0:T(8,128)} %get-tuple-element.14), channel_id=1, replica_groups=mesh['row'=64,'col'=8] {'col'}, dimensions={0} | all-to-all | bytes 786432 | tf_op jit(solution)/shard_map/all_to_all | solution.py:343
  (68 shorter events, 50.5 us)
Async XLA Ops:
  0.6 17.7 %collective-permute-start.2 = (f32[1,256,256]{2,1,0:T(8,128)}, f32[1,256,256]{2,1,0:T(8,128)S(1)}, u32[]{:S(2)}, u32[]{:S(2)}) collective-permute-start(f32[1,256,256]{2,1,0:T(8,128)} %panel_ref.1), channel_id=1, source_target_pairs={{0,1},{1,2},{2,3},{3,4},{4,5},{5,6},{6,7},{7,0},{8,9},{9,10},{10,1... | collective-permute-start | bytes 786440 | tf_op jit(solution)/shard_map/ppermute | solution.py:322
  5.5 14.8 %collective-permute-start = (f32[1,256,256]{2,1,0:T(8,128)}, f32[1,256,256]{2,1,0:T(8,128)S(1)}, u32[]{:S(2)}, u32[]{:S(2)}) collective-permute-start(f32[1,256,256]{2,1,0:T(8,128)} %panel_ref.1), channel_id=1, source_target_pairs={{0,7},{1,0},{2,1},{3,2},{4,3},{5,4},{6,5},{7,6},{8,15},{9,8},{10,9... | collective-permute-start | bytes 786440 | tf_op jit(solution)/shard_map/ppermute | solution.py:322
  18.3 30.8 %copy-start.3 = (f32[1,256,256]{2,1,0:T(8,128)}, f32[1,256,256]{2,1,0:T(8,128)S(1)}, u32[]{:S(2)}) copy-start(f32[1,256,256]{2,1,0:T(8,128)S(1)} %collective-permute-done.2.refs_5_) | copy-start | bytes 786436
  18.3 9.7 %collective-permute-start.3 = (f32[1,256,256]{2,1,0:T(8,128)S(1)}, f32[1,256,256]{2,1,0:T(8,128)S(1)}, u32[]{:S(2)}, u32[]{:S(2)}) collective-permute-start(f32[1,256,256]{2,1,0:T(8,128)S(1)} %collective-permute-done.2.refs_5_), channel_id=1, source_target_pairs={{0,1},{1,2},{2,3},{3,4},{4,5},{5,6},{6,7},{7,0},{8,9},{9,10},{10,1... | collective-permute-start | bytes 786440 | tf_op jit(solution)/shard_map/ppermute | solution.py:322
  20.3 28.9 %copy-start.4 = (f32[1,256,256]{2,1,0:T(8,128)}, f32[1,256,256]{2,1,0:T(8,128)S(1)}, u32[]{:S(2)}) copy-start(f32[1,256,256]{2,1,0:T(8,128)S(1)} %collective-permute-done.refs_3_) | copy-start | bytes 786436
  20.3 9.7 %collective-permute-start.1 = (f32[1,256,256]{2,1,0:T(8,128)S(1)}, f32[1,256,256]{2,1,0:T(8,128)S(1)}, u32[]{:S(2)}, u32[]{:S(2)}) collective-permute-start(f32[1,256,256]{2,1,0:T(8,128)S(1)} %collective-permute-done.refs_3_), channel_id=1, source_target_pairs={{0,7},{1,0},{2,1},{3,2},{4,3},{5,4},{6,5},{7,6},{8,15},{9,8},{10,9... | collective-permute-start | bytes 786440 | tf_op jit(solution)/shard_map/ppermute | solution.py:322
  28.0 21.1 %copy-start.5 = (f32[1,256,256]{2,1,0:T(8,128)}, f32[1,256,256]{2,1,0:T(8,128)S(1)}, u32[]{:S(2)}) copy-start(f32[1,256,256]{2,1,0:T(8,128)S(1)} %collective-permute-done.3.refs_6_) | copy-start | bytes 786436
  28.0 13.6 %collective-permute-start.5 = (f32[1,256,256]{2,1,0:T(8,128)S(1)}, f32[1,256,256]{2,1,0:T(8,128)S(1)}, u32[]{:S(2)}, u32[]{:S(2)}) collective-permute-start(f32[1,256,256]{2,1,0:T(8,128)S(1)} %collective-permute-done.3.refs_6_), channel_id=1, source_target_pairs={{0,1},{1,2},{2,3},{3,4},{4,5},{5,6},{6,7},{7,0},{8,9},{9,10},{10,1... | collective-permute-start | bytes 786440 | tf_op jit(solution)/shard_map/ppermute | solution.py:322
  30.0 19.2 %copy-start.6 = (f32[1,256,256]{2,1,0:T(8,128)}, f32[1,256,256]{2,1,0:T(8,128)S(1)}, u32[]{:S(2)}) copy-start(f32[1,256,256]{2,1,0:T(8,128)S(1)} %collective-permute-done.1.refs_2_) | copy-start | bytes 786436
  33.1 28.3 %copy-start.12 = (s32[8,1]{0,1:T(1,128)S(1)}, s32[8,1]{0,1:T(1,128)}, u32[]{:S(2)}) copy-start(s32[8,1]{0,1:T(1,128)} %param.5) | copy-start | bytes 100
  34.6 35.5 %collective-permute-start.9 = (f32[5,256,256]{2,1,0:T(8,128)}, f32[5,256,256]{2,1,0:T(8,128)S(1)}, u32[]{:S(2)}, u32[]{:S(2)}) collective-permute-start(f32[5,256,256]{2,1,0:T(8,128)} %constant_dynamic-update-slice_fusion), channel_id=1, source_target_pairs={{8,0},{16,8},{24,16},{32,24},{40,32},{48,40},{56,48},{64,56},{72,6... | collective-permute-start | bytes 3932168 | tf_op jit(solution)/shard_map/ppermute | solution.py:317
  38.6 31.5 %collective-permute-start.4 = (f32[5,256,256]{2,1,0:T(8,128)}, f32[5,256,256]{2,1,0:T(8,128)S(1)}, u32[]{:S(2)}, u32[]{:S(2)}) collective-permute-start(f32[5,256,256]{2,1,0:T(8,128)} %constant_dynamic-update-slice_fusion), channel_id=1, source_target_pairs={{0,8},{8,16},{16,24},{24,32},{32,40},{40,48},{48,56},{56,64},{64,7... | collective-permute-start | bytes 3932168 | tf_op jit(solution)/shard_map/ppermute | solution.py:317
  41.6 12.9 %copy-start.7 = (f32[1,256,256]{2,1,0:T(8,128)}, f32[1,256,256]{2,1,0:T(8,128)S(1)}, u32[]{:S(2)}) copy-start(f32[1,256,256]{2,1,0:T(8,128)S(1)} %collective-permute-done.5.refs_7_) | copy-start | bytes 786436
  41.6 11.1 %collective-permute-start.6 = (f32[1,256,256]{2,1,0:T(8,128)S(1)}, f32[1,256,256]{2,1,0:T(8,128)S(1)}, u32[]{:S(2)}, u32[]{:S(2)}) collective-permute-start(f32[1,256,256]{2,1,0:T(8,128)S(1)} %collective-permute-done.5.refs_7_), channel_id=1, source_target_pairs={{0,1},{1,2},{2,3},{3,4},{4,5},{5,6},{6,7},{7,0},{8,9},{9,10},{10,1... | collective-permute-start | bytes 786440 | tf_op jit(solution)/shard_map/ppermute | solution.py:322
  43.5 11.0 %collective-permute-start.7 = (f32[1,256,256]{2,1,0:T(8,128)S(1)}, f32[1,256,256]{2,1,0:T(8,128)S(1)}, u32[]{:S(2)}, u32[]{:S(2)}) collective-permute-start(f32[1,256,256]{2,1,0:T(8,128)S(1)} %collective-permute-done.1.refs_2_), channel_id=1, source_target_pairs={{0,7},{1,0},{2,1},{3,2},{4,3},{5,4},{6,5},{7,6},{8,15},{9,8},{10,9... | collective-permute-start | bytes 786440 | tf_op jit(solution)/shard_map/ppermute | solution.py:322
  55.3 13.5 %collective-permute-start.10 = (f32[3,256,256]{2,1,0:T(8,128)}, f32[3,256,256]{2,1,0:T(8,128)S(1)}, u32[]{:S(2)}, u32[]{:S(2)}) collective-permute-start(f32[3,256,256]{2,1,0:T(8,128)} %constant_dynamic-update-slice_fusion.5), channel_id=1, source_target_pairs={{8,0},{16,8},{24,16},{32,24},{40,32},{48,40},{56,48},{64,56},{72,6... | collective-permute-start | bytes 2359304 | tf_op jit(solution)/shard_map/ppermute | solution.py:317
  57.5 12.6 %collective-permute-start.8 = (f32[3,256,256]{2,1,0:T(8,128)}, f32[3,256,256]{2,1,0:T(8,128)}, u32[]{:S(2)}, u32[]{:S(2)}) collective-permute-start(f32[3,256,256]{2,1,0:T(8,128)} %constant_dynamic-update-slice_fusion.5), channel_id=1, source_target_pairs={{0,8},{8,16},{16,24},{24,32},{32,40},{40,48},{48,56},{56,64},{64,7... | collective-permute-start | bytes 2359304 | tf_op jit(solution)/shard_map/ppermute | solution.py:317
  76.9 13.5 %collective-permute-start.14 = (f32[1,256,256]{2,1,0:T(8,128)S(1)}, f32[1,256,256]{2,1,0:T(8,128)S(1)}, u32[]{:S(2)}, u32[]{:S(2)}) collective-permute-start(f32[1,256,256]{2,1,0:T(8,128)S(1)} %get-tuple-element.20), channel_id=1, source_target_pairs={{0,7},{1,0},{2,1},{3,2},{4,3},{5,4},{6,5},{7,6},{8,15},{9,8},{10,9... | collective-permute-start | bytes 786440 | tf_op jit(solution)/shard_map/ppermute | solution.py:322
  82.1 13.9 %collective-permute-start.11 = (f32[1,256,256]{2,1,0:T(8,128)S(1)}, f32[1,256,256]{2,1,0:T(8,128)S(1)}, u32[]{:S(2)}, u32[]{:S(2)}) collective-permute-start(f32[1,256,256]{2,1,0:T(8,128)S(1)} %get-tuple-element.21), channel_id=1, source_target_pairs={{0,1},{1,2},{2,3},{3,4},{4,5},{5,6},{6,7},{7,0},{8,9},{9,10},{10,1... | collective-permute-start | bytes 786440 | tf_op jit(solution)/shard_map/ppermute | solution.py:322
  91.4 7.9 %collective-permute-start.15 = (f32[1,256,256]{2,1,0:T(8,128)S(1)}, f32[1,256,256]{2,1,0:T(8,128)S(1)}, u32[]{:S(2)}, u32[]{:S(2)}) collective-permute-start(f32[1,256,256]{2,1,0:T(8,128)S(1)} %slice_add_fusion.2), channel_id=1, source_target_pairs={{0,7},{1,0},{2,1},{3,2},{4,3},{5,4},{6,5},{7,6},{8,15},{9,8},{10,9... | collective-permute-start | bytes 786440 | tf_op jit(solution)/shard_map/ppermute | solution.py:322
  100.4 8.3 %collective-permute-start.16 = (f32[1,256,256]{2,1,0:T(8,128)S(1)}, f32[1,256,256]{2,1,0:T(8,128)S(1)}, u32[]{:S(2)}, u32[]{:S(2)}) collective-permute-start(f32[1,256,256]{2,1,0:T(8,128)S(1)} %get-tuple-element.18), channel_id=1, source_target_pairs={{0,7},{1,0},{2,1},{3,2},{4,3},{5,4},{6,5},{7,6},{8,15},{9,8},{10,9... | collective-permute-start | bytes 786440 | tf_op jit(solution)/shard_map/ppermute | solution.py:322
  105.4 8.3 %collective-permute-start.12 = (f32[1,256,256]{2,1,0:T(8,128)S(1)}, f32[1,256,256]{2,1,0:T(8,128)S(1)}, u32[]{:S(2)}, u32[]{:S(2)}) collective-permute-start(f32[1,256,256]{2,1,0:T(8,128)S(1)} %get-tuple-element.19), channel_id=1, source_target_pairs={{0,1},{1,2},{2,3},{3,4},{4,5},{5,6},{6,7},{7,0},{8,9},{9,10},{10,1... | collective-permute-start | bytes 786440 | tf_op jit(solution)/shard_map/ppermute | solution.py:322
  114.9 7.1 %collective-permute-start.17 = (f32[1,256,256]{2,1,0:T(8,128)S(1)}, f32[1,256,256]{2,1,0:T(8,128)S(1)}, u32[]{:S(2)}, u32[]{:S(2)}) collective-permute-start(f32[1,256,256]{2,1,0:T(8,128)S(1)} %get-tuple-element.16), channel_id=1, source_target_pairs={{0,7},{1,0},{2,1},{3,2},{4,3},{5,4},{6,5},{7,6},{8,15},{9,8},{10,9... | collective-permute-start | bytes 786440 | tf_op jit(solution)/shard_map/ppermute | solution.py:322
  116.8 8.3 %collective-permute-start.13 = (f32[1,256,256]{2,1,0:T(8,128)S(1)}, f32[1,256,256]{2,1,0:T(8,128)S(1)}, u32[]{:S(2)}, u32[]{:S(2)}) collective-permute-start(f32[1,256,256]{2,1,0:T(8,128)S(1)} %get-tuple-element.17), channel_id=1, source_target_pairs={{0,1},{1,2},{2,3},{3,4},{4,5},{5,6},{6,7},{7,0},{8,9},{9,10},{10,1... | collective-permute-start | bytes 786440 | tf_op jit(solution)/shard_map/ppermute | solution.py:322
  (7 other events, 12.8 us)

commit v3 on v1

--- a/solution.py
+++ b/solution.py
@@ -87,57 +87,39 @@
     return jax.ShapeDtypeStruct(dims, jnp.float32)
 
 
-def near_products(offsets, near_blocks, low, own, high):
-    leaf_count, _, size, _ = near_blocks.shape
-    width = own.shape[2]
-
-    def kernel(offset_ref, near_ref, low_ref, own_ref, high_ref, out_ref):
-        offset = offset_ref[pl.program_id(0)]
-        for part, ref in enumerate((low_ref, own_ref, high_ref)):
-
-            @pl.when(offset // leaf_count == part)
-            def _():
-                out_ref[0] = dot(near_ref[0, 0], ref[0], ((1,), (0,)))
-
-    def panel_spec(part):
-        return pl.BlockSpec(
-            (1, size, width),
-            lambda i, offset_ref: (jnp.clip(offset_ref[i] - part * leaf_count, 0, leaf_count - 1), 0, 0),
-        )
-
+def leaf_sample(index, offsets, near, panels, panel, nugget):
+    parts, size, width = panels[0].shape
+    split = size // 2
+
+    def kernel(index_ref, offset_ref, near_ref, more_ref, *refs):
+        panel_refs, (panel_ref, nugget_ref, sample_ref, gram_ref, buffer, sems) = refs[:3], refs[3:]
+        for k in range(parts):
+            offset = offset_ref[k]
+            for part, ref in enumerate(panel_refs):
+
+                @pl.when(offset // parts == part)
+                def _():
+                    pltpu.make_async_copy(ref.at[lax.rem(offset, parts)], buffer.at[k], sems.at[k]).start()
+
+        row = nugget_ref[pl.ds(index_ref[1], 1), :]
+        column = jnp.broadcast_to(row, (8, size)).T[:, :1]
+        sample_ref[...] = column * panel_ref[0]
+        for k in range(parts):
+            pltpu.make_async_copy(panel_refs[0].at[0], buffer.at[k], sems.at[k]).wait()
+            sample_ref[:split] += dot(near_ref[k, :split], buffer[k], ((1,), (0,)))
+            sample_ref[split:] += dot(more_ref[k], buffer[k], ((1,), (0,)))
+        gram_ref[...] = dot(sample_ref[:, : width // 2], sample_ref[...], ((0,), (0,)))
+
+    anywhere = pl.BlockSpec(memory_space=pl.ANY)
+    smem = pl.BlockSpec(memory_space=pltpu.SMEM)
     return pl.pallas_call(
         kernel,
-        grid_spec=pltpu.PrefetchScalarGridSpec(
-            num_scalar_prefetch=1,
-            grid=(leaf_count,),
-            in_specs=[
-                pl.BlockSpec((1, 1, size, size), lambda i, offset_ref: (i, 0, 0, 0)),
-                panel_spec(0),
-                panel_spec(1),
-                panel_spec(2),
-            ],
-            out_specs=pl.BlockSpec((1, size, width), lambda i, offset_ref: (i, 0, 0)),
-        ),
-        out_shape=shape(leaf_count, size, width),
-        name="near_products",
-    )(offsets, near_blocks, low, own, high)
-
-
-def leaf_grams(partial_sum, panel, nugget):
-    size, width = panel.shape
-
-    def kernel(sum_ref, panel_ref, nugget_ref, sample_ref, gram_ref):
-        sample = sum_ref[...] + nugget_ref[...] * panel_ref[...]
-        sample_ref[...] = sample
-        gram_ref[...] = dot(sample[:, : width // 2], sample, ((0,), (0,)))
-
-    return pl.pallas_call(
-        kernel,
-        in_specs=[vmem()] * 3,
+        in_specs=[smem, smem, vmem(), vmem()] + [anywhere] * 3 + [vmem()] * 2,
         out_specs=[vmem()] * 2,
         out_shape=[shape(size, width), shape(width // 2, width)],
-        name="leaf_grams",
-    )(partial_sum, panel, nugget)
+        scratch_shapes=[pltpu.VMEM((parts, size, width), jnp.float32), pltpu.SemaphoreType.DMA((parts,))],
+        name="leaf_sample",
+    )(index, offsets, *near, *panels, panel, nugget)
 
 
 def node_children(leaf_count):
@@ -261,41 +243,22 @@
 
         @pl.when(jnp.logical_not(root))
         def _():
-            upper_ref[...] = dot(m_ref[5], u_ref[4, pl.ds(at, share), :], ((1,), (1,)))
+            upper_ref[...] = dot(u_ref[4, pl.ds(at, share), :], m_ref[5], ((1,), (1,)))
 
         @pl.when(root)
         def _():
             reduced_root = dot(m_ref[5], u_ref[4], ((1,), (0,)))
             u_ref[0] = jnp.where(column < parts // 2, u_ref[5], reduced_root).T * root_scale
-            upper_ref[...] = u_ref[0, pl.ds(at, share), :].T
+            upper_ref[...] = u_ref[0, pl.ds(at, share), :]
 
     return pl.pallas_call(
         kernel,
         in_specs=[pl.BlockSpec(memory_space=pltpu.SMEM), vmem(), vmem(), vmem()],
         out_specs=[vmem()] * 2,
-        out_shape=[shape(parts, 3, share, half), shape(half, share)],
+        out_shape=[shape(parts, 3, share, half), shape(share, half)],
         scratch_shapes=[pltpu.VMEM((6, half, half), jnp.float32)] * 2,
         name="node_bases",
     )(index, received, gram, sample)
-
-
-def placed_outputs(received):
-    parts, _, share, half = received.shape
-
-    def kernel(received_ref, basis_ref, miss_ref, local_ref):
-        for c in range(parts):
-            basis_ref[c] = received_ref[c, 0].T
-            miss_ref[c] = received_ref[c, 1].T
-            if c < parts - 1:
-                local_ref[c] = received_ref[c, 2].T
-
-    return pl.pallas_call(
-        kernel,
-        in_specs=[vmem()],
-        out_specs=[vmem()] * 3,
-        out_shape=[shape(parts, half, share), shape(parts, half, share), shape(parts - 1, half, share)],
-        name="placed_outputs",
-    )(received)
 
 
 def neighbours(block):
@@ -318,14 +281,16 @@
     row_index = lax.axis_index("row")
     col_index = lax.axis_index("col")
     index = jnp.stack([row_index, col_index]).astype(jnp.int32)
-    offsets = (column_block - (row_index - 1) * leaf_count).reshape(-1)
-
+
+    split = size // 2
+    number = jnp.broadcast_to(column_block[:, :, None].astype(jnp.float32), (leaf_count, 8, size))
+    near = exchange(jnp.concatenate([near_blocks[:, 0, :split], number], axis=1), "col")
     own = lax.all_gather(test_panels, "col", axis=0, tiled=True)
+    rest, own = lax.optimization_barrier((near_blocks[:, 0, split:], own))
     low, high = neighbours(own)
-    partial_sums = near_products(offsets, near_blocks, low, own, high)
-    summed = lax.psum_scatter(partial_sums, "col", scatter_dimension=0, tiled=True)
-    own_nugget = lax.dynamic_slice_in_dim(nugget, col_index, 1, 0).reshape(size, 1)
-    sample, gram = leaf_grams(summed[0], test_panels[0], own_nugget)
+    more = exchange(rest, "col")
+    offsets = near[:, split, 0].astype(jnp.int32) - (row_index - 1) * leaf_count
+    sample, gram = leaf_sample(index, offsets, (near, more), (low, own, high), test_panels, nugget)
 
     grams = exchange(gram.reshape(col_count, half // col_count, 2 * half), "col")
     local, sums = local_sums(grams, row_count)
@@ -333,8 +298,9 @@
     received = exchange(gram_message(local, sums, index), "col")
     root_scale = 1.0 / math.sqrt(leaf_count * row_count * size)
     message, upper = node_bases(index, received, gram, sample, root_scale)
-    leaf_basis, leaf_miss, local_basis = placed_outputs(exchange(message, "col"))
-    return leaf_basis, leaf_miss, local_basis, upper[None]
+    outputs = exchange(message, "col")
+    stored = (outputs[:, 0], outputs[:, 1], outputs[: col_count - 1, 2], upper[None])
+    return tuple(jnp.swapaxes(output, 1, 2) for output in stored)
 
 
 def solution(mesh):

time: 265 us -> 229 us (0.86)
  waiting for transfers between devices: 136 us -> 78.2 us
  blocking collectives: 53.4 us -> 80.4 us
  Pallas kernels: 29.7 us -> 22.6 us
  starting transfers between devices: 17.7 us -> 22.5 us
  local copies, waits for them, and re-layouts: 10.8 us -> 6.72 us
    reduce_scatter x1 -> x0, waiting for transfers between devices: 41.2 us -> none  [on_device(): lax.psum_scatter(partial_sums, 'col', scatter_dimension=0, tiled=True)]
    all_to_all x3 -> x5, blocking collectives: 53.4 us -> 80.4 us  [exchange(): return lax.all_to_all(block, axis, 0, 0, tiled=True)]
    ppermute x1, waiting for transfers between devices: 20.2 us -> 0.01 us  [neighbours(): lax.ppermute(block, 'row', forward)]
    all_to_all x2, starting transfers between devices: 7.97 us -> 15.3 us  [exchange(): return lax.all_to_all(block, axis, 0, 0, tiled=True)]
    pallas_call x3 -> x1, Pallas kernels: 13.2 us -> 6.11 us  [leaf_sample(): pl.pallas_call(kernel, in_specs=[smem, smem, vmem(), vmem()] + [anywhere]...]
    unnamed x11 -> x5, local copies, waits for them, and re-layouts: 8.49 us -> 1.66 us
    all_to_all x2, waiting for transfers between devices: 22 us -> 27.9 us  [exchange(): return lax.all_to_all(block, axis, 0, 0, tiled=True)]
    ppermute x1, starting transfers between devices: 7.74 us -> 3.02 us  [neighbours(): lax.ppermute(block, 'row', forward)]
  transfers between devices with their start and end apart: 6 -> 5, of which waited for: 6 -> 2; matrix products, arithmetic and copies ran while one was open for 2% -> 3% of each run, Pallas kernels for 0% -> 0%
where the time goes in v3:
time: 229 us; the launch traced here: 228 us
  blocking collectives  80.4 us (35%)
  waiting for transfers between devices  78.2 us (34%)
  Pallas kernels  22.6 us (10%)
  starting transfers between devices  22.5 us (10%)
  between operations  14.1 us (6%)
  local copies, waits for them, and re-layouts  6.72 us (3%)
  other arithmetic  3.1 us (1%)
    all_to_all x5, blocking collectives, exchange(): return lax.all_to_all(block, axis, 0, 0, tiled=True)  80.4 us
    all_gather x1, waiting for transfers between devices, on_device(): own = lax.all_gather(test_panels, 'col', axis=0, tiled=True)  49.7 us
    all_to_all x2, waiting for transfers between devices, exchange(): return lax.all_to_all(block, axis, 0, 0, tiled=True)  27.9 us
    all_to_all x2, starting transfers between devices, exchange(): return lax.all_to_all(block, axis, 0, 0, tiled=True)  15.3 us
    pallas_call x1, Pallas kernels, node_bases(): pl.pallas_call(kernel, in_specs=[pl.BlockSpec(memory_space=pltpu.SMEM), v...  11.7 us
    pallas_call x1, Pallas kernels, leaf_sample(): pl.pallas_call(kernel, in_specs=[smem, smem, vmem(), vmem()] + [anywhere]...  6.11 us
  transfers between devices with their start and end apart: 5, of which 2 were waited for; matrix products, arithmetic and copies ran while one was open for 3% of the time, Pallas kernels for 0%

profile of v3, /device:TPU:1, one launch (start us, length us, event | category | flops | bytes accessed | tf_op | source)
XLA Modules:
  0.0 227.6 jit_solution(12331450730825733302)
XLA Ops:
  7.2 0.7 all-gather.2.cloned.1.call-update
  7.9 0.7 convert_bitcast_fusion
  8.6 2.7 %slice_bitcast_fusion = (f32[8,128,256]{2,1,0:T(8,128)}, f32[8,128,256]{2,1,0:T(8,128)S(1)}) fusion(f32[8,1,256,256]{3,2,0,1:T(8,128)} %bitcast.33), kind=kLoop, calls=%fused_computation.1 | loop fusion | bytes 4194304 | tf_op jit(solution)/shard_map/squeeze | solution.py:289
  11.3 1.1 pad_maximum_fusion
  12.4 10.9 %all-to-all-start = ((f32[8,136,256]{2,1,0:T(8,128)}), f32[8,136,256]{2,1,0:T(8,128)S(1)}, u32[]{:S(2)}, u32[]{:S(2)}) async-start(f32[8,136,256]{2,1,0:T(8,128)} %pad_maximum_fusion), calls=%async_computation | async-start | bytes 2228224 | tf_op jit(solution)/shard_map/all_to_all | solution.py:272
  23.3 49.7 %all-gather.2.cloned.1.call-done.refs_1_ = f32[8,256,256]{2,1,0:T(8,128)} async-done(((f32[1,256,256]{2,1,0:T(8,128)}), f32[8,256,256]{2,1,0:T(8,128)}) %all-gather.2.cloned.1.call-update) | async-done | bytes 2097168 | tf_op jit(solution)/shard_map/all_gather | solution.py:288
  73.0 4.1 %collective-permute-start.1 = (f32[8,256,256]{2,1,0:T(8,128)}, f32[8,256,256]{2,1,0:T(8,128)}, u32[]{:S(2)}, u32[]{:S(2)}) collective-permute-start(f32[8,256,256]{2,1,0:T(8,128)} %all-gather.2.cloned.1.call-done.refs_1_), channel_id=1, source_target_pairs={{8,0},{16,8},{24,16},{32,24},{40,32},{48,40},{56,48},{64,56},{72,6... | collective-permute-start | bytes 6291464 | tf_op jit(solution)/shard_map/ppermute | solution.py:268
  77.1 3.0 %collective-permute-start = (f32[8,256,256]{2,1,0:T(8,128)}, f32[8,256,256]{2,1,0:T(8,128)}, u32[]{:S(2)}, u32[]{:S(2)}) collective-permute-start(f32[8,256,256]{2,1,0:T(8,128)} %all-gather.2.cloned.1.call-done.refs_1_), channel_id=1, source_target_pairs={{0,8},{8,16},{16,24},{24,32},{32,40},{40,48},{48,56},{56,64},{64,7... | collective-permute-start | bytes 6291464 | tf_op jit(solution)/shard_map/ppermute | solution.py:268
  80.2 4.4 %all-to-all-start.1 = ((f32[8,128,256]{2,1,0:T(8,128)}), f32[8,128,256]{2,1,0:T(8,128)S(1)}, u32[]{:S(2)}, u32[]{:S(2)}) async-start(f32[8,128,256]{2,1,0:T(8,128)} %get-tuple-element.12), calls=%async_computation.1 | async-start | bytes 2097152 | tf_op jit(solution)/shard_map/all_to_all | solution.py:272
  85.2 0.8 fusion.1.offset_ref
  86.0 27.9 %all-to-all-done.1.more_ref = f32[8,128,256]{2,1,0:T(8,128)S(1)} async-done(((f32[8,128,256]{2,1,0:T(8,128)}), f32[8,128,256]{2,1,0:T(8,128)S(1)}, u32[]{:S(2)}, u32[]{:S(2)}) %all-to-all-start.1) | async-done | bytes 1048608 | tf_op jit(solution)/shard_map/all_to_all | solution.py:272
  113.8 1.0 copy-done.1
  114.8 6.1 %leaf_sample.1 = (f32[256,256]{1,0:T(8,128)}, f32[128,256]{1,0:T(8,128)}) custom-call(s32[2]{0:T(128)} %pad_add_fusion.index_ref.row_ref, s32[8]{0:T(128)} %fusion.1.offset_ref, f32[8,136,256]{2,1,0:T(8,128)} %copy-done, f32[8,128,256]{2,1,0:T(8,128)} %copy-done.1, f32[8,256,256]{2,1,0:T(8,128)} %collective-permute-done.refs_0_, ...), custom_call_target="tpu_custom_call" | custom-call | tf_op jit(solution)/shard_map/leaf_sample/pallas_call | solution.py:115
  121.0 12.1 %all_to_all.47.grams_ref = f32[8,16,256]{2,1,0:T(8,128)} all-to-all(f32[8,16,256]{2,1,0:T(8,128)} %bitcast.34), channel_id=1, replica_groups=mesh['row'=64,'col'=8] {'col'}, dimensions={0} | all-to-all | bytes 262144 | tf_op jit(solution)/shard_map/all_to_all | solution.py:272
  133.1 1.6 local_sums.1
  134.7 21.3 %all_to_all.48 = f32[64,1,128]{2,1,0:T(1,128)} all-to-all(f32[64,1,128]{2,1,0:T(1,128)} %bitcast.38), channel_id=1, replica_groups=mesh['row'=64,'col'=8] {'row'}, dimensions={0} | all-to-all | bytes 65536 | tf_op jit(solution)/shard_map/all_to_all | solution.py:272
  155.9 1.6 tree_sums.1
  157.5 0.9 copy.15
  158.4 14.1 %all_to_all.49 = f32[64,1,256]{2,1,0:T(1,128)S(1)} all-to-all(f32[64,1,256]{2,1,0:T(1,128)S(1)} %copy.15), channel_id=1, replica_groups=mesh['row'=64,'col'=8] {'row'}, dimensions={0} | all-to-all | bytes 131072 | tf_op jit(solution)/shard_map/all_to_all | solution.py:272
  173.2 1.6 gram_message.1
  174.8 16.0 %all_to_all.50.received_ref = f32[8,4,16,128]{3,2,1,0:T(8,128)} all-to-all(f32[8,4,16,128]{3,2,1,0:T(8,128)} %gram_message.1), channel_id=1, replica_groups=mesh['row'=64,'col'=8] {'col'}, dimensions={0} | all-to-all | bytes 524288 | tf_op jit(solution)/shard_map/all_to_all | solution.py:272
  190.8 11.7 %node_bases.1 = (f32[8,3,32,128]{3,2,1,0:T(8,128)}, f32[32,128]{1,0:T(8,128)}) custom-call(s32[2]{0:T(128)} %pad_add_fusion.index_ref.row_ref, f32[8,4,16,128]{3,2,1,0:T(8,128)} %all_to_all.50.received_ref, f32[128,256]{1,0:T(8,128)} %get-tuple-element.14.gram_ref, f32[256,256]{1,0:T(8,128)} %get-tuple-element.17.sample_ref), custom_call_target="tpu_custom_call" | custom-call | tf_op jit(solution)/shard_map/node_bases/pallas_call | solution.py:254
  202.5 16.9 %all_to_all.51 = f32[8,3,32,128]{3,2,1,0:T(8,128)S(1)} all-to-all(f32[8,3,32,128]{3,2,1,0:T(8,128)} %get-tuple-element.18), channel_id=1, replica_groups=mesh['row'=64,'col'=8] {'col'}, dimensions={0} | all-to-all | bytes 786432 | tf_op jit(solution)/shard_map/all_to_all | solution.py:272
  220.1 0.7 slice_bitcast_fusion.2
  (11 shorter events, 2.0 us)
Async XLA Ops:
  7.2 65.8 %all-gather.2.cloned.1.call-start = ((), (), s32[]{:S(2)}) async-start(), calls=%async_computation.7 | async-start | bytes 2359296 | tf_op jit(solution)/shard_map/all_gather | solution.py:288
  12.4 67.7 %all-to-all-start = ((f32[8,136,256]{2,1,0:T(8,128)}), f32[8,136,256]{2,1,0:T(8,128)S(1)}, u32[]{:S(2)}, u32[]{:S(2)}) async-start(f32[8,136,256]{2,1,0:T(8,128)} %pad_maximum_fusion), calls=%async_computation | async-start | bytes 2228224 | tf_op jit(solution)/shard_map/all_to_all | solution.py:272
  73.0 40.8 %collective-permute-start.1 = (f32[8,256,256]{2,1,0:T(8,128)}, f32[8,256,256]{2,1,0:T(8,128)}, u32[]{:S(2)}, u32[]{:S(2)}) collective-permute-start(f32[8,256,256]{2,1,0:T(8,128)} %all-gather.2.cloned.1.call-done.refs_1_), channel_id=1, source_target_pairs={{8,0},{16,8},{24,16},{32,24},{40,32},{48,40},{56,48},{64,56},{72,6... | collective-permute-start | bytes 6291464 | tf_op jit(solution)/shard_map/ppermute | solution.py:268
  77.1 36.7 %collective-permute-start = (f32[8,256,256]{2,1,0:T(8,128)}, f32[8,256,256]{2,1,0:T(8,128)}, u32[]{:S(2)}, u32[]{:S(2)}) collective-permute-start(f32[8,256,256]{2,1,0:T(8,128)} %all-gather.2.cloned.1.call-done.refs_1_), channel_id=1, source_target_pairs={{0,8},{8,16},{16,24},{24,32},{32,40},{40,48},{48,56},{56,64},{64,7... | collective-permute-start | bytes 6291464 | tf_op jit(solution)/shard_map/ppermute | solution.py:268
  80.2 33.7 %copy-start = (f32[8,136,256]{2,1,0:T(8,128)}, f32[8,136,256]{2,1,0:T(8,128)S(1)}, u32[]{:S(2)}) copy-start(f32[8,136,256]{2,1,0:T(8,128)S(1)} %all-to-all-done.near_ref) | copy-start | bytes 3342340
  80.2 33.6 %all-to-all-start.1 = ((f32[8,128,256]{2,1,0:T(8,128)}), f32[8,128,256]{2,1,0:T(8,128)S(1)}, u32[]{:S(2)}, u32[]{:S(2)}) async-start(f32[8,128,256]{2,1,0:T(8,128)} %get-tuple-element.12), calls=%async_computation.1 | async-start | bytes 2097152 | tf_op jit(solution)/shard_map/all_to_all | solution.py:272
  113.8 1.0 copy-start.1
Sparse Core Ops, SparseCore 0:
  10.1 62.8 all-gather.1

commit v4 on v3

--- a/solution.py
+++ b/solution.py
@@ -87,12 +87,20 @@
     return jax.ShapeDtypeStruct(dims, jnp.float32)
 
 
+PIECE = 32
+
+
+def turned(value, pieces):
+    shift = pieces * PIECE % value.shape[1]
+    return pltpu.roll(value, shift, 1) if shift else value
+
+
 def leaf_sample(index, offsets, near, panels, panel, nugget):
     parts, size, width = panels[0].shape
     split = size // 2
 
     def kernel(index_ref, offset_ref, near_ref, more_ref, *refs):
-        panel_refs, (panel_ref, nugget_ref, sample_ref, gram_ref, buffer, sems) = refs[:3], refs[3:]
+        panel_refs, (panel_ref, nugget_ref, sample_ref, gram_ref, packed_ref, buffer, sems) = refs[:3], refs[3:]
         for k in range(parts):
             offset = offset_ref[k]
             for part, ref in enumerate(panel_refs):
@@ -108,15 +116,25 @@
             pltpu.make_async_copy(panel_refs[0].at[0], buffer.at[k], sems.at[k]).wait()
             sample_ref[:split] += dot(near_ref[k, :split], buffer[k], ((1,), (0,)))
             sample_ref[split:] += dot(more_ref[k], buffer[k], ((1,), (0,)))
-        gram_ref[...] = dot(sample_ref[:, : width // 2], sample_ref[...], ((0,), (0,)))
+        half = width // 2
+        gram_ref[...] = dot(sample_ref[:, :half], sample_ref[...], ((0,), (0,)))
+        lane = iota((half, half), 1)
+        for q in range(half // PIECE):
+            gram = turned(gram_ref[:, :half], -q)
+            cross = turned(gram_ref[:, half:], 1 - q)
+            packed_ref[half * q : half * (q + 1)] = jnp.where(lane < PIECE, gram, cross)
 
     anywhere = pl.BlockSpec(memory_space=pl.ANY)
     smem = pl.BlockSpec(memory_space=pltpu.SMEM)
     return pl.pallas_call(
         kernel,
         in_specs=[smem, smem, vmem(), vmem()] + [anywhere] * 3 + [vmem()] * 2,
-        out_specs=[vmem()] * 2,
-        out_shape=[shape(size, width), shape(width // 2, width)],
+        out_specs=[vmem()] * 3,
+        out_shape=[
+            shape(size, width),
+            shape(width // 2, width),
+            shape(width // 2 * (width // 2 // PIECE), width // 2),
+        ],
         scratch_shapes=[pltpu.VMEM((parts, size, width), jnp.float32), pltpu.SemaphoreType.DMA((parts,))],
         name="leaf_sample",
     )(index, offsets, *near, *panels, panel, nugget)
@@ -132,91 +150,52 @@
     return nodes
 
 
-def local_sums(grams, row_count):
-    leaf_count, rows, width = grams.shape
-    half = width // 2
-    nodes = node_children(leaf_count)
-    nodes = nodes + [nodes[-1]] * (leaf_count - len(nodes))
-
-    def kernel(grams_ref, local_ref, sums_ref):
-        known = {(i,): grams_ref[i] for i in range(leaf_count)}
-        for n, children in enumerate(nodes):
-            a, b = tuple(children[0]), tuple(children[1])
-            local_ref[n, 0] = known[a][:, :half]
-            local_ref[n, 1] = known[b][:, :half]
-            known[a + b] = known[a] + known[b]
-        total = known[tuple(range(leaf_count))]
-        sums_ref[...] = jnp.zeros_like(sums_ref)
-        sums_ref[:rows] = total[:, :half]
-        sums_ref[rows : 2 * rows] = total[:, half:]
-
-    return pl.pallas_call(
-        kernel,
-        in_specs=[vmem()],
-        out_specs=[vmem()] * 2,
-        out_shape=[shape(leaf_count, 2, rows, half), shape(row_count, half)],
-        name="local_sums",
-    )(grams)
-
-
-def tree_sums(rows_of_all):
-    count, width = rows_of_all.shape
-
-    def kernel(rows_ref, out_ref):
+def tree_sums(pieces, leaf_count):
+    total_leaves, width = pieces.shape
+    count = total_leaves // leaf_count
+
+    def kernel(pieces_ref, out_ref):
+        rows = sum(pieces_ref[pl.ds(i, count, stride=leaf_count), :] for i in range(leaf_count))
         r = iota((count, count), 0)
         s = iota((count, count), 1)
         stride = r & -r
         root = r == 0
         left = root | ((s >= r - stride) & (s < r))
-        right = root | ((s >= r) & (s < r + stride))
-        rows = rows_ref[...]
-        out_ref[:, :width] = dot(jnp.where(left, 1.0, 0.0), rows, ((1,), (0,)))
-        out_ref[:, width:] = dot(jnp.where(right, 1.0, 0.0), rows, ((1,), (0,)))
+        right = (s >= r) & (s < r + stride)
+        a = dot(jnp.where(left, 1.0, 0.0), rows, ((1,), (0,)))
+        b = dot(jnp.where(right, 1.0, 0.0), rows, ((1,), (0,)))
+        lane = iota((count, width), 1)
+        root = iota((count, width), 0) == 0
+        total = turned(a + b, 1)
+        cross = turned(a, -1)
+        for c in range(leaf_count):
+            child = jnp.where(root, cross, a if c < leaf_count // 2 else b)
+            out_ref[pl.ds(c, count, stride=leaf_count), :] = jnp.where(lane < PIECE, child, total)
 
     return pl.pallas_call(
-        kernel, in_specs=[vmem()], out_specs=vmem(), out_shape=shape(count, 2 * width), name="tree_sums"
-    )(rows_of_all)
-
-
-def gram_message(local, sums, row_index):
-    leaf_count, _, rows, half = local.shape
-
-    def kernel(row_ref, local_ref, sums_ref, out_ref):
-        root = row_ref[0] == 0
-        a = sums_ref[:rows, :half]
-        b = sums_ref[:rows, half:]
-        cross = sums_ref[rows : 2 * rows, :half]
-        total = jnp.where(root, a, a + b)
-        for c in range(leaf_count):
-            out_ref[c, 0] = local_ref[c, 0]
-            out_ref[c, 1] = local_ref[c, 1]
-            out_ref[c, 2] = jnp.where(root, cross, a if c < leaf_count // 2 else b)
-            out_ref[c, 3] = total
-
-    return pl.pallas_call(
-        kernel,
-        in_specs=[pl.BlockSpec(memory_space=pltpu.SMEM), vmem(), vmem()],
-        out_specs=vmem(),
-        out_shape=shape(leaf_count, 4, rows, half),
-        name="gram_message",
-    )(row_index, local, sums)
-
-
-def node_bases(index, received, gram, sample, root_scale):
-    parts, _, rows, half = received.shape
+        kernel, in_specs=[vmem()], out_specs=vmem(), out_shape=shape(total_leaves, width), name="tree_sums"
+    )(pieces)
+
+
+def local_bases(index, grams, gram, sample):
+    parts = grams.shape[0]
     size, width = sample.shape
+    half = width // 2
     share = width // parts
-
-    def kernel(index_ref, received_ref, gram_ref, sample_ref, message_ref, upper_ref, m_ref, u_ref):
-        for c in range(parts):
-            piece = slice(rows * c, rows * (c + 1))
-            a, b = received_ref[c, 0], received_ref[c, 1]
-            m_ref[0, piece, :] = gram_ref[piece, :half]
-            m_ref[1, piece, :] = a
-            m_ref[2, piece, :] = b
-            m_ref[3, piece, :] = a + b
-            m_ref[4, piece, :] = received_ref[c, 2]
-            m_ref[5, piece, :] = received_ref[c, 3]
+    nodes = node_children(parts)
+    nodes = nodes + [nodes[-1]] * (parts - len(nodes))
+
+    def kernel(index_ref, grams_ref, gram_ref, sample_ref, message_ref, m_ref, u_ref):
+        column = index_ref[1]
+        m_ref[0] = gram_ref[:, :half]
+        for c, children in enumerate(nodes):
+
+            @pl.when(column == c)
+            def _():
+                for side in range(2):
+                    m_ref[1 + side] = sum(grams_ref[i, :, :half] for i in children[side])
+
+        m_ref[3] = m_ref[1] + m_ref[2]
         factorize(m_ref, u_ref, 32, 8)
         inverse = m_ref[0]
         basis = dot(sample_ref[:, :half], inverse, ((1,), (1,)))
@@ -230,35 +209,58 @@
             node = node_a if c < parts // 2 else node_b
             at = share * (c % (parts // 2))
             message_ref[c, 2] = node[at : at + share]
-        root = index_ref[0] == 0
-        column = index_ref[1]
-
-        @pl.when(root)
-        def _():
-            for c in range(parts):
-                piece = slice(rows * c, rows * (c + 1))
-                u_ref[4, piece, :] = received_ref[c, 2]
-
-        at = pl.multiple_of(share * lax.rem(column, parts // 2), share)
-
-        @pl.when(jnp.logical_not(root))
-        def _():
-            upper_ref[...] = dot(u_ref[4, pl.ds(at, share), :], m_ref[5], ((1,), (1,)))
-
-        @pl.when(root)
-        def _():
-            reduced_root = dot(m_ref[5], u_ref[4], ((1,), (0,)))
-            u_ref[0] = jnp.where(column < parts // 2, u_ref[5], reduced_root).T * root_scale
-            upper_ref[...] = u_ref[0, pl.ds(at, share), :]
 
     return pl.pallas_call(
         kernel,
         in_specs=[pl.BlockSpec(memory_space=pltpu.SMEM), vmem(), vmem(), vmem()],
-        out_specs=[vmem()] * 2,
-        out_shape=[shape(parts, 3, share, half), shape(share, half)],
-        scratch_shapes=[pltpu.VMEM((6, half, half), jnp.float32)] * 2,
-        name="node_bases",
-    )(index, received, gram, sample)
+        out_specs=vmem(),
+        out_shape=shape(parts, 3, share, half),
+        scratch_shapes=[pltpu.VMEM((4, half, half), jnp.float32)] * 2,
+        cost_estimate=pl.CostEstimate(flops=2 * 10**9, bytes_accessed=2 * 10**7, transcendentals=0),
+        name="local_bases",
+    )(index, grams, gram, sample)
+
+
+def upper_share(index, received, root_scale, parts):
+    half = received.shape[1]
+    share = 2 * half // parts
+
+    def kernel(index_ref, received_ref, upper_ref, m_ref, u_ref):
+        lane = iota((half, half), 1)
+
+        def assembled(t):
+            value = turned(received_ref[:half], -t)
+            for q in range(1, half // PIECE):
+                piece = turned(received_ref[half * q : half * (q + 1)], q - t)
+                value = jnp.where(lane < q * PIECE, value, piece)
+            return value
+
+        m_ref[0] = assembled(0)
+        m_ref[1] = assembled(1)
+        factorize(m_ref, u_ref, 32, 8)
+        root = index_ref[0] == 0
+        column = index_ref[1]
+        at = pl.multiple_of(share * lax.rem(column, parts // 2), share)
+
+        @pl.when(jnp.logical_not(root))
+        def _():
+            upper_ref[...] = dot(u_ref[0, pl.ds(at, share), :], m_ref[1], ((1,), (1,)))
+
+        @pl.when(root)
+        def _():
+            reduced_root = dot(m_ref[1], assembled(0), ((1,), (0,)))
+            u_ref[0] = jnp.where(column < parts // 2, u_ref[1], reduced_root).T * root_scale
+            upper_ref[...] = u_ref[0, pl.ds(at, share), :]
+
+    return pl.pallas_call(
+        kernel,
+        in_specs=[pl.BlockSpec(memory_space=pltpu.SMEM), vmem()],
+        out_specs=vmem(),
+        out_shape=shape(share, half),
+        scratch_shapes=[pltpu.VMEM((2, half, half), jnp.float32)] * 2,
+        cost_estimate=pl.CostEstimate(flops=10**9, bytes_accessed=10**7, transcendentals=0),
+        name="upper_share",
+    )(index, received)
 
 
 def neighbours(block):
@@ -290,15 +292,14 @@
     low, high = neighbours(own)
     more = exchange(rest, "col")
     offsets = near[:, split, 0].astype(jnp.int32) - (row_index - 1) * leaf_count
-    sample, gram = leaf_sample(index, offsets, (near, more), (low, own, high), test_panels, nugget)
-
-    grams = exchange(gram.reshape(col_count, half // col_count, 2 * half), "col")
-    local, sums = local_sums(grams, row_count)
-    sums = exchange(tree_sums(exchange(sums, "row")), "row")
-    received = exchange(gram_message(local, sums, index), "col")
+    sample, gram, packed = leaf_sample(index, offsets, (near, more), (low, own, high), test_panels, nugget)
+
+    pieces = exchange(packed, ("row", "col"))
+    grams = lax.all_gather(gram, "col", axis=0)
+    received = exchange(tree_sums(pieces, leaf_count), ("row", "col"))
+    outputs = exchange(local_bases(index, grams, gram, sample), "col")
     root_scale = 1.0 / math.sqrt(leaf_count * row_count * size)
-    message, upper = node_bases(index, received, gram, sample, root_scale)
-    outputs = exchange(message, "col")
+    upper = upper_share(index, received, root_scale, col_count)
     stored = (outputs[:, 0], outputs[:, 1], outputs[: col_count - 1, 2], upper[None])
     return tuple(jnp.swapaxes(output, 1, 2) for output in stored)
 

time: 229 us -> 207 us (0.904)
  blocking collectives: 80.4 us -> 30.7 us
  waiting for transfers between devices: 78.2 us -> 94.7 us
  starting transfers between devices: 22.5 us -> 34.3 us
    all_to_all x5 -> x1, blocking collectives: 80.4 us -> 30.7 us  [exchange(): return lax.all_to_all(block, axis, 0, 0, tiled=True)]
    all_to_all x2 -> x4, waiting for transfers between devices: 27.9 us -> 44.2 us  [exchange(): return lax.all_to_all(block, axis, 0, 0, tiled=True)]
    all_to_all x2 -> x4, starting transfers between devices: 15.3 us -> 27.1 us  [exchange(): return lax.all_to_all(block, axis, 0, 0, tiled=True)]
    pallas_call x3 -> x2, Pallas kernels: 14.9 us -> 15.7 us  [the longest x1 9.24 us: local_bases(): pl.pallas_call(kernel, in_specs=[pl.BlockSpec(memory_space=pltpu.SMEM), v...]
  transfers between devices with their start and end apart: 5 -> 8, of which waited for: 2 -> 4; matrix products, arithmetic and copies ran while one was open for 3% -> 3% of each run, Pallas kernels for 0% -> 9%
where the time goes in v4:
time: 207 us; the launch traced here: 206 us
  waiting for transfers between devices  94.7 us (46%)
  starting transfers between devices  34.3 us (17%)
  blocking collectives  30.7 us (15%)
  Pallas kernels  24 us (12%)
  between operations  14.1 us (7%)
  local copies, waits for them, and re-layouts  5.22 us (3%)
  other arithmetic  3.08 us (1%)
    all_gather x1, waiting for transfers between devices, on_device(): own = lax.all_gather(test_panels, 'col', axis=0, tiled=True)  49.7 us
    all_to_all x4, waiting for transfers between devices, exchange(): return lax.all_to_all(block, axis, 0, 0, tiled=True)  44.2 us
    all_to_all x1, blocking collectives, exchange(): return lax.all_to_all(block, axis, 0, 0, tiled=True)  30.7 us
    all_to_all x4, starting transfers between devices, exchange(): return lax.all_to_all(block, axis, 0, 0, tiled=True)  27.1 us
    pallas_call x1, Pallas kernels, local_bases(): pl.pallas_call(kernel, in_specs=[pl.BlockSpec(memory_space=pltpu.SMEM), v...  9.24 us
    pallas_call x1, Pallas kernels, upper_share(): pl.pallas_call(kernel, in_specs=[pl.BlockSpec(memory_space=pltpu.SMEM), v...  6.45 us
    pallas_call x1, Pallas kernels, leaf_sample(): pl.pallas_call(kernel, in_specs=[smem, smem, vmem(), vmem()] + [anywhere]...  6.31 us
  transfers between devices with their start and end apart: 8, of which 4 were waited for; matrix products, arithmetic and copies ran while one was open for 3% of the time, Pallas kernels for 9%

profile of v4, /device:TPU:1, one launch (start us, length us, event | category | flops | bytes accessed | tf_op | source)
XLA Modules:
  0.0 206.1 jit_solution(17959942134099904892)
XLA Ops:
  7.2 0.7 all-gather.4.cloned.1.call-update
  7.9 0.7 convert_bitcast_fusion
  8.6 2.7 %slice_bitcast_fusion = (f32[8,128,256]{2,1,0:T(8,128)}, f32[8,128,256]{2,1,0:T(8,128)S(1)}) fusion(f32[8,1,256,256]{3,2,0,1:T(8,128)} %bitcast.33), kind=kLoop, calls=%fused_computation.1 | loop fusion | bytes 4194304 | tf_op jit(solution)/shard_map/squeeze | solution.py:291
  11.4 1.1 pad_maximum_fusion
  12.4 10.9 %all-to-all-start = ((f32[8,136,256]{2,1,0:T(8,128)}), f32[8,136,256]{2,1,0:T(8,128)S(1)}, u32[]{:S(2)}, u32[]{:S(2)}) async-start(f32[8,136,256]{2,1,0:T(8,128)} %pad_maximum_fusion), calls=%async_computation | async-start | bytes 2228224 | tf_op jit(solution)/shard_map/all_to_all | solution.py:274
  23.3 49.7 %all-gather.4.cloned.1.call-done.refs_1_ = f32[8,256,256]{2,1,0:T(8,128)} async-done(((f32[1,256,256]{2,1,0:T(8,128)}), f32[8,256,256]{2,1,0:T(8,128)}) %all-gather.4.cloned.1.call-update) | async-done | bytes 2097168 | tf_op jit(solution)/shard_map/all_gather | solution.py:290
  73.0 4.1 %collective-permute-start.1 = (f32[8,256,256]{2,1,0:T(8,128)}, f32[8,256,256]{2,1,0:T(8,128)}, u32[]{:S(2)}, u32[]{:S(2)}) collective-permute-start(f32[8,256,256]{2,1,0:T(8,128)} %all-gather.4.cloned.1.call-done.refs_1_), channel_id=1, source_target_pairs={{8,0},{16,8},{24,16},{32,24},{40,32},{48,40},{56,48},{64,56},{72,6... | collective-permute-start | bytes 6291464 | tf_op jit(solution)/shard_map/ppermute | solution.py:270
  77.1 3.0 %collective-permute-start = (f32[8,256,256]{2,1,0:T(8,128)}, f32[8,256,256]{2,1,0:T(8,128)}, u32[]{:S(2)}, u32[]{:S(2)}) collective-permute-start(f32[8,256,256]{2,1,0:T(8,128)} %all-gather.4.cloned.1.call-done.refs_1_), channel_id=1, source_target_pairs={{0,8},{8,16},{16,24},{24,32},{32,40},{40,48},{48,56},{56,64},{64,7... | collective-permute-start | bytes 6291464 | tf_op jit(solution)/shard_map/ppermute | solution.py:270
  80.2 4.4 %all-to-all-start.1 = ((f32[8,128,256]{2,1,0:T(8,128)}), f32[8,128,256]{2,1,0:T(8,128)S(1)}, u32[]{:S(2)}, u32[]{:S(2)}) async-start(f32[8,128,256]{2,1,0:T(8,128)} %get-tuple-element.9), calls=%async_computation.1 | async-start | bytes 2097152 | tf_op jit(solution)/shard_map/all_to_all | solution.py:274
  84.7 0.6 pad_add_fusion.index_ref
  85.2 0.8 fusion.1.offset_ref
  86.0 27.8 %all-to-all-done.1.more_ref = f32[8,128,256]{2,1,0:T(8,128)S(1)} async-done(((f32[8,128,256]{2,1,0:T(8,128)}), f32[8,128,256]{2,1,0:T(8,128)S(1)}, u32[]{:S(2)}, u32[]{:S(2)}) %all-to-all-start.1) | async-done | bytes 1048608 | tf_op jit(solution)/shard_map/all_to_all | solution.py:274
  113.8 1.0 copy-done.1
  114.9 6.3 %leaf_sample.1 = (f32[256,256]{1,0:T(8,128)}, f32[128,256]{1,0:T(8,128)}, f32[512,128]{1,0:T(8,128)}) custom-call(s32[2]{0:T(128)} %pad_add_fusion.index_ref, s32[8]{0:T(128)} %fusion.1.offset_ref, f32[8,136,256]{2,1,0:T(8,128)} %copy-done, f32[8,128,256]{2,1,0:T(8,128)} %copy-done.1, f32[8,256,256]{2,1,0:T(8,128)} %collective-permute-done.refs_0_, ...), custom_call_target="tpu_custom_call" | custom-call | tf_op jit(solution)/shard_map/leaf_sample/pallas_call | solution.py:129
  121.2 30.7 %all_to_all.37 = f32[512,1,128]{2,1,0:T(1,128)} all-to-all(f32[512,1,128]{2,1,0:T(1,128)} %bitcast.37), channel_id=1, replica_groups=mesh['row'=64,'col'=8] {'row','col'}, dimensions={0} | all-to-all | bytes 524288 | tf_op jit(solution)/shard_map/all_to_all | solution.py:274
  151.9 2.0 tree_sums.1
  153.9 8.3 %all-to-all-start.4 = ((f32[512,1,128]{2,1,0:T(1,128)}), f32[512,1,128]{2,1,0:T(1,128)S(1)}, u32[]{:S(2)}, u32[]{:S(2)}) async-start(f32[512,1,128]{2,1,0:T(1,128)} %bitcast.34), calls=%async_computation.4 | async-start | bytes 524288 | tf_op jit(solution)/shard_map/all_to_all | solution.py:274
  162.3 9.2 %local_bases.1 = f32[8,3,32,128]{3,2,1,0:T(8,128)} custom-call(s32[2]{0:T(128)} %pad_add_fusion.index_ref, f32[8,128,256]{2,1,0:T(8,128)} %bitcast.38, f32[128,256]{1,0:T(8,128)} %get-tuple-element.11.gram_ref, f32[256,256]{1,0:T(8,128)} %get-tuple-element.12.sample_ref), custom_call_target="tpu_custom_call" | custom-call | flops 2000000000 | bytes 20000000 | tf_op jit(solution)/shard_map/local_bases/pallas_call | solution.py:213
  171.5 7.8 %all-to-all-done.4 = f32[512,1,128]{2,1,0:T(1,128)S(1)} async-done(((f32[512,1,128]{2,1,0:T(1,128)}), f32[512,1,128]{2,1,0:T(1,128)S(1)}, u32[]{:S(2)}, u32[]{:S(2)}) %all-to-all-start.4) | async-done | bytes 262176 | tf_op jit(solution)/shard_map/all_to_all | solution.py:274
  179.3 3.5 %all-to-all-start.2 = ((f32[8,3,32,128]{3,2,1,0:T(8,128)}), f32[8,3,32,128]{3,2,1,0:T(8,128)S(1)}, u32[]{:S(2)}, u32[]{:S(2)}) async-start(f32[8,3,32,128]{3,2,1,0:T(8,128)} %local_bases.1), calls=%async_computation.2 | async-start | bytes 786432 | tf_op jit(solution)/shard_map/all_to_all | solution.py:274
  182.8 6.5 %upper_share.1 = f32[32,128]{1,0:T(8,128)} custom-call(s32[2]{0:T(128)} %pad_add_fusion.index_ref, f32[512,128]{1,0:T(8,128)} %bitcast.36), custom_call_target="tpu_custom_call" | custom-call | flops 1000000000 | bytes 10000000 | tf_op jit(solution)/shard_map/upper_share/pallas_call | solution.py:255
  189.3 8.6 %all-to-all-done.2 = f32[8,3,32,128]{3,2,1,0:T(8,128)S(1)} async-done(((f32[8,3,32,128]{3,2,1,0:T(8,128)}), f32[8,3,32,128]{3,2,1,0:T(8,128)S(1)}, u32[]{:S(2)}, u32[]{:S(2)}) %all-to-all-start.2) | async-done | bytes 393248 | tf_op jit(solution)/shard_map/all_to_all | solution.py:274
  197.9 0.7 slice_bitcast_fusion.4
  198.5 0.7 slice_bitcast_fusion.2
  (13 shorter events, 0.2 us)
Async XLA Ops:
  7.2 65.9 %all-gather.4.cloned.1.call-start = ((), (), s32[]{:S(2)}) async-start(), calls=%async_computation.5 | async-start | bytes 2359296 | tf_op jit(solution)/shard_map/all_gather | solution.py:290
  12.4 67.7 %all-to-all-start = ((f32[8,136,256]{2,1,0:T(8,128)}), f32[8,136,256]{2,1,0:T(8,128)S(1)}, u32[]{:S(2)}, u32[]{:S(2)}) async-start(f32[8,136,256]{2,1,0:T(8,128)} %pad_maximum_fusion), calls=%async_computation | async-start | bytes 2228224 | tf_op jit(solution)/shard_map/all_to_all | solution.py:274
  73.0 40.8 %collective-permute-start.1 = (f32[8,256,256]{2,1,0:T(8,128)}, f32[8,256,256]{2,1,0:T(8,128)}, u32[]{:S(2)}, u32[]{:S(2)}) collective-permute-start(f32[8,256,256]{2,1,0:T(8,128)} %all-gather.4.cloned.1.call-done.refs_1_), channel_id=1, source_target_pairs={{8,0},{16,8},{24,16},{32,24},{40,32},{48,40},{56,48},{64,56},{72,6... | collective-permute-start | bytes 6291464 | tf_op jit(solution)/shard_map/ppermute | solution.py:270
  77.1 36.7 %collective-permute-start = (f32[8,256,256]{2,1,0:T(8,128)}, f32[8,256,256]{2,1,0:T(8,128)}, u32[]{:S(2)}, u32[]{:S(2)}) collective-permute-start(f32[8,256,256]{2,1,0:T(8,128)} %all-gather.4.cloned.1.call-done.refs_1_), channel_id=1, source_target_pairs={{0,8},{8,16},{16,24},{24,32},{32,40},{40,48},{48,56},{56,64},{64,7... | collective-permute-start | bytes 6291464 | tf_op jit(solution)/shard_map/ppermute | solution.py:270
  80.2 33.7 %copy-start = (f32[8,136,256]{2,1,0:T(8,128)}, f32[8,136,256]{2,1,0:T(8,128)S(1)}, u32[]{:S(2)}) copy-start(f32[8,136,256]{2,1,0:T(8,128)S(1)} %all-to-all-done.near_ref) | copy-start | bytes 3342340
  80.2 33.6 %all-to-all-start.1 = ((f32[8,128,256]{2,1,0:T(8,128)}), f32[8,128,256]{2,1,0:T(8,128)S(1)}, u32[]{:S(2)}, u32[]{:S(2)}) async-start(f32[8,128,256]{2,1,0:T(8,128)} %get-tuple-element.9), calls=%async_computation.1 | async-start | bytes 2097152 | tf_op jit(solution)/shard_map/all_to_all | solution.py:274
  84.6 77.6 %all-gather.6.cloned.1.call-start = ((), (), s32[]{:S(2)}) async-start(), calls=%async_computation.6 | async-start | bytes 1179648 | tf_op jit(solution)/shard_map/all_gather | solution.py:298
  113.8 1.1 copy-start.1
  153.9 25.5 %all-to-all-start.4 = ((f32[512,1,128]{2,1,0:T(1,128)}), f32[512,1,128]{2,1,0:T(1,128)S(1)}, u32[]{:S(2)}, u32[]{:S(2)}) async-start(f32[512,1,128]{2,1,0:T(1,128)} %bitcast.34), calls=%async_computation.4 | async-start | bytes 524288 | tf_op jit(solution)/shard_map/all_to_all | solution.py:274
  179.3 3.5 %copy-start.2 = (f32[512,1,128]{2,1,0:T(1,128)}, f32[512,1,128]{2,1,0:T(1,128)S(1)}, u32[]{:S(2)}) copy-start(f32[512,1,128]{2,1,0:T(1,128)S(1)} %all-to-all-done.4) | copy-start | bytes 786436
  179.3 18.5 %all-to-all-start.2 = ((f32[8,3,32,128]{3,2,1,0:T(8,128)}), f32[8,3,32,128]{3,2,1,0:T(8,128)S(1)}, u32[]{:S(2)}, u32[]{:S(2)}) async-start(f32[8,3,32,128]{3,2,1,0:T(8,128)} %local_bases.1), calls=%async_computation.2 | async-start | bytes 786432 | tf_op jit(solution)/shard_map/all_to_all | solution.py:274
Sparse Core Ops, SparseCore 0:
  10.1 62.9 all-gather.3
  121.3 35.6 all-gather.5

commit v5 on v4

--- a/solution.py
+++ b/solution.py
@@ -96,10 +96,10 @@
 
 
 def leaf_sample(index, offsets, near, panels, panel, nugget):
-    parts, size, width = panels[0].shape
-    split = size // 2
-
-    def kernel(index_ref, offset_ref, near_ref, more_ref, *refs):
+    parts, size, _ = near.shape
+    width = panel.shape[2]
+
+    def kernel(index_ref, offset_ref, near_ref, *refs):
         panel_refs, (panel_ref, nugget_ref, sample_ref, gram_ref, packed_ref, buffer, sems) = refs[:3], refs[3:]
         for k in range(parts):
             offset = offset_ref[k]
@@ -107,15 +107,16 @@
 
                 @pl.when(offset // parts == part)
                 def _():
-                    pltpu.make_async_copy(ref.at[lax.rem(offset, parts)], buffer.at[k], sems.at[k]).start()
+                    pltpu.make_async_copy(
+                        ref.at[lax.rem(offset, parts), pl.ds(0, size)], buffer.at[k], sems.at[k]
+                    ).start()
 
         row = nugget_ref[pl.ds(index_ref[1], 1), :]
         column = jnp.broadcast_to(row, (8, size)).T[:, :1]
         sample_ref[...] = column * panel_ref[0]
         for k in range(parts):
-            pltpu.make_async_copy(panel_refs[0].at[0], buffer.at[k], sems.at[k]).wait()
-            sample_ref[:split] += dot(near_ref[k, :split], buffer[k], ((1,), (0,)))
-            sample_ref[split:] += dot(more_ref[k], buffer[k], ((1,), (0,)))
+            pltpu.make_async_copy(panel_refs[0].at[0, pl.ds(0, size)], buffer.at[k], sems.at[k]).wait()
+            sample_ref[...] += dot(near_ref[k], buffer[k], ((1,), (0,)))
         half = width // 2
         gram_ref[...] = dot(sample_ref[:, :half], sample_ref[...], ((0,), (0,)))
         lane = iota((half, half), 1)
@@ -128,7 +129,7 @@
     smem = pl.BlockSpec(memory_space=pltpu.SMEM)
     return pl.pallas_call(
         kernel,
-        in_specs=[smem, smem, vmem(), vmem()] + [anywhere] * 3 + [vmem()] * 2,
+        in_specs=[smem, smem, vmem()] + [anywhere] * 3 + [vmem()] * 2,
         out_specs=[vmem()] * 3,
         out_shape=[
             shape(size, width),
@@ -137,7 +138,7 @@
         ],
         scratch_shapes=[pltpu.VMEM((parts, size, width), jnp.float32), pltpu.SemaphoreType.DMA((parts,))],
         name="leaf_sample",
-    )(index, offsets, *near, *panels, panel, nugget)
+    )(index, offsets, near, *panels, panel, nugget)
 
 
 def node_children(leaf_count):
@@ -284,15 +285,14 @@
     col_index = lax.axis_index("col")
     index = jnp.stack([row_index, col_index]).astype(jnp.int32)
 
-    split = size // 2
-    number = jnp.broadcast_to(column_block[:, :, None].astype(jnp.float32), (leaf_count, 8, size))
-    near = exchange(jnp.concatenate([near_blocks[:, 0, :split], number], axis=1), "col")
-    own = lax.all_gather(test_panels, "col", axis=0, tiled=True)
-    rest, own = lax.optimization_barrier((near_blocks[:, 0, split:], own))
+    numbers = column_block.reshape(1, 1, leaf_count).astype(jnp.float32)
+    numbers = jnp.pad(numbers, ((0, 0), (0, 7), (0, 2 * half - leaf_count)))
+    own = lax.all_gather(jnp.concatenate([test_panels, numbers], axis=1), "col", axis=0, tiled=True)
+    near = exchange(near_blocks[:, 0], "col")
     low, high = neighbours(own)
-    more = exchange(rest, "col")
-    offsets = near[:, split, 0].astype(jnp.int32) - (row_index - 1) * leaf_count
-    sample, gram, packed = leaf_sample(index, offsets, (near, more), (low, own, high), test_panels, nugget)
+    columns = lax.dynamic_slice(own, (0, size, col_index), (col_count, 1, 1)).reshape(-1)
+    offsets = columns.astype(jnp.int32) - (row_index - 1) * leaf_count
+    sample, gram, packed = leaf_sample(index, offsets, near, (low, own, high), test_panels, nugget)
 
     pieces = exchange(packed, ("row", "col"))
     grams = lax.all_gather(gram, "col", axis=0)

time: 207 us -> 220 us (1.063)
  waiting for transfers between devices: 94.7 us -> 108 us
  blocking collectives: 30.7 us -> 37.7 us
  starting transfers between devices: 34.3 us -> 28.4 us
  local copies, waits for them, and re-layouts: 5.22 us -> 1.38 us
    all_to_all x4 -> x3, waiting for transfers between devices: 44.2 us -> 16.6 us  [exchange(): return lax.all_to_all(block, axis, 0, 0, tiled=True)]
    ppermute x1, waiting for transfers between devices: 0.01 us -> 20.6 us  [neighbours(): lax.ppermute(block, 'row', backward)]
    all_gather x1, waiting for transfers between devices: 49.7 us -> 69.5 us  [on_device(): lax.all_gather(jnp.concatenate([test_panels, numbers], axis=1), 'col', ax...]
    all_to_all x1, blocking collectives: 30.7 us -> 37.7 us  [exchange(): return lax.all_to_all(block, axis, 0, 0, tiled=True)]
    all_to_all x4 -> x3, starting transfers between devices: 27.1 us -> 22.7 us  [exchange(): return lax.all_to_all(block, axis, 0, 0, tiled=True)]
    squeeze x1 -> x0, local copies, waits for them, and re-layouts: 2.74 us -> none  [on_device(): rest, own = lax.optimization_barrier((near_blocks[:, 0, split:], own))]
  transfers between devices with their start and end apart: 8 -> 7, of which waited for: 4 -> 5; matrix products, arithmetic and copies ran while one was open for 3% -> 1% of each run, Pallas kernels for 9% -> 8%
where the time goes in v5:
time: 220 us; the launch traced here: 219 us
  waiting for transfers between devices  108 us (49%)
  blocking collectives  37.7 us (17%)
  starting transfers between devices  28.4 us (13%)
  Pallas kernels  25.3 us (12%)
  between operations  14.1 us (6%)
  other arithmetic  4.49 us (2%)
    all_gather x1, waiting for transfers between devices, on_device(): lax.all_gather(jnp.concatenate([test_panels, numbers], axis=1), 'col', ax...  69.5 us
    all_to_all x1, blocking collectives, exchange(): return lax.all_to_all(block, axis, 0, 0, tiled=True)  37.7 us
    all_to_all x3, starting transfers between devices, exchange(): return lax.all_to_all(block, axis, 0, 0, tiled=True)  22.7 us
    ppermute x1, waiting for transfers between devices, neighbours(): lax.ppermute(block, 'row', backward)  20.6 us
    all_to_all x3, waiting for transfers between devices, exchange(): return lax.all_to_all(block, axis, 0, 0, tiled=True)  16.6 us
    pallas_call x1, Pallas kernels, local_bases(): pl.pallas_call(kernel, in_specs=[pl.BlockSpec(memory_space=pltpu.SMEM), v...  9.22 us
    pallas_call x1, Pallas kernels, leaf_sample(): pl.pallas_call(kernel, in_specs=[smem, smem, vmem()] + [anywhere] * 3 + [...  7.62 us
    pallas_call x1, Pallas kernels, upper_share(): pl.pallas_call(kernel, in_specs=[pl.BlockSpec(memory_space=pltpu.SMEM), v...  6.45 us
  transfers between devices with their start and end apart: 7, of which 5 were waited for; matrix products, arithmetic and copies ran while one was open for 1% of the time, Pallas kernels for 8%

profile of v5, /device:TPU:1, one launch (start us, length us, event | category | flops | bytes accessed | tf_op | source)
XLA Modules:
  0.0 219.4 jit_solution(11204281030964817703)
XLA Ops:
  7.2 0.0 all-gather.4.cloned.1.call-start
  7.2 0.7 convert_bitcast_fusion
  7.9 1.7 select_maximum_fusion
  9.6 10.9 %all-to-all-start = ((f32[8,256,256]{2,1,0:T(8,128)}), f32[8,256,256]{2,1,0:T(8,128)S(1)}, u32[]{:S(2)}, u32[]{:S(2)}) async-start(f32[8,256,256]{2,1,0:T(8,128)} %bitcast.29), calls=%async_computation | async-start | bytes 4194304 | tf_op jit(solution)/shard_map/all_to_all | solution.py:275
  20.4 0.0 all-gather.6.cloned.1.call-start
  20.5 69.5 %all-gather.4.cloned.1.call-done.refs_1_ = f32[8,264,256]{2,1,0:T(8,128)} async-done(((f32[1,264,256]{2,1,0:T(8,128)}), f32[8,264,256]{2,1,0:T(8,128)}) %all-gather.4.cloned.1.call-update) | async-done | bytes 2162704 | tf_op jit(solution)/shard_map/all_gather | solution.py:290
  90.0 2.7 %collective-permute-start.1 = (f32[8,264,256]{2,1,0:T(8,128)}, f32[8,264,256]{2,1,0:T(8,128)}, u32[]{:S(2)}, u32[]{:S(2)}) collective-permute-start(f32[8,264,256]{2,1,0:T(8,128)} %all-gather.4.cloned.1.call-done.refs_1_), channel_id=1, source_target_pairs={{8,0},{16,8},{24,16},{32,24},{40,32},{48,40},{56,48},{64,56},{72,6... | collective-permute-start | bytes 6488072 | tf_op jit(solution)/shard_map/ppermute | solution.py:271
  92.7 3.0 %collective-permute-start = (f32[8,264,256]{2,1,0:T(8,128)}, f32[8,264,256]{2,1,0:T(8,128)}, u32[]{:S(2)}, u32[]{:S(2)}) collective-permute-start(f32[8,264,256]{2,1,0:T(8,128)} %all-gather.4.cloned.1.call-done.refs_1_), channel_id=1, source_target_pairs={{0,8},{8,16},{16,24},{24,32},{32,40},{40,48},{48,56},{56,64},{64,7... | collective-permute-start | bytes 6488072 | tf_op jit(solution)/shard_map/ppermute | solution.py:271
  95.7 0.6 pad_add_fusion.index_ref
  96.3 1.6 subtract_reduce_fusion.offset_ref
  97.9 20.6 %collective-permute-done.1.refs_2_ = f32[8,264,256]{2,1,0:T(8,128)} collective-permute-done((f32[8,264,256]{2,1,0:T(8,128)}, f32[8,264,256]{2,1,0:T(8,128)}, u32[]{:S(2)}, u32[]{:S(2)}) %collective-permute-start.1) | collective-permute-done | bytes 2162720 | tf_op jit(solution)/shard_map/ppermute | solution.py:271
  118.5 1.2 collective-permute-done.refs_0_
  119.7 7.6 %leaf_sample.1 = (f32[256,256]{1,0:T(8,128)}, f32[128,256]{1,0:T(8,128)}, f32[512,128]{1,0:T(8,128)}) custom-call(s32[2]{0:T(128)} %pad_add_fusion.index_ref, s32[8]{0:T(128)} %subtract_reduce_fusion.offset_ref, f32[8,256,256]{2,1,0:T(8,128)} %copy-done, f32[8,264,256]{2,1,0:T(8,128)} %collective-permute-done.refs_0_, ...), custom_call_target="tpu_custom_call" | custom-call | tf_op jit(solution)/shard_map/leaf_sample/pallas_call | solution.py:130
  127.3 37.7 %all_to_all.32 = f32[512,1,128]{2,1,0:T(1,128)} all-to-all(f32[512,1,128]{2,1,0:T(1,128)} %bitcast.33), channel_id=1, replica_groups=mesh['row'=64,'col'=8] {'row','col'}, dimensions={0} | all-to-all | bytes 524288 | tf_op jit(solution)/shard_map/all_to_all | solution.py:275
  165.1 2.0 tree_sums.1
  167.0 8.3 %all-to-all-start.3 = ((f32[512,1,128]{2,1,0:T(1,128)}), f32[512,1,128]{2,1,0:T(1,128)S(1)}, u32[]{:S(2)}, u32[]{:S(2)}) async-start(f32[512,1,128]{2,1,0:T(1,128)} %bitcast.30), calls=%async_computation.3 | async-start | bytes 524288 | tf_op jit(solution)/shard_map/all_to_all | solution.py:275
  175.4 0.0 all-gather.6.cloned.1.call-done
  175.4 9.2 %local_bases.1 = f32[8,3,32,128]{3,2,1,0:T(8,128)} custom-call(s32[2]{0:T(128)} %pad_add_fusion.index_ref, f32[8,128,256]{2,1,0:T(8,128)} %bitcast.34, f32[128,256]{1,0:T(8,128)} %get-tuple-element.7.gram_ref, f32[256,256]{1,0:T(8,128)} %get-tuple-element.8.sample_ref), custom_call_target="tpu_custom_call" | custom-call | flops 2000000000 | bytes 20000000 | tf_op jit(solution)/shard_map/local_bases/pallas_call | solution.py:214
  184.6 8.0 %all-to-all-done.3 = f32[512,1,128]{2,1,0:T(1,128)S(1)} async-done(((f32[512,1,128]{2,1,0:T(1,128)}), f32[512,1,128]{2,1,0:T(1,128)S(1)}, u32[]{:S(2)}, u32[]{:S(2)}) %all-to-all-start.3) | async-done | bytes 262176 | tf_op jit(solution)/shard_map/all_to_all | solution.py:275
  192.6 3.5 %all-to-all-start.1 = ((f32[8,3,32,128]{3,2,1,0:T(8,128)}), f32[8,3,32,128]{3,2,1,0:T(8,128)S(1)}, u32[]{:S(2)}, u32[]{:S(2)}) async-start(f32[8,3,32,128]{3,2,1,0:T(8,128)} %local_bases.1), calls=%async_computation.1 | async-start | bytes 786432 | tf_op jit(solution)/shard_map/all_to_all | solution.py:275
  196.1 6.5 %upper_share.1 = f32[32,128]{1,0:T(8,128)} custom-call(s32[2]{0:T(128)} %pad_add_fusion.index_ref, f32[512,128]{1,0:T(8,128)} %bitcast.32), custom_call_target="tpu_custom_call" | custom-call | flops 1000000000 | bytes 10000000 | tf_op jit(solution)/shard_map/upper_share/pallas_call | solution.py:256
  202.6 8.6 %all-to-all-done.1 = f32[8,3,32,128]{3,2,1,0:T(8,128)S(1)} async-done(((f32[8,3,32,128]{3,2,1,0:T(8,128)}), f32[8,3,32,128]{3,2,1,0:T(8,128)S(1)}, u32[]{:S(2)}, u32[]{:S(2)}) %all-to-all-start.1) | async-done | bytes 393248 | tf_op jit(solution)/shard_map/all_to_all | solution.py:275
  211.1 0.7 slice_bitcast_fusion.2
  211.8 0.7 slice_bitcast_fusion
  (7 shorter events, 0.0 us)
Async XLA Ops:
  7.2 82.8 %all-gather.4.cloned.1.call-start = ((), (), s32[]{:S(2)}) async-start(), calls=%async_computation.4 | async-start | bytes 2433024 | tf_op jit(solution)/shard_map/all_gather | solution.py:290
  9.6 88.3 %all-to-all-start = ((f32[8,256,256]{2,1,0:T(8,128)}), f32[8,256,256]{2,1,0:T(8,128)S(1)}, u32[]{:S(2)}, u32[]{:S(2)}) async-start(f32[8,256,256]{2,1,0:T(8,128)} %bitcast.29), calls=%async_computation | async-start | bytes 4194304 | tf_op jit(solution)/shard_map/all_to_all | solution.py:275
  20.4 155.0 %all-gather.6.cloned.1.call-start = ((), (), s32[]{:S(2)}) async-start(), calls=%async_computation.5 | async-start | bytes 1179648 | tf_op jit(solution)/shard_map/all_gather | solution.py:298
  90.0 28.5 %collective-permute-start.1 = (f32[8,264,256]{2,1,0:T(8,128)}, f32[8,264,256]{2,1,0:T(8,128)}, u32[]{:S(2)}, u32[]{:S(2)}) collective-permute-start(f32[8,264,256]{2,1,0:T(8,128)} %all-gather.4.cloned.1.call-done.refs_1_), channel_id=1, source_target_pairs={{8,0},{16,8},{24,16},{32,24},{40,32},{48,40},{56,48},{64,56},{72,6... | collective-permute-start | bytes 6488072 | tf_op jit(solution)/shard_map/ppermute | solution.py:271
  92.7 27.0 %collective-permute-start = (f32[8,264,256]{2,1,0:T(8,128)}, f32[8,264,256]{2,1,0:T(8,128)}, u32[]{:S(2)}, u32[]{:S(2)}) collective-permute-start(f32[8,264,256]{2,1,0:T(8,128)} %all-gather.4.cloned.1.call-done.refs_1_), channel_id=1, source_target_pairs={{0,8},{8,16},{16,24},{24,32},{32,40},{40,48},{48,56},{56,64},{64,7... | collective-permute-start | bytes 6488072 | tf_op jit(solution)/shard_map/ppermute | solution.py:271
  97.9 21.8 %copy-start = (f32[8,256,256]{2,1,0:T(8,128)}, f32[8,256,256]{2,1,0:T(8,128)S(1)}, u32[]{:S(2)}) copy-start(f32[8,256,256]{2,1,0:T(8,128)S(1)} %all-to-all-done.near_ref) | copy-start | bytes 6291460
  167.0 25.6 %all-to-all-start.3 = ((f32[512,1,128]{2,1,0:T(1,128)}), f32[512,1,128]{2,1,0:T(1,128)S(1)}, u32[]{:S(2)}, u32[]{:S(2)}) async-start(f32[512,1,128]{2,1,0:T(1,128)} %bitcast.30), calls=%async_computation.3 | async-start | bytes 524288 | tf_op jit(solution)/shard_map/all_to_all | solution.py:275
  192.6 3.5 %copy-start.1 = (f32[512,1,128]{2,1,0:T(1,128)}, f32[512,1,128]{2,1,0:T(1,128)S(1)}, u32[]{:S(2)}) copy-start(f32[512,1,128]{2,1,0:T(1,128)S(1)} %all-to-all-done.3) | copy-start | bytes 786436
  192.6 18.5 %all-to-all-start.1 = ((f32[8,3,32,128]{3,2,1,0:T(8,128)}), f32[8,3,32,128]{3,2,1,0:T(8,128)S(1)}, u32[]{:S(2)}, u32[]{:S(2)}) async-start(f32[8,3,32,128]{3,2,1,0:T(8,128)} %local_bases.1), calls=%async_computation.1 | async-start | bytes 786432 | tf_op jit(solution)/shard_map/all_to_all | solution.py:275
Sparse Core Ops, SparseCore 0:
  10.1 79.8 all-gather.3
  127.4 43.2 all-gather.5

commit v6 on v4

--- a/solution.py
+++ b/solution.py
@@ -6,6 +6,7 @@
 from jax.experimental import pallas as pl
 from jax.experimental.pallas import tpu as pltpu
 from jax.sharding import PartitionSpec as P
+
 
 HIGHEST = lax.Precision.HIGHEST
 
@@ -88,6 +89,7 @@
 
 
 PIECE = 32
+FIRST_ROWS = 104
 
 
 def turned(value, pieces):
@@ -97,7 +99,7 @@
 
 def leaf_sample(index, offsets, near, panels, panel, nugget):
     parts, size, width = panels[0].shape
-    split = size // 2
+    split = FIRST_ROWS
 
     def kernel(index_ref, offset_ref, near_ref, more_ref, *refs):
         panel_refs, (panel_ref, nugget_ref, sample_ref, gram_ref, packed_ref, buffer, sems) = refs[:3], refs[3:]
@@ -179,7 +181,7 @@
 
 def local_bases(index, grams, gram, sample):
     parts = grams.shape[0]
-    size, width = sample.shape
+    _, width = sample.shape
     half = width // 2
     share = width // parts
     nodes = node_children(parts)
@@ -277,20 +279,20 @@
 def on_device(near_blocks, column_block, test_panels, nugget):
     leaf_count = near_blocks.shape[0]
     size = near_blocks.shape[2]
-    half = test_panels.shape[2] // 2
     row_count = lax.axis_size("row")
     col_count = lax.axis_size("col")
     row_index = lax.axis_index("row")
     col_index = lax.axis_index("col")
     index = jnp.stack([row_index, col_index]).astype(jnp.int32)
 
-    split = size // 2
+    split = FIRST_ROWS
     number = jnp.broadcast_to(column_block[:, :, None].astype(jnp.float32), (leaf_count, 8, size))
     near = exchange(jnp.concatenate([near_blocks[:, 0, :split], number], axis=1), "col")
     own = lax.all_gather(test_panels, "col", axis=0, tiled=True)
-    rest, own = lax.optimization_barrier((near_blocks[:, 0, split:], own))
+    rest = near_blocks[:, 0, split:]
+    rest, own = lax.optimization_barrier((rest, own))
+    more = exchange(rest, "col")
     low, high = neighbours(own)
-    more = exchange(rest, "col")
     offsets = near[:, split, 0].astype(jnp.int32) - (row_index - 1) * leaf_count
     sample, gram, packed = leaf_sample(index, offsets, (near, more), (low, own, high), test_panels, nugget)
 

time: 207 us -> 203 us (0.981)
  waiting for transfers between devices: 94.7 us -> 85.6 us
  blocking collectives: 30.7 us -> 35.8 us
    all_to_all x4, waiting for transfers between devices: 44.2 us -> 18.7 us  [exchange(): return lax.all_to_all(block, axis, 0, 0, tiled=True)]
    ppermute x1, waiting for transfers between devices: 0.01 us -> 20.9 us  [neighbours(): lax.ppermute(block, 'row', backward)]
    all_gather x1, waiting for transfers between devices: 49.7 us -> 44.2 us  [on_device(): own = lax.all_gather(test_panels, 'col', axis=0, tiled=True)]
    all_to_all x1, blocking collectives: 30.7 us -> 35.8 us  [exchange(): return lax.all_to_all(block, axis, 0, 0, tiled=True)]
  transfers between devices with their start and end apart: 8 -> 8, of which waited for: 4 -> 6; matrix products, arithmetic and copies ran while one was open for 3% -> 3% of each run, Pallas kernels for 9% -> 9%
where the time goes in v6:
time: 203 us; the launch traced here: 202 us
  waiting for transfers between devices  85.6 us (42%)
  blocking collectives  35.8 us (18%)
  starting transfers between devices  34.9 us (17%)
  Pallas kernels  24.2 us (12%)
  between operations  14.1 us (7%)
  local copies, waits for them, and re-layouts  4.85 us (2%)
  other arithmetic  3.02 us (1%)
    all_gather x1, waiting for transfers between devices, on_device(): own = lax.all_gather(test_panels, 'col', axis=0, tiled=True)  44.2 us
    all_to_all x1, blocking collectives, exchange(): return lax.all_to_all(block, axis, 0, 0, tiled=True)  35.8 us
    all_to_all x4, starting transfers between devices, exchange(): return lax.all_to_all(block, axis, 0, 0, tiled=True)  27.1 us
    ppermute x1, waiting for transfers between devices, neighbours(): lax.ppermute(block, 'row', backward)  20.9 us
    all_to_all x4, waiting for transfers between devices, exchange(): return lax.all_to_all(block, axis, 0, 0, tiled=True)  18.7 us
    pallas_call x1, Pallas kernels, local_bases(): pl.pallas_call(kernel, in_specs=[pl.BlockSpec(memory_space=pltpu.SMEM), v...  9.23 us
    pallas_call x1, Pallas kernels, leaf_sample(): pl.pallas_call(kernel, in_specs=[smem, smem, vmem(), vmem()] + [anywhere]...  6.59 us
    pallas_call x1, Pallas kernels, upper_share(): pl.pallas_call(kernel, in_specs=[pl.BlockSpec(memory_space=pltpu.SMEM), v...  6.45 us
  transfers between devices with their start and end apart: 8, of which 6 were waited for; matrix products, arithmetic and copies ran while one was open for 3% of the time, Pallas kernels for 9%

profile of v6, /device:TPU:1, one launch (start us, length us, event | category | flops | bytes accessed | tf_op | source)
XLA Modules:
  0.0 202.5 jit_solution(916461861180591977)
XLA Ops:
  7.2 0.7 all-gather.4.cloned.1.call-update
  8.6 1.2 slice_bitcast_fusion.1
  9.9 1.0 pad_maximum_fusion
  10.9 10.9 %all-to-all-start = ((f32[8,112,256]{2,1,0:T(8,128)}), f32[8,112,256]{2,1,0:T(8,128)S(1)}, u32[]{:S(2)}, u32[]{:S(2)}) async-start(f32[8,112,256]{2,1,0:T(8,128)} %pad_maximum_fusion), calls=%async_computation | async-start | bytes 1835008 | tf_op jit(solution)/shard_map/all_to_all | solution.py:276
  21.7 1.1 slice_bitcast_fusion
  22.9 44.2 %all-gather.4.cloned.1.call-done.refs_1_ = f32[8,256,256]{2,1,0:T(8,128)} async-done(((f32[1,256,256]{2,1,0:T(8,128)}), f32[8,256,256]{2,1,0:T(8,128)}) %all-gather.4.cloned.1.call-update) | async-done | bytes 2097168 | tf_op jit(solution)/shard_map/all_gather | solution.py:291
  67.1 4.5 %all-to-all-start.1 = ((f32[8,152,256]{2,1,0:T(8,128)}), f32[8,152,256]{2,1,0:T(8,128)S(1)}, u32[]{:S(2)}, u32[]{:S(2)}) async-start(f32[8,152,256]{2,1,0:T(8,128)} %slice_bitcast_fusion), calls=%async_computation.1 | async-start | bytes 2490368 | tf_op jit(solution)/shard_map/all_to_all | solution.py:276
  71.7 4.7 %collective-permute-start.1 = (f32[8,256,256]{2,1,0:T(8,128)}, f32[8,256,256]{2,1,0:T(8,128)}, u32[]{:S(2)}, u32[]{:S(2)}) collective-permute-start(f32[8,256,256]{2,1,0:T(8,128)} %all-gather.4.cloned.1.call-done.refs_1_), channel_id=1, source_target_pairs={{8,0},{16,8},{24,16},{32,24},{40,32},{48,40},{56,48},{64,56},{72,6... | collective-permute-start | bytes 6291464 | tf_op jit(solution)/shard_map/ppermute | solution.py:272
  76.4 3.0 %collective-permute-start = (f32[8,256,256]{2,1,0:T(8,128)}, f32[8,256,256]{2,1,0:T(8,128)}, u32[]{:S(2)}, u32[]{:S(2)}) collective-permute-start(f32[8,256,256]{2,1,0:T(8,128)} %all-gather.4.cloned.1.call-done.refs_1_), channel_id=1, source_target_pairs={{0,8},{8,16},{16,24},{24,32},{32,40},{40,48},{48,56},{56,64},{64,7... | collective-permute-start | bytes 6291464 | tf_op jit(solution)/shard_map/ppermute | solution.py:272
  80.0 0.8 fusion.1.offset_ref
  80.8 20.9 %collective-permute-done.1.refs_2_ = f32[8,256,256]{2,1,0:T(8,128)} collective-permute-done((f32[8,256,256]{2,1,0:T(8,128)}, f32[8,256,256]{2,1,0:T(8,128)}, u32[]{:S(2)}, u32[]{:S(2)}) %collective-permute-start.1) | collective-permute-done | bytes 2097184 | tf_op jit(solution)/shard_map/ppermute | solution.py:272
  101.7 1.0 collective-permute-done.refs_0_
  102.7 2.2 %all-to-all-done.1.more_ref = f32[8,152,256]{2,1,0:T(8,128)S(1)} async-done(((f32[8,152,256]{2,1,0:T(8,128)}), f32[8,152,256]{2,1,0:T(8,128)S(1)}, u32[]{:S(2)}, u32[]{:S(2)}) %all-to-all-start.1) | async-done | bytes 1245216 | tf_op jit(solution)/shard_map/all_to_all | solution.py:276
  104.9 1.0 copy-done
  106.0 6.6 %leaf_sample.1 = (f32[256,256]{1,0:T(8,128)}, f32[128,256]{1,0:T(8,128)}, f32[512,128]{1,0:T(8,128)}) custom-call(s32[2]{0:T(128)} %pad_add_fusion.index_ref, s32[8]{0:T(128)} %fusion.1.offset_ref, f32[8,112,256]{2,1,0:T(8,128)} %copy-done.1, f32[8,152,256]{2,1,0:T(8,128)} %copy-done, f32[8,256,256]{2,1,0:T(8,128)} %collective-permute-done.refs_0_, ...), custom_call_target="tpu_custom_call" | custom-call | tf_op jit(solution)/shard_map/leaf_sample/pallas_call | solution.py:131
  112.6 35.8 %all_to_all.37 = f32[512,1,128]{2,1,0:T(1,128)} all-to-all(f32[512,1,128]{2,1,0:T(1,128)} %bitcast.38), channel_id=1, replica_groups=mesh['row'=64,'col'=8] {'row','col'}, dimensions={0} | all-to-all | bytes 524288 | tf_op jit(solution)/shard_map/all_to_all | solution.py:276
  148.3 2.0 tree_sums.1
  150.3 8.3 %all-to-all-start.4 = ((f32[512,1,128]{2,1,0:T(1,128)}), f32[512,1,128]{2,1,0:T(1,128)S(1)}, u32[]{:S(2)}, u32[]{:S(2)}) async-start(f32[512,1,128]{2,1,0:T(1,128)} %bitcast.35), calls=%async_computation.4 | async-start | bytes 524288 | tf_op jit(solution)/shard_map/all_to_all | solution.py:276
  158.7 9.2 %local_bases.1 = f32[8,3,32,128]{3,2,1,0:T(8,128)} custom-call(s32[2]{0:T(128)} %pad_add_fusion.index_ref, f32[8,128,256]{2,1,0:T(8,128)} %bitcast.39, f32[128,256]{1,0:T(8,128)} %get-tuple-element.11.gram_ref, f32[256,256]{1,0:T(8,128)} %get-tuple-element.12.sample_ref), custom_call_target="tpu_custom_call" | custom-call | flops 2000000000 | bytes 20000000 | tf_op jit(solution)/shard_map/local_bases/pallas_call | solution.py:215
  167.9 7.8 %all-to-all-done.4 = f32[512,1,128]{2,1,0:T(1,128)S(1)} async-done(((f32[512,1,128]{2,1,0:T(1,128)}), f32[512,1,128]{2,1,0:T(1,128)S(1)}, u32[]{:S(2)}, u32[]{:S(2)}) %all-to-all-start.4) | async-done | bytes 262176 | tf_op jit(solution)/shard_map/all_to_all | solution.py:276
  175.8 3.5 %all-to-all-start.2 = ((f32[8,3,32,128]{3,2,1,0:T(8,128)}), f32[8,3,32,128]{3,2,1,0:T(8,128)S(1)}, u32[]{:S(2)}, u32[]{:S(2)}) async-start(f32[8,3,32,128]{3,2,1,0:T(8,128)} %local_bases.1), calls=%async_computation.2 | async-start | bytes 786432 | tf_op jit(solution)/shard_map/all_to_all | solution.py:276
  179.2 6.5 %upper_share.1 = f32[32,128]{1,0:T(8,128)} custom-call(s32[2]{0:T(128)} %pad_add_fusion.index_ref, f32[512,128]{1,0:T(8,128)} %bitcast.37), custom_call_target="tpu_custom_call" | custom-call | flops 1000000000 | bytes 10000000 | tf_op jit(solution)/shard_map/upper_share/pallas_call | solution.py:257
  185.7 8.6 %all-to-all-done.2 = f32[8,3,32,128]{3,2,1,0:T(8,128)S(1)} async-done(((f32[8,3,32,128]{3,2,1,0:T(8,128)}), f32[8,3,32,128]{3,2,1,0:T(8,128)S(1)}, u32[]{:S(2)}, u32[]{:S(2)}) %all-to-all-start.2) | async-done | bytes 393248 | tf_op jit(solution)/shard_map/all_to_all | solution.py:276
  194.9 0.7 slice_bitcast_fusion.2
  (16 shorter events, 2.1 us)
Async XLA Ops:
  7.2 60.0 %all-gather.4.cloned.1.call-start = ((), (), s32[]{:S(2)}) async-start(), calls=%async_computation.5 | async-start | bytes 2359296 | tf_op jit(solution)/shard_map/all_gather | solution.py:291
  9.8 12.0 %copy-start.2 = (f32[8,1,256,256]{3,2,1,0:T(8,128)S(1)}, f32[8,1,256,256]{3,2,1,0:T(8,128)}, u32[]{:S(2)}) copy-start(f32[8,1,256,256]{3,2,1,0:T(8,128)} %param.4) | copy-start | bytes 6291460
  10.9 56.3 %all-to-all-start = ((f32[8,112,256]{2,1,0:T(8,128)}), f32[8,112,256]{2,1,0:T(8,128)S(1)}, u32[]{:S(2)}, u32[]{:S(2)}) async-start(f32[8,112,256]{2,1,0:T(8,128)} %pad_maximum_fusion), calls=%async_computation | async-start | bytes 1835008 | tf_op jit(solution)/shard_map/all_to_all | solution.py:276
  67.1 37.8 %copy-start.1 = (f32[8,112,256]{2,1,0:T(8,128)}, f32[8,112,256]{2,1,0:T(8,128)S(1)}, u32[]{:S(2)}) copy-start(f32[8,112,256]{2,1,0:T(8,128)S(1)} %all-to-all-done.near_ref) | copy-start | bytes 2752516
  67.1 37.8 %all-to-all-start.1 = ((f32[8,152,256]{2,1,0:T(8,128)}), f32[8,152,256]{2,1,0:T(8,128)S(1)}, u32[]{:S(2)}, u32[]{:S(2)}) async-start(f32[8,152,256]{2,1,0:T(8,128)} %slice_bitcast_fusion), calls=%async_computation.1 | async-start | bytes 2490368 | tf_op jit(solution)/shard_map/all_to_all | solution.py:276
  71.6 87.1 %all-gather.6.cloned.1.call-start = ((), (), s32[]{:S(2)}) async-start(), calls=%async_computation.6 | async-start | bytes 1179648 | tf_op jit(solution)/shard_map/all_gather | solution.py:300
  71.7 30.0 %collective-permute-start.1 = (f32[8,256,256]{2,1,0:T(8,128)}, f32[8,256,256]{2,1,0:T(8,128)}, u32[]{:S(2)}, u32[]{:S(2)}) collective-permute-start(f32[8,256,256]{2,1,0:T(8,128)} %all-gather.4.cloned.1.call-done.refs_1_), channel_id=1, source_target_pairs={{8,0},{16,8},{24,16},{32,24},{40,32},{48,40},{56,48},{64,56},{72,6... | collective-permute-start | bytes 6291464 | tf_op jit(solution)/shard_map/ppermute | solution.py:272
  76.4 26.3 %collective-permute-start = (f32[8,256,256]{2,1,0:T(8,128)}, f32[8,256,256]{2,1,0:T(8,128)}, u32[]{:S(2)}, u32[]{:S(2)}) collective-permute-start(f32[8,256,256]{2,1,0:T(8,128)} %all-gather.4.cloned.1.call-done.refs_1_), channel_id=1, source_target_pairs={{0,8},{8,16},{16,24},{24,32},{32,40},{40,48},{48,56},{56,64},{64,7... | collective-permute-start | bytes 6291464 | tf_op jit(solution)/shard_map/ppermute | solution.py:272
  104.9 1.0 copy-start
  150.3 25.5 %all-to-all-start.4 = ((f32[512,1,128]{2,1,0:T(1,128)}), f32[512,1,128]{2,1,0:T(1,128)S(1)}, u32[]{:S(2)}, u32[]{:S(2)}) async-start(f32[512,1,128]{2,1,0:T(1,128)} %bitcast.35), calls=%async_computation.4 | async-start | bytes 524288 | tf_op jit(solution)/shard_map/all_to_all | solution.py:276
  175.8 3.5 %copy-start.3 = (f32[512,1,128]{2,1,0:T(1,128)}, f32[512,1,128]{2,1,0:T(1,128)S(1)}, u32[]{:S(2)}) copy-start(f32[512,1,128]{2,1,0:T(1,128)S(1)} %all-to-all-done.4) | copy-start | bytes 786436
  175.8 18.5 %all-to-all-start.2 = ((f32[8,3,32,128]{3,2,1,0:T(8,128)}), f32[8,3,32,128]{3,2,1,0:T(8,128)S(1)}, u32[]{:S(2)}, u32[]{:S(2)}) async-start(f32[8,3,32,128]{3,2,1,0:T(8,128)} %local_bases.1), calls=%async_computation.2 | async-start | bytes 786432 | tf_op jit(solution)/shard_map/all_to_all | solution.py:276
Sparse Core Ops, SparseCore 0:
  10.1 57.0 all-gather.3
  112.7 40.7 all-gather.5

commit v7 on v6

--- a/solution.py
+++ b/solution.py
@@ -102,22 +102,33 @@
     split = FIRST_ROWS
 
     def kernel(index_ref, offset_ref, near_ref, more_ref, *refs):
-        panel_refs, (panel_ref, nugget_ref, sample_ref, gram_ref, packed_ref, buffer, sems) = refs[:3], refs[3:]
+        panel_refs, (panel_ref, nugget_ref, sample_ref, gram_ref, packed_ref, buffer, blocks, sems) = refs[:3], refs[3:]
+
+        def block_copies(k):
+            upper, lower = pl.ds(0, split), pl.ds(split, size - split)
+            return (
+                pltpu.make_async_copy(near_ref.at[k, upper], blocks.at[k, upper], sems.at[1, k]),
+                pltpu.make_async_copy(more_ref.at[k], blocks.at[k, lower], sems.at[2, k]),
+            )
+
         for k in range(parts):
+            for copy in block_copies(k):
+                copy.start()
             offset = offset_ref[k]
             for part, ref in enumerate(panel_refs):
 
                 @pl.when(offset // parts == part)
                 def _():
-                    pltpu.make_async_copy(ref.at[lax.rem(offset, parts)], buffer.at[k], sems.at[k]).start()
+                    pltpu.make_async_copy(ref.at[lax.rem(offset, parts)], buffer.at[k], sems.at[0, k]).start()
 
         row = nugget_ref[pl.ds(index_ref[1], 1), :]
         column = jnp.broadcast_to(row, (8, size)).T[:, :1]
         sample_ref[...] = column * panel_ref[0]
         for k in range(parts):
-            pltpu.make_async_copy(panel_refs[0].at[0], buffer.at[k], sems.at[k]).wait()
-            sample_ref[:split] += dot(near_ref[k, :split], buffer[k], ((1,), (0,)))
-            sample_ref[split:] += dot(more_ref[k], buffer[k], ((1,), (0,)))
+            pltpu.make_async_copy(panel_refs[0].at[0], buffer.at[k], sems.at[0, k]).wait()
+            for copy in block_copies(k):
+                copy.wait()
+            sample_ref[...] += dot(blocks[k], buffer[k], ((1,), (0,)))
         half = width // 2
         gram_ref[...] = dot(sample_ref[:, :half], sample_ref[...], ((0,), (0,)))
         lane = iota((half, half), 1)
@@ -130,14 +141,19 @@
     smem = pl.BlockSpec(memory_space=pltpu.SMEM)
     return pl.pallas_call(
         kernel,
-        in_specs=[smem, smem, vmem(), vmem()] + [anywhere] * 3 + [vmem()] * 2,
+        in_specs=[smem, smem, anywhere, anywhere] + [anywhere] * 3 + [vmem()] * 2,
         out_specs=[vmem()] * 3,
         out_shape=[
             shape(size, width),
             shape(width // 2, width),
             shape(width // 2 * (width // 2 // PIECE), width // 2),
         ],
-        scratch_shapes=[pltpu.VMEM((parts, size, width), jnp.float32), pltpu.SemaphoreType.DMA((parts,))],
+        scratch_shapes=[
+            pltpu.VMEM((parts, size, width), jnp.float32),
+            pltpu.VMEM((parts, size, size), jnp.float32),
+            pltpu.SemaphoreType.DMA((3, parts)),
+        ],
+        compiler_params=pltpu.CompilerParams(vmem_limit_bytes=16 * 2**20),
         name="leaf_sample",
     )(index, offsets, *near, *panels, panel, nugget)
 

time: 203 us -> 206 us (1.015)
  Pallas kernels: 24.2 us -> 26.4 us
    pallas_call x1, Pallas kernels: 6.59 us -> 8.69 us  [leaf_sample(): pl.pallas_call(kernel, in_specs=[smem, smem, anywhere, anywhere] + [anywh...]
  transfers between devices with their start and end apart: 8 -> 8, of which waited for: 6 -> 6; matrix products, arithmetic and copies ran while one was open for 3% -> 2% of each run, Pallas kernels for 9% -> 9%
where the time goes in v7:
time: 206 us; the launch traced here: 205 us
  waiting for transfers between devices  86.5 us (42%)
  blocking collectives  35.3 us (17%)
  starting transfers between devices  34.9 us (17%)
  Pallas kernels  26.4 us (13%)
  between operations  14.2 us (7%)
  local copies, waits for them, and re-layouts  6.13 us (3%)
    all_gather x1, waiting for transfers between devices, on_device(): own = lax.all_gather(test_panels, 'col', axis=0, tiled=True)  44.2 us
    all_to_all x1, blocking collectives, exchange(): return lax.all_to_all(block, axis, 0, 0, tiled=True)  35.3 us
    all_to_all x4, starting transfers between devices, exchange(): return lax.all_to_all(block, axis, 0, 0, tiled=True)  27.1 us
    ppermute x1, waiting for transfers between devices, neighbours(): lax.ppermute(block, 'row', backward)  22 us
    all_to_all x4, waiting for transfers between devices, exchange(): return lax.all_to_all(block, axis, 0, 0, tiled=True)  18.6 us
    pallas_call x1, Pallas kernels, local_bases(): pl.pallas_call(kernel, in_specs=[pl.BlockSpec(memory_space=pltpu.SMEM), v...  9.24 us
    pallas_call x1, Pallas kernels, leaf_sample(): pl.pallas_call(kernel, in_specs=[smem, smem, anywhere, anywhere] + [anywh...  8.69 us
    pallas_call x1, Pallas kernels, upper_share(): pl.pallas_call(kernel, in_specs=[pl.BlockSpec(memory_space=pltpu.SMEM), v...  6.45 us
  transfers between devices with their start and end apart: 8, of which 6 were waited for; matrix products, arithmetic and copies ran while one was open for 2% of the time, Pallas kernels for 9%

profile of v7, /device:TPU:1, one launch (start us, length us, event | category | flops | bytes accessed | tf_op | source)
XLA Modules:
  0.0 205.5 jit_solution(15707374286775478204)
XLA Ops:
  7.2 0.7 all-gather.4.cloned.1.call-update
  8.6 1.2 slice_bitcast_fusion.1
  9.9 1.0 pad_maximum_fusion
  10.9 10.9 %all-to-all-start = ((f32[8,112,256]{2,1,0:T(8,128)}), f32[8,112,256]{2,1,0:T(8,128)S(1)}, u32[]{:S(2)}, u32[]{:S(2)}) async-start(f32[8,112,256]{2,1,0:T(8,128)} %pad_maximum_fusion), calls=%async_computation | async-start | bytes 1835008 | tf_op jit(solution)/shard_map/all_to_all | solution.py:292
  21.8 1.1 slice_bitcast_fusion
  22.9 44.2 %all-gather.4.cloned.1.call-done.refs_1_ = f32[8,256,256]{2,1,0:T(8,128)} async-done(((f32[1,256,256]{2,1,0:T(8,128)}), f32[8,256,256]{2,1,0:T(8,128)}) %all-gather.4.cloned.1.call-update) | async-done | bytes 2097168 | tf_op jit(solution)/shard_map/all_gather | solution.py:307
  67.1 4.5 %all-to-all-start.1 = ((f32[8,152,256]{2,1,0:T(8,128)}), f32[8,152,256]{2,1,0:T(8,128)S(1)}, u32[]{:S(2)}, u32[]{:S(2)}) async-start(f32[8,152,256]{2,1,0:T(8,128)} %slice_bitcast_fusion), calls=%async_computation.1 | async-start | bytes 2490368 | tf_op jit(solution)/shard_map/all_to_all | solution.py:292
  71.7 4.7 %collective-permute-start.1 = (f32[8,256,256]{2,1,0:T(8,128)}, f32[8,256,256]{2,1,0:T(8,128)}, u32[]{:S(2)}, u32[]{:S(2)}) collective-permute-start(f32[8,256,256]{2,1,0:T(8,128)} %all-gather.4.cloned.1.call-done.refs_1_), channel_id=1, source_target_pairs={{8,0},{16,8},{24,16},{32,24},{40,32},{48,40},{56,48},{64,56},{72,6... | collective-permute-start | bytes 6291464 | tf_op jit(solution)/shard_map/ppermute | solution.py:288
  76.4 3.0 %collective-permute-start = (f32[8,256,256]{2,1,0:T(8,128)}, f32[8,256,256]{2,1,0:T(8,128)}, u32[]{:S(2)}, u32[]{:S(2)}) collective-permute-start(f32[8,256,256]{2,1,0:T(8,128)} %all-gather.4.cloned.1.call-done.refs_1_), channel_id=1, source_target_pairs={{0,8},{8,16},{16,24},{24,32},{32,40},{40,48},{48,56},{56,64},{64,7... | collective-permute-start | bytes 6291464 | tf_op jit(solution)/shard_map/ppermute | solution.py:288
  79.7 22.0 %collective-permute-done.1.refs_2_ = f32[8,256,256]{2,1,0:T(8,128)} collective-permute-done((f32[8,256,256]{2,1,0:T(8,128)}, f32[8,256,256]{2,1,0:T(8,128)}, u32[]{:S(2)}, u32[]{:S(2)}) %collective-permute-start.1) | collective-permute-done | bytes 2097184 | tf_op jit(solution)/shard_map/ppermute | solution.py:288
  101.7 1.0 collective-permute-done.refs_0_
  102.7 2.2 %all-to-all-done.1.more_ref = f32[8,152,256]{2,1,0:T(8,128)S(1)} async-done(((f32[8,152,256]{2,1,0:T(8,128)}), f32[8,152,256]{2,1,0:T(8,128)S(1)}, u32[]{:S(2)}, u32[]{:S(2)}) %all-to-all-start.1) | async-done | bytes 1245216 | tf_op jit(solution)/shard_map/all_to_all | solution.py:292
  104.9 1.6 copy-done
  106.5 8.7 %leaf_sample.1 = (f32[256,256]{1,0:T(8,128)S(1)}, f32[128,256]{1,0:T(8,128)}, f32[512,128]{1,0:T(8,128)S(1)}) custom-call(s32[2]{0:T(128)S(1)} %pad_add_fusion.index_ref, s32[8]{0:T(128)S(1)} %fusion.1.offset_ref, f32[8,112,256]{2,1,0:T(8,128)S(1)} %all-to-all-done.near_ref, f32[8,152,256]{2,1,0:T(8,128)S(1)} %all-to-all-done.1.more_ref, ...), custom_call_target="tpu_custom_call" | custom-call | tf_op jit(solution)/shard_map/leaf_sample/pallas_call | solution.py:142
  115.2 0.7 copy-done.4
  116.0 35.3 %all_to_all.37 = f32[512,1,128]{2,1,0:T(1,128)} all-to-all(f32[512,1,128]{2,1,0:T(1,128)S(1)} %bitcast.33), channel_id=1, replica_groups=mesh['row'=64,'col'=8] {'row','col'}, dimensions={0} | all-to-all | bytes 524288 | tf_op jit(solution)/shard_map/all_to_all | solution.py:292
  151.3 2.0 tree_sums.1
  153.3 8.4 %all-to-all-start.4 = ((f32[512,1,128]{2,1,0:T(1,128)}), f32[512,1,128]{2,1,0:T(1,128)S(1)}, u32[]{:S(2)}, u32[]{:S(2)}) async-start(f32[512,1,128]{2,1,0:T(1,128)} %bitcast.36), calls=%async_computation.4 | async-start | bytes 524288 | tf_op jit(solution)/shard_map/all_to_all | solution.py:292
  161.7 9.2 %local_bases.1 = f32[8,3,32,128]{3,2,1,0:T(8,128)} custom-call(s32[2]{0:T(128)} %copy-done.3, f32[8,128,256]{2,1,0:T(8,128)} %bitcast.39, f32[128,256]{1,0:T(8,128)} %get-tuple-element.11.gram_ref, f32[256,256]{1,0:T(8,128)} %copy-done.4), custom_call_target="tpu_custom_call" | custom-call | flops 2000000000 | bytes 20000000 | tf_op jit(solution)/shard_map/local_bases/pallas_call | solution.py:231
  170.9 7.8 %all-to-all-done.4 = f32[512,1,128]{2,1,0:T(1,128)S(1)} async-done(((f32[512,1,128]{2,1,0:T(1,128)}), f32[512,1,128]{2,1,0:T(1,128)S(1)}, u32[]{:S(2)}, u32[]{:S(2)}) %all-to-all-start.4) | async-done | bytes 262176 | tf_op jit(solution)/shard_map/all_to_all | solution.py:292
  178.7 3.5 %all-to-all-start.2 = ((f32[8,3,32,128]{3,2,1,0:T(8,128)}), f32[8,3,32,128]{3,2,1,0:T(8,128)S(1)}, u32[]{:S(2)}, u32[]{:S(2)}) async-start(f32[8,3,32,128]{3,2,1,0:T(8,128)} %local_bases.1), calls=%async_computation.2 | async-start | bytes 786432 | tf_op jit(solution)/shard_map/all_to_all | solution.py:292
  182.2 6.5 %upper_share.1 = f32[32,128]{1,0:T(8,128)} custom-call(s32[2]{0:T(128)} %copy-done.3, f32[512,128]{1,0:T(8,128)} %bitcast.38), custom_call_target="tpu_custom_call" | custom-call | flops 1000000000 | bytes 10000000 | tf_op jit(solution)/shard_map/upper_share/pallas_call | solution.py:273
  188.7 8.6 %all-to-all-done.2 = f32[8,3,32,128]{3,2,1,0:T(8,128)S(1)} async-done(((f32[8,3,32,128]{3,2,1,0:T(8,128)}), f32[8,3,32,128]{3,2,1,0:T(8,128)S(1)}, u32[]{:S(2)}, u32[]{:S(2)}) %all-to-all-start.2) | async-done | bytes 393248 | tf_op jit(solution)/shard_map/all_to_all | solution.py:292
  197.9 0.7 slice_bitcast_fusion.2
  (22 shorter events, 1.8 us)
Async XLA Ops:
  7.2 60.0 %all-gather.4.cloned.1.call-start = ((), (), s32[]{:S(2)}) async-start(), calls=%async_computation.5 | async-start | bytes 2359296 | tf_op jit(solution)/shard_map/all_gather | solution.py:307
  9.8 12.0 %copy-start.5 = (f32[8,1,256,256]{3,2,1,0:T(8,128)S(1)}, f32[8,1,256,256]{3,2,1,0:T(8,128)}, u32[]{:S(2)}) copy-start(f32[8,1,256,256]{3,2,1,0:T(8,128)} %param.4) | copy-start | bytes 6291460
  10.9 56.3 %all-to-all-start = ((f32[8,112,256]{2,1,0:T(8,128)}), f32[8,112,256]{2,1,0:T(8,128)S(1)}, u32[]{:S(2)}, u32[]{:S(2)}) async-start(f32[8,112,256]{2,1,0:T(8,128)} %pad_maximum_fusion), calls=%async_computation | async-start | bytes 1835008 | tf_op jit(solution)/shard_map/all_to_all | solution.py:292
  21.7 83.2 %copy-start.1 = (f32[1,256,256]{2,1,0:T(8,128)S(1)}, f32[1,256,256]{2,1,0:T(8,128)}, u32[]{:S(2)}) copy-start(f32[1,256,256]{2,1,0:T(8,128)} %refs_3_.1) | copy-start | bytes 786436
  21.7 83.2 %copy-start.2 = (f32[8,256]{1,0:T(8,128)S(1)}, f32[8,256]{1,0:T(8,128)}, u32[]{:S(2)}) copy-start(f32[8,256]{1,0:T(8,128)} %refs_4_.1) | copy-start | bytes 24580
  67.1 37.8 %all-to-all-start.1 = ((f32[8,152,256]{2,1,0:T(8,128)}), f32[8,152,256]{2,1,0:T(8,128)S(1)}, u32[]{:S(2)}, u32[]{:S(2)}) async-start(f32[8,152,256]{2,1,0:T(8,128)} %slice_bitcast_fusion), calls=%async_computation.1 | async-start | bytes 2490368 | tf_op jit(solution)/shard_map/all_to_all | solution.py:292
  71.6 90.1 %all-gather.6.cloned.1.call-start = ((), (), s32[]{:S(2)}) async-start(), calls=%async_computation.6 | async-start | bytes 1179648 | tf_op jit(solution)/shard_map/all_gather | solution.py:316
  71.7 30.0 %collective-permute-start.1 = (f32[8,256,256]{2,1,0:T(8,128)}, f32[8,256,256]{2,1,0:T(8,128)}, u32[]{:S(2)}, u32[]{:S(2)}) collective-permute-start(f32[8,256,256]{2,1,0:T(8,128)} %all-gather.4.cloned.1.call-done.refs_1_), channel_id=1, source_target_pairs={{8,0},{16,8},{24,16},{32,24},{40,32},{48,40},{56,48},{64,56},{72,6... | collective-permute-start | bytes 6291464 | tf_op jit(solution)/shard_map/ppermute | solution.py:288
  76.4 26.3 %collective-permute-start = (f32[8,256,256]{2,1,0:T(8,128)}, f32[8,256,256]{2,1,0:T(8,128)}, u32[]{:S(2)}, u32[]{:S(2)}) collective-permute-start(f32[8,256,256]{2,1,0:T(8,128)} %all-gather.4.cloned.1.call-done.refs_1_), channel_id=1, source_target_pairs={{0,8},{8,16},{16,24},{24,32},{32,40},{40,48},{48,56},{56,64},{64,7... | collective-permute-start | bytes 6291464 | tf_op jit(solution)/shard_map/ppermute | solution.py:288
  79.5 35.7 %copy-start.3 = (s32[2]{0:T(128)}, s32[2]{0:T(128)S(1)}, u32[]{:S(2)}) copy-start(s32[2]{0:T(128)S(1)} %pad_add_fusion.index_ref) | copy-start | bytes 28
  104.9 1.6 copy-start
  115.2 0.7 copy-start.4
  153.3 25.4 %all-to-all-start.4 = ((f32[512,1,128]{2,1,0:T(1,128)}), f32[512,1,128]{2,1,0:T(1,128)S(1)}, u32[]{:S(2)}, u32[]{:S(2)}) async-start(f32[512,1,128]{2,1,0:T(1,128)} %bitcast.36), calls=%async_computation.4 | async-start | bytes 524288 | tf_op jit(solution)/shard_map/all_to_all | solution.py:292
  178.7 3.5 %copy-start.6 = (f32[512,1,128]{2,1,0:T(1,128)}, f32[512,1,128]{2,1,0:T(1,128)S(1)}, u32[]{:S(2)}) copy-start(f32[512,1,128]{2,1,0:T(1,128)S(1)} %all-to-all-done.4) | copy-start | bytes 786436
  178.7 18.5 %all-to-all-start.2 = ((f32[8,3,32,128]{3,2,1,0:T(8,128)}), f32[8,3,32,128]{3,2,1,0:T(8,128)S(1)}, u32[]{:S(2)}, u32[]{:S(2)}) async-start(f32[8,3,32,128]{3,2,1,0:T(8,128)} %local_bases.1), calls=%async_computation.2 | async-start | bytes 786432 | tf_op jit(solution)/shard_map/all_to_all | solution.py:292
Sparse Core Ops, SparseCore 0:
  10.1 57.0 all-gather.3
  116.1 41.6 all-gather.5
